TPU v7x, 256 devices: a whole 4x4x8 slice. The times are simulated.
256 devices in a mesh: orb: 64 (over x, z_lo, y, core), pan: 4 (over z_hi).
Axes of the slice: x: 4, y: 4, z: 8 (z_hi: 4, z_lo: 2; z = z_hi * 2 + z_lo), core: 2. Of those that a mesh axis runs over, the one named last changes fastest.
Arguments:
- orbitals: float32 [1024, 110592], P(('orb', 'pan')), may hold values from -6 to 6
- potential: float32 [110592], replicated, may hold values from -1 to 2
- magic_taps: float32 [16], replicated, may hold values from -4 to 4
- kinetic_taps: float32 [29], replicated, may hold values from -3 to 3
Outputs:
- gradient: float32 [1024, 110592], P(('orb', 'pan'))
All inputs are finite; a program needn't handle non-finite values.
Results may differ from a plain program's by a relative error of at most 0.00013.
Values sent between devices are 32-bit elements; how exact they have to be, the bound alone decides.
No kernel may reach another device: no remote copies, remote signals or barrier semaphores. Data moves between devices by JAX's collectives and lax.ppermute only.
A program may use at most 128 MiB of HBM per device.

v0:
```python
import jax
import jax.numpy as jnp
from jax import lax
from jax.experimental import pallas as pl
from jax.experimental.pallas import tpu as pltpu
from jax.sharding import Mesh, PartitionSpec as P

G = 48
NC = 110592
SPLIT = (4, 2, 4, 2, 4)
NAMES = ("x", "zl", "y", "core", "zh")
COEF = ("y", "zl", "zh")
PANEL = ("x", "core")
NSPLIT = 32
HIGH = lax.Precision.HIGH
PLANE = G * G
BLK = 16 * G
F32 = jnp.float32
BF16 = jnp.bfloat16


def split_bf16(value):
    high = value.astype(BF16)
    return high, (value - high.astype(F32)).astype(BF16)


def pick_taps(taps_ref, count, offset):
    out = jnp.zeros(offset.shape, F32)
    for k in range(count):
        out = jnp.where(offset == k, taps_ref[k], out)
    return out


def wrap(offset):
    return jnp.where(offset < 0, offset + G, jnp.where(offset >= G, offset - G, offset))


def ints(shape, dim):
    return lax.broadcasted_iota(jnp.int32, shape, dim)


def div_g(value):
    return (value * 1366) >> 16


def x_matrix(taps_ref, count, rows, transposed):
    shape = (rows, rows)
    r, c = ints(shape, 0), ints(shape, 1)
    gap = (r >> 2) - (c >> 2) if transposed else (c >> 2) - (r >> 2)
    offset = wrap(gap + (count - 1) // 2)
    return jnp.where((r & 3) == (c & 3), pick_taps(taps_ref, count, offset), 0.0)


def z_table(taps_ref, count, transposed):
    shape = (G, BLK)
    lane = ints(shape, 1)
    z_out = lane - G * div_g(lane)
    z_in = ints(shape, 0)
    gap = z_out - z_in if transposed else z_in - z_out
    return pick_taps(taps_ref, count, wrap(gap + (count - 1) // 2))


def y_table(taps_ref, count, reach, transposed):
    shape = (16 + 2 * reach, BLK)
    gap = ints(shape, 0) - reach - div_g(ints(shape, 1))
    if transposed:
        gap = -gap
    return pick_taps(taps_ref, count, gap + (count - 1) // 2)


def h_kernel(magic_ref, kinetic_ref, psi_ref, pot_ref, out_ref,
             s, t, zt, zt2, yt, w_hi, w_lo, lhs, prod, pad, xm):
    rows = s.shape[0]
    n_magic, n_kin = magic_ref.shape[0], kinetic_ref.shape[0]

    def fill_weights(depth, with_identity):
        def body(j, carry):
            value = zt[...] * yt[pl.ds(j, 1), :]
            if with_identity:
                lane = ints((1, BLK), 1)
                same = jnp.where(div_g(lane) == j - 16, 1.0, 0.0).astype(F32)
                value = value + zt2[...] * same
            high, low = split_bf16(value)
            at = pl.multiple_of(j * G, G)
            w_hi[pl.ds(at, G), :] = high
            w_lo[pl.ds(at, G), :] = low
            return carry
        lax.fori_loop(0, depth, body, 0)

    def fill_lhs(source, reach):
        edge = reach * G
        width = (16 + 2 * reach) * G
        for part in range(2):
            pad[:, 0:PLANE] = split_bf16(source[...])[part]
            pad[:, PLANE:2 * PLANE] = pad[:, 0:PLANE]
            for n in range(3):
                start = (BLK * n - edge) % PLANE
                lhs[pl.ds((3 * part + n) * rows, rows), 0:width] = pad[:, start:start + width]

    def kron(width, accumulate, target):
        def body(nt, carry):
            at = pl.multiple_of(nt * 256, 256)
            cols = pl.ds(at, 256)
            prod[...] = jnp.dot(lhs[:, 0:width], w_hi[0:width, cols], preferred_element_type=F32)
            low = jnp.dot(lhs[0:3 * rows, 0:width], w_lo[0:width, cols], preferred_element_type=F32)
            for n in range(3):
                value = (prod[n * rows:(n + 1) * rows, :] + prod[(3 + n) * rows:(4 + n) * rows, :]
                         + low[n * rows:(n + 1) * rows, :])
                place = pl.ds(pl.multiple_of(BLK * n + nt * 256, 256), 256)
                if accumulate:
                    value = value + target[:, place]
                target[:, place] = value
            return carry
        lax.fori_loop(0, 3, body, 0)

    def along_x(matrix, source, finish):
        high, low = split_bf16(matrix)
        xm[0:rows, :] = high
        xm[rows:, :] = low

        def body(nt, carry):
            cols = pl.ds(pl.multiple_of(nt * 256, 256), 256)
            b_hi, b_lo = split_bf16(source[:, cols])
            both = jnp.dot(xm[...], b_hi, preferred_element_type=F32)
            low = jnp.dot(xm[0:rows, :], b_lo, preferred_element_type=F32)
            finish(cols, both[0:rows] + both[rows:] + low)
            return carry
        lax.fori_loop(0, PLANE // 256, body, 0)

    for x in range(G):
        s[4 * x:4 * x + 4, :] = psi_ref[:, x * PLANE:(x + 1) * PLANE]

    zt[...] = z_table(magic_ref, n_magic, False)
    yt[0:32, :] = y_table(magic_ref, n_magic, 8, False)
    fill_weights(32, False)
    fill_lhs(s, 8)
    kron(2 * BLK, False, t)

    def magic_and_potential(cols, value):
        pot = pot_ref[:, cols]
        t[:, cols] = value * jnp.broadcast_to(pot[:, None, :], (G, 4, 256)).reshape(rows, 256)

    along_x(x_matrix(magic_ref, n_magic, rows, False), t, magic_and_potential)

    def keep(cols, value):
        t[:, cols] = value

    along_x(x_matrix(magic_ref, n_magic, rows, True), t, keep)

    zt[...] = z_table(magic_ref, n_magic, True)
    yt[0:32, :] = y_table(magic_ref, n_magic, 8, True)
    fill_weights(32, False)
    fill_lhs(t, 8)

    def start_sum(cols, value):
        t[:, cols] = value

    along_x(x_matrix(kinetic_ref, n_kin, rows, False), s, start_sum)
    kron(2 * BLK, True, t)

    shape = (G, BLK)
    lane = ints(shape, 1)
    zt[...] = jnp.where(lane - G * div_g(lane) == ints(shape, 0), 1.0, 0.0).astype(F32)
    zt2[...] = z_table(kinetic_ref, n_kin, False)
    yt[...] = y_table(kinetic_ref, n_kin, 16, False)
    fill_weights(48, True)
    fill_lhs(s, 16)
    kron(3 * BLK, True, t)

    for x in range(G):
        out_ref[:, x * PLANE:(x + 1) * PLANE] = t[4 * x:4 * x + 4, :]


def hamiltonian(orbitals, potential, magic_taps, kinetic_taps):
    count = orbitals.shape[0]
    rows = count * G
    vmem = pl.BlockSpec(memory_space=pltpu.VMEM)
    smem = pl.BlockSpec(memory_space=pltpu.SMEM)
    return pl.pallas_call(
        h_kernel,
        out_shape=jax.ShapeDtypeStruct(orbitals.shape, F32),
        in_specs=[smem, smem, vmem, vmem],
        out_specs=vmem,
        scratch_shapes=[
            pltpu.VMEM((rows, PLANE), F32),
            pltpu.VMEM((rows, PLANE), F32),
            pltpu.VMEM((G, BLK), F32),
            pltpu.VMEM((G, BLK), F32),
            pltpu.VMEM((G, BLK), F32),
            pltpu.VMEM((PLANE, BLK), BF16),
            pltpu.VMEM((PLANE, BLK), BF16),
            pltpu.VMEM((6 * rows, PLANE), BF16),
            pltpu.VMEM((6 * rows, 256), F32),
            pltpu.VMEM((rows, 2 * PLANE), BF16),
            pltpu.VMEM((2 * rows, rows), BF16),
        ],
        compiler_params=pltpu.CompilerParams(vmem_limit_bytes=48 * 1024 * 1024),
        name="hamiltonian",
    )(magic_taps, kinetic_taps, orbitals, potential.reshape(G, PLANE))


def to_cols(block):
    return lax.all_to_all(block, COEF, split_axis=1, concat_axis=0, tiled=True)


def shards(orbitals, potential, magic_taps, kinetic_taps):
    psi_cols = to_cols(orbitals)
    psi_every = lax.all_gather(psi_cols, PANEL, axis=0, tiled=True)
    hpsi = hamiltonian(orbitals, potential, magic_taps, kinetic_taps)
    hpsi_cols = to_cols(hpsi)
    part = jnp.einsum("jc,ic->ji", psi_every, hpsi_cols, precision=HIGH) * (1.0 / NC)
    rows = part.shape[0] // NSPLIT
    pieces = lax.all_to_all(
        part.reshape(NSPLIT, rows, -1), COEF, split_axis=0, concat_axis=0, tiled=True
    )
    mine = jnp.sum(pieces, axis=0)
    margin = lax.all_to_all(
        jnp.broadcast_to(mine[None], pieces.shape), COEF, split_axis=0, concat_axis=0, tiled=True
    ).reshape(part.shape)
    grad_cols = hpsi_cols - jnp.einsum("ji,jc->ic", margin, psi_every, precision=HIGH)
    return lax.all_to_all(grad_cols, COEF, split_axis=0, concat_axis=1, tiled=True)


def solution(mesh):
    fine = Mesh(mesh.devices.reshape(SPLIT), NAMES)
    placed = (P(NAMES, None), P(), P(), P())
    return jax.shard_map(
        shards, mesh=fine, in_specs=placed, out_specs=P(NAMES, None), check_vma=False
    )
```

profile of v0, /device:TPU:64, one launch (start us, length us, event | category | flops | bytes accessed | tf_op | source)
XLA Modules:
  0.0 261.2 jit_solution(7966497440203189982)
XLA Ops:
  6.5 0.0 all-gather.2.cloned.1.call-start
  6.5 54.8 %all_to_all.67 = f32[4,32,3456]{2,0,1:T(4,128)S(1)} all-to-all(f32[4,32,3456]{2,0,1:T(4,128)} %bitcast.15), channel_id=1, replica_groups=mesh['x'=4,'zl'=2,'y'=4,'core'=2,'zh'=4] {'y','zl','zh'}, dimensions={1} | all-to-all | bytes 3538944 | tf_op jit(solution)/shard_map/all_to_all | solution.py:203
  61.3 0.0 copy-start.3
  61.3 1.8 all_to_all.55
  63.2 0.0 copy-start
  63.2 0.0 copy-start.1
  63.2 0.0 copy-start.2
  63.2 0.0 all-gather.2.cloned.1.call-update
  63.2 0.0 copy-done.3
  63.2 0.1 reshape.19.pot_ref
  63.3 1.4 copy-done
  64.6 0.0 copy-done.1
  64.6 0.0 copy-done.2
  64.6 31.7 %hamiltonian.1 = f32[4,110592]{1,0:T(4,128)S(1)} custom-call(f32[16]{0:T(128)S(1)} %copy-done.1, f32[29]{0:T(128)S(1)} %copy-done.2, f32[4,110592]{1,0:T(4,128)S(1)} %copy-done, f32[48,2304]{1,0:T(8,128)S(1)} %reshape.19.pot_ref), custom_call_target="tpu_custom_call" | custom-call | tf_op jit(solution)/shard_map/hamiltonian/pallas_call | solution.py:179
  96.3 47.8 %all_to_all.68 = f32[4,32,3456]{2,0,1:T(4,128)S(1)} all-to-all(f32[4,32,3456]{2,0,1:T(4,128)S(1)} %bitcast.16), channel_id=1, replica_groups=mesh['x'=4,'zl'=2,'y'=4,'core'=2,'zh'=4] {'y','zl','zh'}, dimensions={1} | all-to-all | bytes 3538944 | tf_op jit(solution)/shard_map/all_to_all | solution.py:203
  144.2 0.6 all_to_all.51
  144.8 0.0 all-gather.2.cloned.1.call-done
  144.8 10.3 %fusion = f32[1024,128]{0,1:T(8,128)S(1)} fusion(f32[128,3456]{1,0:T(8,128)S(1)} %all_to_all.51, f32[1024,3456]{1,0:T(8,128)} %all-gather.2.cloned.1.call-done), kind=kOutput, calls=%fused_computation.2 | convolution fusion | flops 2718040064 | bytes 16449536 | tf_op jit(solution)/shard_map/jc,ic->ji/dot_general | solution.py:211
  155.2 0.2 copy.13
  155.4 20.1 %all_to_all.69 = f32[32,32,128]{2,1,0:T(8,128)S(1)} all-to-all(f32[32,32,128]{2,1,0:T(8,128)S(1)} %bitcast.21), channel_id=1, replica_groups=mesh['x'=4,'zl'=2,'y'=4,'core'=2,'zh'=4] {'y','zl','zh'}, dimensions={0} | all-to-all | bytes 1048576 | tf_op jit(solution)/shard_map/all_to_all | solution.py:213
  175.5 0.1 broadcast_in_dim.2
  175.6 21.1 %all_to_all.70 = f32[32,32,128]{2,1,0:T(8,128)S(1)} all-to-all(f32[32,32,128]{2,1,0:T(8,128)S(1)} %broadcast_in_dim.2), channel_id=1, replica_groups=mesh['x'=4,'zl'=2,'y'=4,'core'=2,'zh'=4] {'y','zl','zh'}, dimensions={0} | all-to-all | bytes 1048576 | tf_op jit(solution)/shard_map/all_to_all | solution.py:217
  196.6 7.8 %convolution_subtract_fusion = f32[128,3456]{1,0:T(8,128)S(1)} fusion(f32[128,3456]{1,0:T(8,128)S(1)} %all_to_all.51, f32[1024,128]{1,0:T(8,128)S(1)} %bitcast.20, f32[1024,3456]{1,0:T(8,128)} %all-gather.2.cloned.1.call-done), kind=kOutput, calls=%fused_computation | convolution fusion | flops 2718351360 | bytes 18219008 | tf_op jit(solution)/shard_map/ji,jc->ic/dot_general | solution.py:220
  204.4 0.5 all_to_all.58
  205.0 48.2 %all_to_all.71 = f32[32,4,3456]{2,1,0:T(4,128)S(1)} all-to-all(f32[32,4,3456]{2,1,0:T(4,128)S(1)} %all_to_all.58), channel_id=1, replica_groups=mesh['x'=4,'zl'=2,'y'=4,'core'=2,'zh'=4] {'y','zl','zh'}, dimensions={0} | all-to-all | bytes 3538944 | tf_op jit(solution)/shard_map/all_to_all | solution.py:221
  253.2 1.2 copy.16
  (1 shorter events, 0.0 us)
Async XLA Ops:
  6.5 138.3 %all-gather.2.cloned.1.call-start = ((), (), s32[]{:S(2)}) async-start(), calls=%async_computation.5 | async-start | bytes 15925248 | tf_op jit(solution)/shard_map/all_gather | solution.py:208
  61.3 1.8 copy-start.3
  63.2 1.5 copy-start
  63.2 1.5 copy-start.1
  63.2 1.5 copy-start.2
Sparse Core Ops, SparseCore 0:
  63.3 73.0 all-gather.1
where the time goes:
time: 262 us; the launch traced here: 261 us
  blocking collectives  192 us (73%)
  Pallas kernels  31.7 us (12%)
  matrix products  18.1 us (7%)
  between operations  13.5 us (5%)
  local copies, waits for them, and re-layouts  5.83 us (2%)
    all_to_all x2, blocking collectives, to_cols(): return lax.all_to_all(block, COEF, split_axis=1, concat_axis=0, tiled=True)  103 us
    all_to_all x1, blocking collectives, shards(): lax.all_to_all(grad_cols, COEF, split_axis=0, concat_axis=1, tiled=True)  48.2 us
    pallas_call x1, Pallas kernels, hamiltonian(): pl.pallas_call(h_kernel, out_shape=jax.ShapeDtypeStruct(orbitals.shape, F...  31.7 us
    all_to_all x1, blocking collectives, shards(): lax.all_to_all(jnp.broadcast_to(mine[None], pieces.shape), COEF, split_ax...  21.1 us
    all_to_all x1, blocking collectives, shards(): lax.all_to_all(part.reshape(NSPLIT, rows, -1), COEF, split_axis=0, concat...  20.1 us
    dot_general x1, matrix products, shards(): jnp.einsum('jc,ic->ji', psi_every, hpsi_cols, precision=HIGH) * (1.0 / NC)  10.3 us
    dot_general x1, matrix products, shards(): jnp.einsum('ji,jc->ic', margin, psi_every, precision=HIGH)  7.79 us
  transfers between devices with their start and end apart: 1, of which 0 were waited for; matrix products, arithmetic and copies ran while one was open for 0% of the time, Pallas kernels for 12%

commit v1 on v0

--- a/solution.py
+++ b/solution.py
@@ -12,6 +12,7 @@
 COEF = ("y", "zl", "zh")
 PANEL = ("x", "core")
 NSPLIT = 32
+FIRST = 14 * 128
 HIGH = lax.Precision.HIGH
 PLANE = G * G
 BLK = 16 * G
@@ -195,29 +196,43 @@
             pltpu.VMEM((2 * rows, rows), BF16),
         ],
         compiler_params=pltpu.CompilerParams(vmem_limit_bytes=48 * 1024 * 1024),
+        cost_estimate=pl.CostEstimate(
+            flops=24_000_000_000, transcendentals=0, bytes_accessed=12 * orbitals.size
+        ),
         name="hamiltonian",
     )(magic_taps, kinetic_taps, orbitals, potential.reshape(G, PLANE))
 
 
 def to_cols(block):
-    return lax.all_to_all(block, COEF, split_axis=1, concat_axis=0, tiled=True)
+    return lax.all_to_all(block, COEF, split_axis=1, concat_axis=0, tiled=True).reshape(
+        NSPLIT * block.shape[0], -1
+    )
 
 
 def shards(orbitals, potential, magic_taps, kinetic_taps):
-    psi_cols = to_cols(orbitals)
-    psi_every = lax.all_gather(psi_cols, PANEL, axis=0, tiled=True)
+    pieces = orbitals.reshape(orbitals.shape[0], NSPLIT, -1)
+    first, second = pieces[:, :, :FIRST], pieces[:, :, FIRST:]
+    cols_1 = to_cols(first)
     hpsi = hamiltonian(orbitals, potential, magic_taps, kinetic_taps)
-    hpsi_cols = to_cols(hpsi)
-    part = jnp.einsum("jc,ic->ji", psi_every, hpsi_cols, precision=HIGH) * (1.0 / NC)
+    cols_1, hpsi, second = lax.optimization_barrier((cols_1, hpsi, second))
+    every_1 = lax.all_gather(cols_1, PANEL, axis=0, tiled=True)
+    cols_2 = to_cols(second)
+    cols_2, hpsi = lax.optimization_barrier((cols_2, hpsi))
+    every_2 = lax.all_gather(cols_2, PANEL, axis=0, tiled=True)
+    hpsi_cols = to_cols(hpsi.reshape(pieces.shape))
+    parts = ((every_1, hpsi_cols[:, :FIRST]), (every_2, hpsi_cols[:, FIRST:]))
+    part = sum(jnp.einsum("jc,ic->ji", psi, own, precision=HIGH) for psi, own in parts) * (1.0 / NC)
     rows = part.shape[0] // NSPLIT
-    pieces = lax.all_to_all(
+    terms = lax.all_to_all(
         part.reshape(NSPLIT, rows, -1), COEF, split_axis=0, concat_axis=0, tiled=True
     )
-    mine = jnp.sum(pieces, axis=0)
+    mine = jnp.sum(terms, axis=0)
     margin = lax.all_to_all(
-        jnp.broadcast_to(mine[None], pieces.shape), COEF, split_axis=0, concat_axis=0, tiled=True
+        jnp.broadcast_to(mine[None], terms.shape), COEF, split_axis=0, concat_axis=0, tiled=True
     ).reshape(part.shape)
-    grad_cols = hpsi_cols - jnp.einsum("ji,jc->ic", margin, psi_every, precision=HIGH)
+    grad_cols = jnp.concatenate(
+        [own - jnp.einsum("ji,jc->ic", margin, psi, precision=HIGH) for psi, own in parts], axis=1
+    )
     return lax.all_to_all(grad_cols, COEF, split_axis=0, concat_axis=1, tiled=True)
 
 

time: 262 us -> 275 us (1.050)
  blocking collectives: 192 us -> 178 us
  starting transfers between devices: 0.01 us -> 11.2 us
  waiting for transfers between devices: 0.04 us -> 6.58 us
  local copies, waits for them, and re-layouts: 5.83 us -> 11.3 us
  matrix products: 18.1 us -> 21.1 us
    all_to_all x3, blocking collectives: 124 us -> 103 us  [the longest x2 80.7 us: to_cols(): lax.all_to_all(block, COEF, split_axis=1, concat_axis=0, tiled=True)]
    all_to_all x0 -> x1, starting transfers between devices: none -> 11.1 us  [to_cols(): lax.all_to_all(block, COEF, split_axis=1, concat_axis=0, tiled=True)]
    all_to_all x1, blocking collectives: 20.1 us -> 27.5 us  [shards(): lax.all_to_all(part.reshape(NSPLIT, rows, -1), COEF, split_axis=0, concat...]
    all_gather x1 -> x2, waiting for transfers between devices: 0.02 us -> 6.55 us  [the longest x1 6.52 us: shards(): every_2 = lax.all_gather(cols_2, PANEL, axis=0, tiled=True)]
    reshape x0 -> x3, local copies, waits for them, and re-layouts: none -> 4.32 us  [to_cols(): lax.all_to_all(block, COEF, split_axis=1, concat_axis=0, tiled=True)]
    slice x0 -> x2, local copies, waits for them, and re-layouts: none -> 3.3 us  [shards(): first, second = (pieces[:, :, :FIRST], pieces[:, :, FIRST:])]
    dot_general x2 -> x4, matrix products: 18.1 us -> 21.1 us  [the longest x2 13.9 us: shards(): jnp.einsum('jc,ic->ji', psi, own, precision=HIGH)]
  transfers between devices with their start and end apart: 1 -> 3, of which waited for: 0 -> 1; matrix products, arithmetic and copies ran while one was open for 0% -> 4% of each run, Pallas kernels for 12% -> 12%
where the time goes in v1:
time: 275 us
  blocking collectives  178 us (65%)
  Pallas kernels  31.7 us (12%)
  matrix products  21.1 us (8%)
  between operations  13.6 us (5%)
  local copies, waits for them, and re-layouts  11.3 us (4%)
  starting transfers between devices  11.2 us (4%)
  waiting for transfers between devices  6.58 us (2%)
    all_to_all x2, blocking collectives, to_cols(): lax.all_to_all(block, COEF, split_axis=1, concat_axis=0, tiled=True)  80.7 us
    all_to_all x1, blocking collectives, shards(): lax.all_to_all(grad_cols, COEF, split_axis=0, concat_axis=1, tiled=True)  48.1 us
    pallas_call x1, Pallas kernels, hamiltonian(): pl.pallas_call(h_kernel, out_shape=jax.ShapeDtypeStruct(orbitals.shape, F...  31.7 us
    all_to_all x1, blocking collectives, shards(): lax.all_to_all(part.reshape(NSPLIT, rows, -1), COEF, split_axis=0, concat...  27.5 us
    all_to_all x1, blocking collectives, shards(): lax.all_to_all(jnp.broadcast_to(mine[None], terms.shape), COEF, split_axi...  21.9 us
    dot_general x2, matrix products, shards(): jnp.einsum('jc,ic->ji', psi, own, precision=HIGH)  13.9 us
    all_to_all x1, starting transfers between devices, to_cols(): lax.all_to_all(block, COEF, split_axis=1, concat_axis=0, tiled=True)  11.1 us
    dot_general x2, matrix products, shards(): jnp.einsum('ji,jc->ic', margin, psi, precision=HIGH)  7.27 us
  transfers between devices with their start and end apart: 3, of which 1 were waited for; matrix products, arithmetic and copies ran while one was open for 4% of the time, Pallas kernels for 12%

profile of v1, /device:TPU:64, one launch (start us, length us, event | category | flops | bytes accessed | tf_op | source)
XLA Modules:
  0.0 274.9 jit_solution(10196707658855191682)
XLA Ops:
  6.5 0.0 copy-start
  6.5 2.3 slice.16
  8.8 0.0 copy-start.7
  8.8 0.0 copy-start.2
  8.8 0.0 copy-start.3
  8.8 11.1 %all-to-all-start = ((f32[4,32,1792]{2,0,1:T(4,128)}), f32[4,32,1792]{2,0,1:T(4,128)}, u32[]{:S(2)}, u32[]{:S(2)}) async-start(f32[4,32,1792]{2,0,1:T(4,128)} %slice.16), calls=%async_computation | async-start | bytes 1835008 | tf_op jit(solution)/shard_map/all_to_all | solution.py:207
  19.9 0.0 all-gather.3.cloned.1.call-start
  20.0 0.0 copy-done
  20.0 1.0 slice.17
  21.0 0.0 copy-done.7
  21.0 0.9 reshape.33.pot_ref
  21.9 0.0 copy-done.2
  21.9 0.0 copy-done.3
  21.9 0.0 copy-start.1
  21.9 1.0 copy-done.1
  22.9 31.7 %hamiltonian.1 = f32[4,110592]{1,0:T(4,128)S(1)} custom-call(f32[16]{0:T(128)S(1)} %copy-done.2, f32[29]{0:T(128)S(1)} %copy-done.3, f32[4,110592]{1,0:T(4,128)S(1)} %copy-done, f32[48,2304]{1,0:T(8,128)S(1)} %copy-done.1), custom_call_target="tpu_custom_call" | custom-call | flops 24000000000 | bytes 5308416 | tf_op jit(solution)/shard_map/hamiltonian/pallas_call | solution.py:180
  54.6 0.0 copy-start.6
  54.6 0.0 all-to-all-done
  54.6 2.5 reshape.32
  57.1 0.0 all-gather.3.cloned.1.call-update
  57.1 0.0 all-gather.5.cloned.1.call-start
  57.2 0.0 copy-done.6
  57.2 33.3 %all_to_all.74 = f32[4,32,1664]{2,0,1:T(4,128)S(1)} all-to-all(f32[4,32,1664]{2,0,1:T(4,128)S(1)} %copy-done.6), channel_id=1, replica_groups=mesh['x'=4,'zl'=2,'y'=4,'core'=2,'zh'=4] {'y','zl','zh'}, dimensions={1} | all-to-all | bytes 1703936 | tf_op jit(solution)/shard_map/all_to_all | solution.py:207
  90.4 1.2 reshape.34
  91.6 0.0 all-gather.5.cloned.1.call-update
  91.7 47.4 %all_to_all.75 = f32[4,32,3456]{2,0,1:T(4,128)S(1)} all-to-all(f32[4,32,3456]{2,0,1:T(4,128)S(1)} %bitcast.29), channel_id=1, replica_groups=mesh['x'=4,'zl'=2,'y'=4,'core'=2,'zh'=4] {'y','zl','zh'}, dimensions={1} | all-to-all | bytes 3538944 | tf_op jit(solution)/shard_map/all_to_all | solution.py:207
  139.1 0.6 reshape.36
  139.7 0.0 copy-start.4
  139.7 0.0 all-gather.3.cloned.1.call-done
  139.7 7.7 %fusion.1 = f32[1024,128]{1,0:T(8,128)} fusion(f32[1024,1792]{1,0:T(8,128)} %all-gather.3.cloned.1.call-done, f32[128,3456]{1,0:T(8,128)S(1)} %reshape.36), kind=kOutput, calls=%fused_computation.5 | convolution fusion | flops 1409286144 | bytes 8781824 | tf_op jit(solution)/shard_map/jc,ic->ji/dot_general | solution.py:224
  147.4 0.0 copy-done.4
  147.4 6.5 %all-gather.5.cloned.1.call-done = f32[1024,1664]{1,0:T(8,128)} async-done(((f32[128,1664]{1,0:T(8,128)}), f32[1024,1664]{1,0:T(8,128)}) %all-gather.5.cloned.1.call-update) | async-done | bytes 6815760 | tf_op jit(solution)/shard_map/all_gather | solution.py:221
  153.9 0.0 slice-start
  153.9 6.2 %fusion = f32[1024,128]{1,0:T(8,128)S(1)} fusion(f32[1024,128]{1,0:T(8,128)} %fusion.1, f32[1024,1664]{1,0:T(8,128)} %all-gather.5.cloned.1.call-done, f32[128,3456]{1,0:T(8,128)} %copy-done.4), kind=kOutput, calls=%fused_computation.4 | convolution fusion | flops 1308884992 | bytes 8716288 | tf_op jit(solution)/shard_map/jc,ic->ji/dot_general | solution.py:224
  160.1 27.5 %all_to_all.76 = f32[32,32,128]{2,1,0:T(8,128)} all-to-all(f32[32,32,128]{2,1,0:T(8,128)S(1)} %bitcast.39), channel_id=1, replica_groups=mesh['x'=4,'zl'=2,'y'=4,'core'=2,'zh'=4] {'y','zl','zh'}, dimensions={0} | all-to-all | bytes 1048576 | tf_op jit(solution)/shard_map/all_to_all | solution.py:226
  187.7 1.1 reduce_sum.9
  188.8 0.0 slice-start.1
  188.8 0.1 broadcast_in_dim.2
  188.8 21.9 %all_to_all.77 = f32[32,32,128]{2,1,0:T(8,128)S(1)} all-to-all(f32[32,32,128]{2,1,0:T(8,128)S(1)} %broadcast_in_dim.2), channel_id=1, replica_groups=mesh['x'=4,'zl'=2,'y'=4,'core'=2,'zh'=4] {'y','zl','zh'}, dimensions={0} | all-to-all | bytes 1048576 | tf_op jit(solution)/shard_map/all_to_all | solution.py:230
  210.7 5.3 %convolution_subtract_fusion = f32[128,1664]{1,0:T(8,128)S(1)} fusion(f32[1024,128]{1,0:T(8,128)S(1)} %bitcast.36, f32[1024,1664]{1,0:T(8,128)} %all-gather.5.cloned.1.call-done, f32[128,3456]{1,0:T(8,128)} %copy-done.4), kind=kOutput, calls=%fused_computation | convolution fusion | flops 1308835840 | bytes 9043968 | tf_op jit(solution)/shard_map/ji,jc->ic/dot_general | solution.py:234
  216.0 0.0 slice-done
  216.0 0.0 slice-done.1
  216.0 0.0 copy-done.5
  216.0 2.0 convolution_subtract_fusion.1
  218.0 0.1 pad_maximum_fusion
  218.1 0.5 all_to_all.64
  218.7 48.1 %all_to_all.78 = f32[32,4,3456]{2,1,0:T(4,128)S(1)} all-to-all(f32[32,4,3456]{2,1,0:T(4,128)S(1)} %all_to_all.64), channel_id=1, replica_groups=mesh['x'=4,'zl'=2,'y'=4,'core'=2,'zh'=4] {'y','zl','zh'}, dimensions={0} | all-to-all | bytes 3538944 | tf_op jit(solution)/shard_map/all_to_all | solution.py:236
  266.8 1.2 copy.16
  (2 shorter events, 0.0 us)
Async XLA Ops:
  6.5 13.4 %copy-start = (f32[4,110592]{1,0:T(4,128)S(1)}, f32[4,110592]{1,0:T(4,128)}, u32[]{:S(2)}) copy-start(f32[4,110592]{1,0:T(4,128)} %psi_ref.1) | copy-start | bytes 5308420
  8.8 12.2 %copy-start.7 = (f32[110592]{0:T(1024)S(1)}, f32[110592]{0:T(1024)}, u32[]{:S(2)}) copy-start(f32[110592]{0:T(1024)} %param.5) | copy-start | bytes 1327108
  8.8 13.0 %copy-start.2 = (f32[16]{0:T(128)S(1)}, f32[16]{0:T(128)}, u32[]{:S(2)}) copy-start(f32[16]{0:T(128)} %magic_ref.1) | copy-start | bytes 196
  8.8 13.0 %copy-start.3 = (f32[29]{0:T(128)S(1)}, f32[29]{0:T(128)}, u32[]{:S(2)}) copy-start(f32[29]{0:T(128)} %kinetic_ref.1) | copy-start | bytes 352
  8.8 45.8 %all-to-all-start = ((f32[4,32,1792]{2,0,1:T(4,128)}), f32[4,32,1792]{2,0,1:T(4,128)}, u32[]{:S(2)}, u32[]{:S(2)}) async-start(f32[4,32,1792]{2,0,1:T(4,128)} %slice.16), calls=%async_computation | async-start | bytes 1835008 | tf_op jit(solution)/shard_map/all_to_all | solution.py:207
  19.9 119.8 %all-gather.3.cloned.1.call-start = ((), (), s32[]{:S(2)}) async-start(), calls=%async_computation.6 | async-start | bytes 8257536 | tf_op jit(solution)/shard_map/all_gather | solution.py:218
  21.9 1.0 copy-start.1
  54.6 2.6 copy-start.6
  57.1 96.8 %all-gather.5.cloned.1.call-start = ((), (), s32[]{:S(2)}) async-start(), calls=%async_computation.7 | async-start | bytes 7667712 | tf_op jit(solution)/shard_map/all_gather | solution.py:221
  139.7 7.7 %copy-start.4 = (f32[128,3456]{1,0:T(8,128)}, f32[128,3456]{1,0:T(8,128)S(1)}, u32[]{:S(2)}) copy-start(f32[128,3456]{1,0:T(8,128)S(1)} %reshape.36) | copy-start | bytes 5308420
  153.9 62.1 %slice-start = ((s8[7340032]{0:T(1024)(128)(4,1)}), s8[3145728]{0:T(1024)(128)(4,1)S(1)}, s32[]{:S(2)}) async-start(s8[7340032]{0:T(1024)(128)(4,1)} %bitcast.32), calls=%async_computation.8 | async-start | bytes 6291456
  188.8 27.2 %slice-start.1 = ((s8[7340032]{0:T(1024)(128)(4,1)}), s8[4194304]{0:T(1024)(128)(4,1)S(1)}, s32[]{:S(2)}) async-start(s8[7340032]{0:T(1024)(128)(4,1)} %bitcast.32), calls=%async_computation.9 | async-start | bytes 8388608
  210.7 5.3 %copy-start.5 = (f32[128,3456]{1,0:T(8,128)S(1)}, f32[128,3456]{1,0:T(8,128)}, u32[]{:S(2)}) copy-start(f32[128,3456]{1,0:T(8,128)} %copy-done.4) | copy-start | bytes 5308420
Sparse Core Ops, SparseCore 0:
  57.2 48.9 all-gather.2
  108.1 45.7 all-gather.4

commit v2 on v0

--- a/solution.py
+++ b/solution.py
@@ -10,7 +10,6 @@
 SPLIT = (4, 2, 4, 2, 4)
 NAMES = ("x", "zl", "y", "core", "zh")
 COEF = ("y", "zl", "zh")
-PANEL = ("x", "core")
 NSPLIT = 32
 HIGH = lax.Precision.HIGH
 PLANE = G * G
@@ -195,30 +194,61 @@
             pltpu.VMEM((2 * rows, rows), BF16),
         ],
         compiler_params=pltpu.CompilerParams(vmem_limit_bytes=48 * 1024 * 1024),
+        cost_estimate=pl.CostEstimate(
+            flops=24_000_000_000, transcendentals=0, bytes_accessed=12 * orbitals.size
+        ),
         name="hamiltonian",
     )(magic_taps, kinetic_taps, orbitals, potential.reshape(G, PLANE))
 
 
 def to_cols(block):
-    return lax.all_to_all(block, COEF, split_axis=1, concat_axis=0, tiled=True)
+    pieces = block.reshape(block.shape[0], NSPLIT, -1).transpose(1, 0, 2)
+    return lax.all_to_all(pieces, COEF, split_axis=0, concat_axis=0, tiled=True)
+
+
+def flat(pieces):
+    return pieces.reshape(-1, pieces.shape[-1])
+
+
+def step_x(pieces, step):
+    return lax.ppermute(pieces, "x", [(i, (i + step) % 4) for i in range(4)])
+
+
+def swap_core(value):
+    return lax.ppermute(value, "core", [(0, 1), (1, 0)])
 
 
 def shards(orbitals, potential, magic_taps, kinetic_taps):
-    psi_cols = to_cols(orbitals)
-    psi_every = lax.all_gather(psi_cols, PANEL, axis=0, tiled=True)
+    own = to_cols(orbitals)
     hpsi = hamiltonian(orbitals, potential, magic_taps, kinetic_taps)
+    own, hpsi = lax.optimization_barrier((own, hpsi))
+    left, right = step_x(own, 1), step_x(own, -1)
     hpsi_cols = to_cols(hpsi)
-    part = jnp.einsum("jc,ic->ji", psi_every, hpsi_cols, precision=HIGH) * (1.0 / NC)
+    half = NSPLIT // 2
+    far_a, far_b = step_x(left[:half], 1), step_x(right[half:], -1)
+    hpsi_swap = swap_core(hpsi_cols)
+    both = jnp.concatenate([flat(hpsi_cols), flat(hpsi_swap)], axis=0)
+    panels = [flat(v) for v in (own, left, right, far_a, far_b)]
+    part = jnp.concatenate(
+        [jnp.einsum("jc,ic->ji", psi, both, precision=HIGH) for psi in panels], axis=0
+    ) * (1.0 / NC)
     rows = part.shape[0] // NSPLIT
-    pieces = lax.all_to_all(
+    terms = lax.all_to_all(
         part.reshape(NSPLIT, rows, -1), COEF, split_axis=0, concat_axis=0, tiled=True
     )
-    mine = jnp.sum(pieces, axis=0)
+    mine = jnp.sum(terms, axis=0)
     margin = lax.all_to_all(
-        jnp.broadcast_to(mine[None], pieces.shape), COEF, split_axis=0, concat_axis=0, tiled=True
+        jnp.broadcast_to(mine[None], terms.shape), COEF, split_axis=0, concat_axis=0, tiled=True
     ).reshape(part.shape)
-    grad_cols = hpsi_cols - jnp.einsum("ji,jc->ic", margin, psi_every, precision=HIGH)
-    return lax.all_to_all(grad_cols, COEF, split_axis=0, concat_axis=1, tiled=True)
+    stack = jnp.concatenate(panels, axis=0)
+    cols = margin.shape[1] // 2
+    other = jnp.einsum("ji,jc->ic", margin[:, cols:], stack, precision=HIGH)
+    from_other = swap_core(other)
+    grad_cols = flat(hpsi_cols) - jnp.einsum("ji,jc->ic", margin[:, :cols], stack, precision=HIGH) - from_other
+    back = lax.all_to_all(
+        grad_cols.reshape(hpsi_cols.shape), COEF, split_axis=0, concat_axis=0, tiled=True
+    )
+    return back.transpose(1, 0, 2).reshape(orbitals.shape)
 
 
 def solution(mesh):

time: 262 us -> 264 us (level)
  blocking collectives: 192 us -> 49.3 us
  waiting for transfers between devices: 0.04 us -> 93.3 us
  starting transfers between devices: 0.01 us -> 34 us
  local copies, waits for them, and re-layouts: 5.83 us -> 33 us
  between operations: 13.5 us -> 0.27 us
    all_to_all x5 -> x1, blocking collectives: 192 us -> 49.3 us  [shards(): lax.all_to_all(grad_cols.reshape(hpsi_cols.shape), COEF, split_axis=0, co...]
    all_to_all x0 -> x4, waiting for transfers between devices: none -> 75.3 us  [the longest x2 50.1 us: to_cols(): return lax.all_to_all(pieces, COEF, split_axis=0, concat_axis=0, tiled=True)]
    all_to_all x0 -> x4, starting transfers between devices: none -> 28.3 us  [the longest x2 17.2 us: to_cols(): return lax.all_to_all(pieces, COEF, split_axis=0, concat_axis=0, tiled=True)]
    ppermute x0 -> x6, waiting for transfers between devices: none -> 18 us  [the longest x4 14.3 us: step_x(): return lax.ppermute(pieces, 'x', [(i, (i + step) % 4) for i in range(4)])]
    reshape x0 -> x8, local copies, waits for them, and re-layouts: none -> 17.7 us  [the longest x7 17.2 us: flat(): return pieces.reshape(-1, pieces.shape[-1])]
    unnamed x9 -> x34, local copies, waits for them, and re-layouts: 2.57 us -> 9.63 us
    ppermute x0 -> x6, starting transfers between devices: none -> 5.7 us  [the longest x4 5.6 us: step_x(): return lax.ppermute(pieces, 'x', [(i, (i + step) % 4) for i in range(4)])]
    all_to_all x3 -> x0, local copies, waits for them, and re-layouts: 2.94 us -> none  [the longest x2 2.42 us: to_cols(): return lax.all_to_all(block, COEF, split_axis=1, concat_axis=0, tiled=True)]
  transfers between devices with their start and end apart: 1 -> 10, of which waited for: 0 -> 7; matrix products, arithmetic and copies ran while one was open for 0% -> 10% of each run, Pallas kernels for 12% -> 12%
where the time goes in v2:
time: 264 us
  waiting for transfers between devices  93.3 us (35%)
  blocking collectives  49.3 us (19%)
  starting transfers between devices  34 us (13%)
  local copies, waits for them, and re-layouts  33 us (12%)
  Pallas kernels  32.9 us (12%)
  matrix products  19 us (7%)
    all_to_all x2, waiting for transfers between devices, to_cols(): return lax.all_to_all(pieces, COEF, split_axis=0, concat_axis=0, tiled=True)  50.1 us
    all_to_all x1, blocking collectives, shards(): lax.all_to_all(grad_cols.reshape(hpsi_cols.shape), COEF, split_axis=0, co...  49.3 us
    pallas_call x1, Pallas kernels, hamiltonian(): pl.pallas_call(h_kernel, out_shape=jax.ShapeDtypeStruct(orbitals.shape, F...  32.9 us
    all_to_all x2, starting transfers between devices, to_cols(): return lax.all_to_all(pieces, COEF, split_axis=0, concat_axis=0, tiled=True)  17.2 us
    reshape x7, local copies, waits for them, and re-layouts, flat(): return pieces.reshape(-1, pieces.shape[-1])  17.2 us
    ppermute x4, waiting for transfers between devices, step_x(): return lax.ppermute(pieces, 'x', [(i, (i + step) % 4) for i in range(4)])  14.3 us
    all_to_all x1, waiting for transfers between devices, shards(): lax.all_to_all(jnp.broadcast_to(mine[None], terms.shape), COEF, split_axi...  13.2 us
    all_to_all x1, waiting for transfers between devices, shards(): lax.all_to_all(part.reshape(NSPLIT, rows, -1), COEF, split_axis=0, concat...  12.1 us
  transfers between devices with their start and end apart: 10, of which 7 were waited for; matrix products, arithmetic and copies ran while one was open for 10% of the time, Pallas kernels for 12%

profile of v2, /device:TPU:64, one launch (start us, length us, event | category | flops | bytes accessed | tf_op | source)
XLA Modules:
  0.0 263.7 jit_solution(16204481867703931986)
XLA Ops:
  0.0 11.1 %all-to-all-start = ((f32[32,4,3456]{2,1,0:T(4,128)}), f32[32,4,3456]{2,1,0:T(4,128)}, u32[]{:S(2)}, u32[]{:S(2)}) async-start(f32[32,4,3456]{2,1,0:T(4,128)} %bitcast.23), calls=%async_computation | async-start | bytes 3538944 | tf_op jit(solution)/shard_map/all_to_all | solution.py:206
  11.1 0.1 reshape.46.pot_ref
  11.2 32.9 %hamiltonian.1 = f32[4,110592]{1,0:T(4,128)} custom-call(f32[16]{0:T(128)S(1)} %copy-done.1, f32[29]{0:T(128)S(1)} %copy-done.2, f32[4,110592]{1,0:T(4,128)S(1)} %copy-done, f32[48,2304]{1,0:T(8,128)S(1)} %reshape.46.pot_ref), custom_call_target="tpu_custom_call" | custom-call | flops 24000000000 | bytes 5308416 | tf_op jit(solution)/shard_map/hamiltonian/pallas_call | solution.py:178
  44.1 10.1 %all-to-all-done = f32[32,4,3456]{2,1,0:T(4,128)} async-done(((f32[32,4,3456]{2,1,0:T(4,128)}), f32[32,4,3456]{2,1,0:T(4,128)}, u32[]{:S(2)}, u32[]{:S(2)}) %all-to-all-start) | async-done | bytes 1769504 | tf_op jit(solution)/shard_map/all_to_all | solution.py:206
  54.3 6.1 %all-to-all-start.1 = ((f32[32,4,3456]{2,1,0:T(4,128)}), f32[32,4,3456]{2,1,0:T(4,128)}, u32[]{:S(2)}, u32[]{:S(2)}) async-start(f32[32,4,3456]{2,1,0:T(4,128)} %bitcast.3), calls=%async_computation.1 | async-start | bytes 3538944 | tf_op jit(solution)/shard_map/all_to_all | solution.py:206
  60.4 2.8 %collective-permute-start.2 = (f32[32,4,3456]{2,1,0:T(4,128)}, f32[32,4,3456]{2,1,0:T(4,128)S(1)}, u32[]{:S(2)}, u32[]{:S(2)}) collective-permute-start(f32[32,4,3456]{2,1,0:T(4,128)} %all-to-all-done), channel_id=1, source_target_pairs={{0,192},{64,0},{128,64},{192,128},{1,193},{65,1},{129,65},{193,129... | collective-permute-start | bytes 5308424 | tf_op jit(solution)/shard_map/ppermute | solution.py:214
  63.2 0.0 collective-permute-start.1
  63.2 40.0 %all-to-all-done.1 = f32[32,4,3456]{2,1,0:T(4,128)} async-done(((f32[32,4,3456]{2,1,0:T(4,128)}), f32[32,4,3456]{2,1,0:T(4,128)}, u32[]{:S(2)}, u32[]{:S(2)}) %all-to-all-start.1) | async-done | bytes 1769504 | tf_op jit(solution)/shard_map/all_to_all | solution.py:206
  103.2 0.0 collective-permute-done.2
  103.2 1.0 slice.17
  104.2 2.8 %collective-permute-start.4 = (f32[16,4,3456]{2,1,0:T(4,128)}, f32[16,4,3456]{2,1,0:T(4,128)}, u32[]{:S(2)}, u32[]{:S(2)}) collective-permute-start(f32[16,4,3456]{2,1,0:T(4,128)} %slice.17), channel_id=1, source_target_pairs={{0,192},{64,0},{128,64},{192,128},{1,193},{65,1},{129,65},{193,129... | collective-permute-start | bytes 2654216 | tf_op jit(solution)/shard_map/ppermute | solution.py:214
  107.0 1.0 slice.16
  108.0 2.8 %reshape.49 = f32[128,3456]{1,0:T(8,128)} reshape(f32[32,4,3456]{2,1,0:T(4,128)} %all-to-all-done) | data formatting | bytes 3538944 | tf_op jit(solution)/shard_map/reshape | solution.py:210
  110.8 1.8 reshape.52
  112.7 1.8 reshape.51
  114.5 12.4 %collective-permute-done.4 = f32[16,4,3456]{2,1,0:T(4,128)} collective-permute-done((f32[16,4,3456]{2,1,0:T(4,128)}, f32[16,4,3456]{2,1,0:T(4,128)}, u32[]{:S(2)}, u32[]{:S(2)}) %collective-permute-start.4) | collective-permute-done | bytes 884768 | tf_op jit(solution)/shard_map/ppermute | solution.py:214
  126.9 2.5 reshape.54
  129.3 2.0 collective-permute-done.3
  131.3 2.4 reshape.53
  133.7 2.9 %reshape.48 = f32[128,3456]{1,0:T(8,128)} reshape(f32[32,4,3456]{2,1,0:T(4,128)} %all-to-all-done.1) | data formatting | bytes 3538944 | tf_op jit(solution)/shard_map/reshape | solution.py:210
  136.6 1.6 constant_dynamic-update-slice_fusion.1
  138.2 2.9 %reshape.50 = f32[128,3456]{1,0:T(8,128)} reshape(f32[32,4,3456]{2,1,0:T(4,128)} %collective-permute-done) | data formatting | bytes 3538944 | tf_op jit(solution)/shard_map/reshape | solution.py:210
  141.1 1.7 constant_dynamic-update-slice_fusion
  142.8 0.3 copy-done.6
  143.1 1.6 convolution_dynamic-update-slice_fusion.2
  144.8 1.6 convolution_dynamic-update-slice_fusion.1
  146.4 1.6 convolution_dynamic-update-slice_fusion
  148.1 1.6 convolution_dynamic-update-slice_fusion.4
  149.7 1.6 convolution_dynamic-update-slice_fusion.3
  151.4 0.8 broadcast_multiply_fusion
  152.2 5.8 %all-to-all-start.2 = ((f32[32,16,256]{2,1,0:T(8,128)}), f32[32,16,256]{2,1,0:T(8,128)}, u32[]{:S(2)}, u32[]{:S(2)}) async-start(f32[32,16,256]{2,1,0:T(8,128)} %bitcast.4), calls=%async_computation.2 | async-start | bytes 1048576 | tf_op jit(solution)/shard_map/all_to_all | solution.py:236
  158.1 2.8 %constant_dynamic-update-slice_fusion.6 = f32[512,3456]{1,0:T(8,128)} fusion(f32[128,3456]{1,0:T(8,128)} %reshape.49), kind=kLoop, calls=%fused_computation.17 | loop fusion | bytes 3538944
  160.9 1.3 constant_dynamic-update-slice_fusion.5
  162.2 12.1 %all-to-all-done.2 = f32[32,16,256]{2,1,0:T(8,128)} async-done(((f32[32,16,256]{2,1,0:T(8,128)}), f32[32,16,256]{2,1,0:T(8,128)}, u32[]{:S(2)}, u32[]{:S(2)}) %all-to-all-start.2) | async-done | bytes 524320 | tf_op jit(solution)/shard_map/all_to_all | solution.py:236
  174.3 1.1 reduce_sum.9
  175.4 0.9 broadcast_in_dim.2
  176.3 5.3 %all-to-all-start.3 = ((f32[32,16,256]{2,1,0:T(8,128)}), f32[32,16,256]{2,1,0:T(8,128)}, u32[]{:S(2)}, u32[]{:S(2)}) async-start(f32[32,16,256]{2,1,0:T(8,128)} %broadcast_in_dim.2), calls=%async_computation.3 | async-start | bytes 1048576 | tf_op jit(solution)/shard_map/all_to_all | solution.py:240
  181.6 1.4 constant_dynamic-update-slice_fusion.4
  182.9 1.0 constant_dynamic-update-slice_fusion.3
  183.9 1.0 constant_dynamic-update-slice_fusion.2
  184.9 13.2 %all-to-all-done.3 = f32[32,16,256]{2,1,0:T(8,128)} async-done(((f32[32,16,256]{2,1,0:T(8,128)}), f32[32,16,256]{2,1,0:T(8,128)}, u32[]{:S(2)}, u32[]{:S(2)}) %all-to-all-start.3) | async-done | bytes 524320 | tf_op jit(solution)/shard_map/all_to_all | solution.py:240
  198.1 5.4 %fusion.1 = f32[128,3456]{1,0:T(8,128)S(1)} fusion(f32[512,3456]{1,0:T(8,128)} %constant_dynamic-update-slice_fusion.2, f32[512,256]{1,0:T(8,128)} %bitcast.5), kind=kOutput, calls=%fused_computation.7 | convolution fusion | flops 1358954496 | bytes 9109504 | tf_op jit(solution)/shard_map/ji,jc->ic/dot_general | solution.py:245
  203.5 0.1 collective-permute-start.5
  203.6 3.7 %collective-permute-done.5 = f32[128,3456]{1,0:T(8,128)S(1)} collective-permute-done((f32[128,3456]{1,0:T(8,128)S(1)}, f32[128,3456]{1,0:T(8,128)S(1)}, u32[]{:S(2)}, u32[]{:S(2)}) %collective-permute-start.5) | collective-permute-done | bytes 1769504 | tf_op jit(solution)/shard_map/ppermute | solution.py:218
  207.3 5.4 %fusion = f32[128,3456]{1,0:T(8,128)S(1)} fusion(f32[128,3456]{1,0:T(8,128)S(1)} %collective-permute-done.5, f32[128,3456]{1,0:T(8,128)S(1)} %copy-done.3, f32[512,3456]{1,0:T(8,128)} %constant_dynamic-update-slice_fusion.2, f32[512,256]{1,0:T(8,128)} %bitcast.5), kind=kOutput, calls=%fused_computation.1 | convolution fusion | flops 1359839232 | bytes 12648448 | tf_op jit(solution)/shard_map/ji,jc->ic/dot_general | solution.py:247
  212.7 0.5 reshape.56
  213.2 49.3 %all_to_all.25 = f32[32,4,3456]{2,1,0:T(4,128)S(1)} all-to-all(f32[32,4,3456]{2,1,0:T(4,128)S(1)} %reshape.56), channel_id=1, replica_groups=mesh['x'=4,'zl'=2,'y'=4,'core'=2,'zh'=4] {'y','zl','zh'}, dimensions={0} | all-to-all | bytes 3538944 | tf_op jit(solution)/shard_map/all_to_all | solution.py:248
  262.5 1.2 copy.25
  (31 shorter events, 0.1 us)
Async XLA Ops:
  0.0 11.2 %copy-start = (f32[4,110592]{1,0:T(4,128)S(1)}, f32[4,110592]{1,0:T(4,128)}, u32[]{:S(2)}) copy-start(f32[4,110592]{1,0:T(4,128)} %psi_ref.1) | copy-start | bytes 5308420
  0.0 11.1 %copy-start.13 = (f32[110592]{0:T(1024)S(1)}, f32[110592]{0:T(1024)}, u32[]{:S(2)}) copy-start(f32[110592]{0:T(1024)} %param.5) | copy-start | bytes 1327108
  0.0 11.2 %copy-start.2 = (f32[29]{0:T(128)S(1)}, f32[29]{0:T(128)}, u32[]{:S(2)}) copy-start(f32[29]{0:T(128)} %kinetic_ref.1) | copy-start | bytes 352
  0.0 11.2 %copy-start.1 = (f32[16]{0:T(128)S(1)}, f32[16]{0:T(128)}, u32[]{:S(2)}) copy-start(f32[16]{0:T(128)} %magic_ref.1) | copy-start | bytes 196
  0.0 54.3 %all-to-all-start = ((f32[32,4,3456]{2,1,0:T(4,128)}), f32[32,4,3456]{2,1,0:T(4,128)}, u32[]{:S(2)}, u32[]{:S(2)}) async-start(f32[32,4,3456]{2,1,0:T(4,128)} %bitcast.23), calls=%async_computation | async-start | bytes 3538944 | tf_op jit(solution)/shard_map/all_to_all | solution.py:206
  54.3 48.9 %all-to-all-start.1 = ((f32[32,4,3456]{2,1,0:T(4,128)}), f32[32,4,3456]{2,1,0:T(4,128)}, u32[]{:S(2)}, u32[]{:S(2)}) async-start(f32[32,4,3456]{2,1,0:T(4,128)} %bitcast.3), calls=%async_computation.1 | async-start | bytes 3538944 | tf_op jit(solution)/shard_map/all_to_all | solution.py:206
  60.4 42.8 %collective-permute-start.2 = (f32[32,4,3456]{2,1,0:T(4,128)}, f32[32,4,3456]{2,1,0:T(4,128)S(1)}, u32[]{:S(2)}, u32[]{:S(2)}) collective-permute-start(f32[32,4,3456]{2,1,0:T(4,128)} %all-to-all-done), channel_id=1, source_target_pairs={{0,192},{64,0},{128,64},{192,128},{1,193},{65,1},{129,65},{193,129... | collective-permute-start | bytes 5308424 | tf_op jit(solution)/shard_map/ppermute | solution.py:214
  63.2 43.8 %collective-permute-start.1 = (f32[32,4,3456]{2,1,0:T(4,128)}, f32[32,4,3456]{2,1,0:T(4,128)S(1)}, u32[]{:S(2)}, u32[]{:S(2)}) collective-permute-start(f32[32,4,3456]{2,1,0:T(4,128)} %all-to-all-done), channel_id=1, source_target_pairs={{0,64},{64,128},{128,192},{192,0},{1,65},{65,129},{129,193},{193,1... | collective-permute-start | bytes 5308424 | tf_op jit(solution)/shard_map/ppermute | solution.py:214
  103.2 35.0 %collective-permute-start = (f32[32,4,3456]{2,1,0:T(4,128)}, f32[32,4,3456]{2,1,0:T(4,128)}, u32[]{:S(2)}, u32[]{:S(2)}) collective-permute-start(f32[32,4,3456]{2,1,0:T(4,128)} %all-to-all-done.1), channel_id=1, source_target_pairs={{0,4},{4,0},{1,5},{5,1},{2,6},{6,2},{3,7},{7,3},{8,12},{12,8},{9,1... | collective-permute-start | bytes 5308424 | tf_op jit(solution)/shard_map/ppermute | solution.py:218
  104.2 22.7 %collective-permute-start.4 = (f32[16,4,3456]{2,1,0:T(4,128)}, f32[16,4,3456]{2,1,0:T(4,128)}, u32[]{:S(2)}, u32[]{:S(2)}) collective-permute-start(f32[16,4,3456]{2,1,0:T(4,128)} %slice.17), channel_id=1, source_target_pairs={{0,192},{64,0},{128,64},{192,128},{1,193},{65,1},{129,65},{193,129... | collective-permute-start | bytes 2654216 | tf_op jit(solution)/shard_map/ppermute | solution.py:214
  108.0 23.3 %collective-permute-start.3 = (f32[16,4,3456]{2,1,0:T(4,128)}, f32[16,4,3456]{2,1,0:T(4,128)}, u32[]{:S(2)}, u32[]{:S(2)}) collective-permute-start(f32[16,4,3456]{2,1,0:T(4,128)} %slice.16), channel_id=1, source_target_pairs={{0,64},{64,128},{128,192},{192,0},{1,65},{65,129},{129,193},{193,1... | collective-permute-start | bytes 2654216 | tf_op jit(solution)/shard_map/ppermute | solution.py:214
  141.1 2.0 copy-start.6
  143.1 1.6 copy-start.7
  144.7 1.7 copy-start.4
  146.4 1.7 copy-start.11
  148.1 1.7 copy-start.9
  151.4 9.5 %copy-start.8 = (f32[128,3456]{1,0:T(8,128)S(1)}, f32[128,3456]{1,0:T(8,128)}, u32[]{:S(2)}) copy-start(f32[128,3456]{1,0:T(8,128)} %reshape.51) | copy-start | bytes 5308420
  152.2 22.1 %all-to-all-start.2 = ((f32[32,16,256]{2,1,0:T(8,128)}), f32[32,16,256]{2,1,0:T(8,128)}, u32[]{:S(2)}, u32[]{:S(2)}) async-start(f32[32,16,256]{2,1,0:T(8,128)} %bitcast.4), calls=%async_computation.2 | async-start | bytes 1048576 | tf_op jit(solution)/shard_map/all_to_all | solution.py:236
  160.9 20.7 %copy-start.5 = (f32[128,3456]{1,0:T(8,128)S(1)}, f32[128,3456]{1,0:T(8,128)}, u32[]{:S(2)}) copy-start(f32[128,3456]{1,0:T(8,128)} %reshape.52) | copy-start | bytes 5308420
  162.2 20.7 %copy-start.12 = (f32[64,3456]{1,0:T(8,128)S(1)}, f32[64,3456]{1,0:T(8,128)}, u32[]{:S(2)}) copy-start(f32[64,3456]{1,0:T(8,128)} %reshape.53) | copy-start | bytes 2654212
  175.4 8.5 %copy-start.10 = (f32[64,3456]{1,0:T(8,128)S(1)}, f32[64,3456]{1,0:T(8,128)}, u32[]{:S(2)}) copy-start(f32[64,3456]{1,0:T(8,128)} %reshape.54) | copy-start | bytes 2654212
  176.3 21.8 %all-to-all-start.3 = ((f32[32,16,256]{2,1,0:T(8,128)}), f32[32,16,256]{2,1,0:T(8,128)}, u32[]{:S(2)}, u32[]{:S(2)}) async-start(f32[32,16,256]{2,1,0:T(8,128)} %broadcast_in_dim.2), calls=%async_computation.3 | async-start | bytes 1048576 | tf_op jit(solution)/shard_map/all_to_all | solution.py:240
  198.1 9.2 %copy-start.3 = (f32[128,3456]{1,0:T(8,128)S(1)}, f32[128,3456]{1,0:T(8,128)}, u32[]{:S(2)}) copy-start(f32[128,3456]{1,0:T(8,128)} %reshape.48) | copy-start | bytes 5308420
  203.5 3.8 %collective-permute-start.5 = (f32[128,3456]{1,0:T(8,128)S(1)}, f32[128,3456]{1,0:T(8,128)S(1)}, u32[]{:S(2)}, u32[]{:S(2)}) collective-permute-start(f32[128,3456]{1,0:T(8,128)S(1)} %fusion.1), channel_id=1, source_target_pairs={{0,4},{4,0},{1,5},{5,1},{2,6},{6,2},{3,7},{7,3},{8,12},{12,8},{9,1... | collective-permute-start | bytes 5308424 | tf_op jit(solution)/shard_map/ppermute | solution.py:218

commit v3 on v2

--- a/solution.py
+++ b/solution.py
@@ -1,3 +1,5 @@
+import functools
+
 import jax
 import jax.numpy as jnp
 from jax import lax
@@ -11,7 +13,7 @@
 NAMES = ("x", "zl", "y", "core", "zh")
 COEF = ("y", "zl", "zh")
 NSPLIT = 32
-HIGH = lax.Precision.HIGH
+CHUNK = 384
 PLANE = G * G
 BLK = 16 * G
 F32 = jnp.float32
@@ -206,16 +208,122 @@
     return lax.all_to_all(pieces, COEF, split_axis=0, concat_axis=0, tiled=True)
 
 
-def flat(pieces):
-    return pieces.reshape(-1, pieces.shape[-1])
-
-
 def step_x(pieces, step):
     return lax.ppermute(pieces, "x", [(i, (i + step) % 4) for i in range(4)])
 
 
 def swap_core(value):
     return lax.ppermute(value, "core", [(0, 1), (1, 0)])
+
+
+def rows_of(ref, scratch, start):
+    count = ref.shape[0]
+    for s in range(count):
+        scratch[start + 4 * s:start + 4 * s + 4, :] = ref[s]
+
+
+NT = (((1,), (1,)), ((), ()))
+
+
+def margin_kernel(*refs):
+    panels, (own_ref, swap_ref, out_ref, psi, hps) = refs[:-5], refs[-5:]
+    rows_of(own_ref, hps, 0)
+    rows_of(swap_ref, hps, hps.shape[0] // 2)
+    at = 0
+    for ref in panels:
+        rows_of(ref, psi, at)
+        at += 4 * ref.shape[0]
+    h_hi, h_lo = split_bf16(hps[...])
+    p_hi, p_lo = split_bf16(psi[...])
+
+    def times(a, b):
+        return lax.dot_general(a, b, NT, preferred_element_type=F32)
+
+    total = (times(p_hi, h_hi) + times(p_hi, h_lo) + times(p_lo, h_hi)) * (1.0 / NC)
+
+    @pl.when(pl.program_id(0) == 0)
+    def _():
+        out_ref[...] = total
+
+    @pl.when(pl.program_id(0) > 0)
+    def _():
+        out_ref[...] += total
+
+
+def chunk_spec(array):
+    return pl.BlockSpec((array.shape[0], array.shape[1], CHUNK), lambda k: (0, 0, k))
+
+
+def margin_part(panels, own, swap):
+    rows = sum(4 * v.shape[0] for v in panels)
+    cols = 8 * own.shape[0]
+    width = own.shape[2]
+    arrays = [*panels, own, swap]
+    return pl.pallas_call(
+        margin_kernel,
+        grid=(width // CHUNK,),
+        out_shape=jax.ShapeDtypeStruct((rows, cols), F32),
+        in_specs=[chunk_spec(v) for v in arrays],
+        out_specs=pl.BlockSpec((rows, cols), lambda k: (0, 0)),
+        scratch_shapes=[pltpu.VMEM((rows, CHUNK), F32), pltpu.VMEM((cols, CHUNK), F32)],
+        cost_estimate=pl.CostEstimate(
+            flops=6 * rows * cols * width, transcendentals=0, bytes_accessed=4 * (rows + cols) * width
+        ),
+        compiler_params=pltpu.CompilerParams(vmem_limit_bytes=40 * 1024 * 1024),
+        name="margin_part",
+    )(*arrays)
+
+
+def rotate_kernel(column, negate, *refs):
+    if negate:
+        base_ref, out_ref, psi, turn, res = refs[-5:]
+        panels = refs[1:-5]
+    else:
+        out_ref, psi, turn, res = refs[-4:]
+        panels = refs[1:-4]
+    margin_ref = refs[0]
+    cols = turn.shape[0] // 2
+
+    @pl.when(pl.program_id(0) == 0)
+    def _():
+        high, low = split_bf16(margin_ref[:, column * cols:(column + 1) * cols].T)
+        turn[0:cols, :] = high
+        turn[cols:, :] = low
+
+    at = 0
+    for ref in panels:
+        rows_of(ref, psi, at)
+        at += 4 * ref.shape[0]
+    p_hi, p_lo = split_bf16(psi[...])
+    both = jnp.dot(turn[...], p_hi, preferred_element_type=F32)
+    res[...] = both[0:cols] + both[cols:] + jnp.dot(turn[0:cols, :], p_lo, preferred_element_type=F32)
+    for s in range(out_ref.shape[0]):
+        value = res[4 * s:4 * s + 4, :]
+        out_ref[s] = base_ref[s] - value if negate else value
+
+
+def rotated(margin, panels, column, base=None):
+    rows, cols = margin.shape[0], margin.shape[1] // 2
+    shape = (cols // 4, 4, panels[0].shape[2])
+    arrays = [*panels] + ([] if base is None else [base])
+    return pl.pallas_call(
+        functools.partial(rotate_kernel, column, base is not None),
+        grid=(shape[2] // CHUNK,),
+        out_shape=jax.ShapeDtypeStruct(shape, F32),
+        in_specs=[pl.BlockSpec(margin.shape, lambda k: (0, 0))] + [chunk_spec(v) for v in arrays],
+        out_specs=pl.BlockSpec((shape[0], 4, CHUNK), lambda k: (0, 0, k)),
+        scratch_shapes=[
+            pltpu.VMEM((rows, CHUNK), F32),
+            pltpu.VMEM((2 * cols, rows), BF16),
+            pltpu.VMEM((cols, CHUNK), F32),
+        ],
+        cost_estimate=pl.CostEstimate(
+            flops=6 * rows * cols * shape[2], transcendentals=0,
+            bytes_accessed=4 * (rows + 2 * cols) * shape[2],
+        ),
+        compiler_params=pltpu.CompilerParams(vmem_limit_bytes=40 * 1024 * 1024),
+        name="rotated",
+    )(margin, *arrays)
 
 
 def shards(orbitals, potential, magic_taps, kinetic_taps):
@@ -227,11 +335,9 @@
     half = NSPLIT // 2
     far_a, far_b = step_x(left[:half], 1), step_x(right[half:], -1)
     hpsi_swap = swap_core(hpsi_cols)
-    both = jnp.concatenate([flat(hpsi_cols), flat(hpsi_swap)], axis=0)
-    panels = [flat(v) for v in (own, left, right, far_a, far_b)]
-    part = jnp.concatenate(
-        [jnp.einsum("jc,ic->ji", psi, both, precision=HIGH) for psi in panels], axis=0
-    ) * (1.0 / NC)
+    near = margin_part([own, left, right], hpsi_cols, hpsi_swap)
+    far = margin_part([far_a, far_b], hpsi_cols, hpsi_swap)
+    part = jnp.concatenate([near, far], axis=0)
     rows = part.shape[0] // NSPLIT
     terms = lax.all_to_all(
         part.reshape(NSPLIT, rows, -1), COEF, split_axis=0, concat_axis=0, tiled=True
@@ -240,14 +346,10 @@
     margin = lax.all_to_all(
         jnp.broadcast_to(mine[None], terms.shape), COEF, split_axis=0, concat_axis=0, tiled=True
     ).reshape(part.shape)
-    stack = jnp.concatenate(panels, axis=0)
-    cols = margin.shape[1] // 2
-    other = jnp.einsum("ji,jc->ic", margin[:, cols:], stack, precision=HIGH)
-    from_other = swap_core(other)
-    grad_cols = flat(hpsi_cols) - jnp.einsum("ji,jc->ic", margin[:, :cols], stack, precision=HIGH) - from_other
-    back = lax.all_to_all(
-        grad_cols.reshape(hpsi_cols.shape), COEF, split_axis=0, concat_axis=0, tiled=True
-    )
+    panels = [own, left, right, far_a, far_b]
+    from_other = swap_core(rotated(margin, panels, 1))
+    grad_cols = rotated(margin, panels, 0, hpsi_cols) - from_other
+    back = lax.all_to_all(grad_cols, COEF, split_axis=0, concat_axis=0, tiled=True)
     return back.transpose(1, 0, 2).reshape(orbitals.shape)
 
 

time: 264 us -> 248 us (0.939)
  blocking collectives: 49.3 us -> 93.6 us
  waiting for transfers between devices: 93.3 us -> 58 us
  Pallas kernels: 32.9 us -> 60.2 us
  local copies, waits for them, and re-layouts: 33 us -> 9.43 us
  matrix products: 19 us -> 0 us
  starting transfers between devices: 34 us -> 23.9 us
    all_to_all x1 -> x3, blocking collectives: 49.3 us -> 93.6 us  [the longest x1 49.6 us: shards(): lax.all_to_all(grad_cols, COEF, split_axis=0, concat_axis=0, tiled=True)]
    pallas_call x0 -> x4, Pallas kernels: none -> 28.5 us  [the longest x2 16 us: rotated(): pl.pallas_call(functools.partial(rotate_kernel, column, base is not None)...]
    all_to_all x2 -> x0, waiting for transfers between devices: 25.3 us -> none  [the longest x1 13.2 us: shards(): lax.all_to_all(jnp.broadcast_to(mine[None], terms.shape), COEF, split_axi...]
    dot_general x7 -> x0, matrix products: 19 us -> none  [the longest x5 8.2 us: shards(): jnp.einsum('jc,ic->ji', psi, both, precision=HIGH)]
    reshape x8 -> x0, local copies, waits for them, and re-layouts: 17.7 us -> none  [the longest x7 17.2 us: flat(): return pieces.reshape(-1, pieces.shape[-1])]
    all_to_all x2 -> x0, starting transfers between devices: 11.1 us -> none  [the longest x1 5.82 us: shards(): lax.all_to_all(part.reshape(NSPLIT, rows, -1), COEF, split_axis=0, concat...]
    all_to_all x2, waiting for transfers between devices: 50.1 us -> 46.3 us  [to_cols(): return lax.all_to_all(pieces, COEF, split_axis=0, concat_axis=0, tiled=True)]
    ppermute x2, waiting for transfers between devices: 3.68 us -> 0.01 us  [swap_core(): return lax.ppermute(value, 'core', [(0, 1), (1, 0)])]
  transfers between devices with their start and end apart: 10 -> 8, of which waited for: 7 -> 4; matrix products, arithmetic and copies ran while one was open for 10% -> 1% of each run, Pallas kernels for 12% -> 19%
where the time goes in v3:
time: 248 us; the launch traced here: 247 us
  blocking collectives  93.6 us (38%)
  Pallas kernels  60.2 us (24%)
  waiting for transfers between devices  58 us (23%)
  starting transfers between devices  23.9 us (10%)
  local copies, waits for them, and re-layouts  9.43 us (4%)
    all_to_all x1, blocking collectives, shards(): lax.all_to_all(grad_cols, COEF, split_axis=0, concat_axis=0, tiled=True)  49.6 us
    all_to_all x2, waiting for transfers between devices, to_cols(): return lax.all_to_all(pieces, COEF, split_axis=0, concat_axis=0, tiled=True)  46.3 us
    pallas_call x1, Pallas kernels, hamiltonian(): pl.pallas_call(h_kernel, out_shape=jax.ShapeDtypeStruct(orbitals.shape, F...  31.7 us
    all_to_all x1, blocking collectives, shards(): lax.all_to_all(part.reshape(NSPLIT, rows, -1), COEF, split_axis=0, concat...  22.5 us
    all_to_all x1, blocking collectives, shards(): lax.all_to_all(jnp.broadcast_to(mine[None], terms.shape), COEF, split_axi...  21.6 us
    all_to_all x2, starting transfers between devices, to_cols(): return lax.all_to_all(pieces, COEF, split_axis=0, concat_axis=0, tiled=True)  17.1 us
    pallas_call x2, Pallas kernels, rotated(): pl.pallas_call(functools.partial(rotate_kernel, column, base is not None)...  16 us
    pallas_call x2, Pallas kernels, margin_part(): pl.pallas_call(margin_kernel, grid=(width // CHUNK,), out_shape=jax.Shape...  12.5 us
  transfers between devices with their start and end apart: 8, of which 4 were waited for; matrix products, arithmetic and copies ran while one was open for 1% of the time, Pallas kernels for 19%

profile of v3, /device:TPU:64, one launch (start us, length us, event | category | flops | bytes accessed | tf_op | source)
XLA Modules:
  0.0 246.9 jit_solution(6376052515860894203)
XLA Ops:
  0.0 0.0 copy-start.9
  0.0 0.0 copy-start.7
  0.0 0.0 copy-start.8
  0.0 11.0 %all-to-all-start = ((f32[32,4,3456]{2,1,0:T(4,128)}), f32[32,4,3456]{2,1,0:T(4,128)S(1)}, u32[]{:S(2)}, u32[]{:S(2)}) async-start(f32[32,4,3456]{2,1,0:T(4,128)} %bitcast.13), calls=%async_computation | async-start | bytes 3538944 | tf_op jit(solution)/shard_map/all_to_all | solution.py:208
  11.1 0.0 copy-done.9
  11.1 0.8 reshape.20.pot_ref
  11.9 0.0 copy-done.7
  11.9 0.0 copy-done.8
  11.9 0.0 copy-start.4
  11.9 1.5 copy-done.4
  13.4 0.0 copy-start.6
  13.4 1.0 copy-done.6
  14.4 31.7 %hamiltonian.1 = f32[4,110592]{1,0:T(4,128)S(1)} custom-call(f32[16]{0:T(128)S(1)} %copy-done.7, f32[29]{0:T(128)S(1)} %copy-done.8, f32[4,110592]{1,0:T(4,128)S(1)} %copy-done.4, f32[48,2304]{1,0:T(8,128)S(1)} %copy-done.6), custom_call_target="tpu_custom_call" | custom-call | flops 24000000000 | bytes 5308416 | tf_op jit(solution)/shard_map/hamiltonian/pallas_call | solution.py:180
  46.1 0.0 copy-start.5
  46.1 1.2 copy-done.5
  47.3 6.9 %all-to-all-done.refs_0_.refs_1_ = f32[32,4,3456]{2,1,0:T(4,128)S(1)} async-done(((f32[32,4,3456]{2,1,0:T(4,128)}), f32[32,4,3456]{2,1,0:T(4,128)S(1)}, u32[]{:S(2)}, u32[]{:S(2)}) %all-to-all-start) | async-done | bytes 1769504 | tf_op jit(solution)/shard_map/all_to_all | solution.py:208
  54.2 6.0 %all-to-all-start.1 = ((f32[32,4,3456]{2,1,0:T(4,128)}), f32[32,4,3456]{2,1,0:T(4,128)S(1)}, u32[]{:S(2)}, u32[]{:S(2)}) async-start(f32[32,4,3456]{2,1,0:T(4,128)} %bitcast.14), calls=%async_computation.1 | async-start | bytes 3538944 | tf_op jit(solution)/shard_map/all_to_all | solution.py:208
  60.2 1.6 collective-permute-start
  61.8 1.7 collective-permute-start.1
  63.5 39.4 %all-to-all-done.1.refs_3_.refs_2_.refs_6_ = f32[32,4,3456]{2,1,0:T(4,128)S(1)} async-done(((f32[32,4,3456]{2,1,0:T(4,128)}), f32[32,4,3456]{2,1,0:T(4,128)S(1)}, u32[]{:S(2)}, u32[]{:S(2)}) %all-to-all-start.1) | async-done | bytes 1769504 | tf_op jit(solution)/shard_map/all_to_all | solution.py:208
  103.0 0.0 collective-permute-start.2
  103.0 0.0 collective-permute-done.refs_1_.refs_2_
  103.0 1.2 slice.8
  104.2 1.6 collective-permute-start.3
  105.8 0.0 collective-permute-done.1.refs_2_.refs_3_
  105.8 1.2 slice.9
  107.0 1.8 collective-permute-start.4
  108.8 0.0 collective-permute-done.2.refs_4_.refs_3_
  108.8 8.3 %margin_part.2 = f32[384,256]{1,0:T(8,128)S(1)} custom-call(f32[32,4,3456]{2,1,0:T(4,128)S(1)} %all-to-all-done.refs_0_.refs_1_, f32[32,4,3456]{2,1,0:T(4,128)} %collective-permute-done.refs_1_.refs_2_, f32[32,4,3456]{2,1,0:T(4,128)} %collective-permute-done.1.refs_2_.refs_3_, f32[32,4,3456]{2,1,0:T(4,128)S(1)} %all-to-all-done.1.refs_3_.refs_2_.refs_6_, ...), custom_call_target="tpu_custom_call" | custom-call | flops 2038431744 | bytes 8847360 | tf_op jit(solution)/shard_map/margin_part/pallas_call | solution.py:262
  117.1 10.4 %collective-permute-done.3.refs_0_.refs_4_ = f32[16,4,3456]{2,1,0:T(4,128)S(1)} collective-permute-done((f32[16,4,3456]{2,1,0:T(4,128)S(1)}, f32[16,4,3456]{2,1,0:T(4,128)S(1)}, u32[]{:S(2)}, u32[]{:S(2)}) %collective-permute-start.3) | collective-permute-done | bytes 884768 | tf_op jit(solution)/shard_map/ppermute | solution.py:212
  127.5 0.0 copy-start
  127.5 1.3 collective-permute-done.4.refs_1_.refs_5_
  128.9 4.3 %margin_part.3 = f32[128,256]{1,0:T(8,128)S(1)} custom-call(f32[16,4,3456]{2,1,0:T(4,128)S(1)} %collective-permute-done.3.refs_0_.refs_4_, f32[16,4,3456]{2,1,0:T(4,128)S(1)} %collective-permute-done.4.refs_1_.refs_5_, f32[32,4,3456]{2,1,0:T(4,128)S(1)} %all-to-all-done.1.refs_3_.refs_2_.refs_6_, f32[32,4,3456]{2,1,0:T(4,128)S(1)} %collective-permute-done.2.refs_4_.refs_3_), custom_call_target="tpu_custom_call" | custom-call | flops 679477248 | bytes 5308416 | tf_op jit(solution)/shard_map/margin_part/pallas_call | solution.py:262
  133.1 0.0 copy-done
  133.1 0.0 copy-done.2
  133.2 22.5 %all_to_all.25 = f32[32,16,256]{2,1,0:T(8,128)} all-to-all(f32[32,16,256]{2,1,0:T(8,128)S(1)} %bitcast.16), channel_id=1, replica_groups=mesh['x'=4,'zl'=2,'y'=4,'core'=2,'zh'=4] {'y','zl','zh'}, dimensions={0} | all-to-all | bytes 1048576 | tf_op jit(solution)/shard_map/all_to_all | solution.py:342
  155.7 1.1 reduce_sum.9
  156.7 0.1 broadcast_in_dim.2
  156.8 21.6 %all_to_all.26 = f32[32,16,256]{2,1,0:T(8,128)S(1)} all-to-all(f32[32,16,256]{2,1,0:T(8,128)S(1)} %broadcast_in_dim.2), channel_id=1, replica_groups=mesh['x'=4,'zl'=2,'y'=4,'core'=2,'zh'=4] {'y','zl','zh'}, dimensions={0} | all-to-all | bytes 1048576 | tf_op jit(solution)/shard_map/all_to_all | solution.py:346
  178.4 0.0 copy-done.1
  178.4 1.2 copy-done.3
  179.6 8.0 %rotated.3 = f32[32,4,3456]{2,1,0:T(4,128)S(1)} custom-call(f32[512,256]{1,0:T(8,128)S(1)} %bitcast.11, f32[32,4,3456]{2,1,0:T(4,128)S(1)} %all-to-all-done.refs_0_.refs_1_, f32[32,4,3456]{2,1,0:T(4,128)} %collective-permute-done.refs_1_.refs_2_, f32[32,4,3456]{2,1,0:T(4,128)} %collective-permute-done.1.refs_2_.refs_3_, f32[16,4,3456]{2,1,0:T(4,128)S(1)} %copy-done.1, ...), custom_call_target="tpu_custom_call" | custom-call | flops 1358954496 | bytes 10616832 | tf_op jit(solution)/shard_map/rotated/pallas_call | solution.py:309
  187.5 0.1 collective-permute-start.5
  187.6 8.0 %rotated.2 = f32[32,4,3456]{2,1,0:T(4,128)S(1)} custom-call(f32[512,256]{1,0:T(8,128)S(1)} %bitcast.12, f32[32,4,3456]{2,1,0:T(4,128)S(1)} %all-to-all-done.refs_0_.refs_1_, f32[32,4,3456]{2,1,0:T(4,128)} %collective-permute-done.refs_1_.refs_2_, f32[32,4,3456]{2,1,0:T(4,128)} %collective-permute-done.1.refs_2_.refs_3_, f32[16,4,3456]{2,1,0:T(4,128)S(1)} %copy-done.1, ...), custom_call_target="tpu_custom_call" | custom-call | flops 1358954496 | bytes 10616832 | tf_op jit(solution)/shard_map/rotated/pallas_call | solution.py:309
  195.7 0.0 collective-permute-done.5
  195.7 0.5 sub.3
  196.1 49.6 %all_to_all.27 = f32[32,4,3456]{2,1,0:T(4,128)S(1)} all-to-all(f32[32,4,3456]{2,1,0:T(4,128)S(1)} %sub.3), channel_id=1, replica_groups=mesh['x'=4,'zl'=2,'y'=4,'core'=2,'zh'=4] {'y','zl','zh'}, dimensions={0} | all-to-all | bytes 3538944 | tf_op jit(solution)/shard_map/all_to_all | solution.py:352
  245.7 1.2 copy.6
  (4 shorter events, 0.0 us)
Async XLA Ops:
  0.0 11.1 %copy-start.9 = (f32[110592]{0:T(1024)S(1)}, f32[110592]{0:T(1024)}, u32[]{:S(2)}) copy-start(f32[110592]{0:T(1024)} %param.5) | copy-start | bytes 1327108
  0.0 11.9 %copy-start.7 = (f32[16]{0:T(128)S(1)}, f32[16]{0:T(128)}, u32[]{:S(2)}) copy-start(f32[16]{0:T(128)} %magic_ref.1) | copy-start | bytes 196
  0.0 11.9 %copy-start.8 = (f32[29]{0:T(128)S(1)}, f32[29]{0:T(128)}, u32[]{:S(2)}) copy-start(f32[29]{0:T(128)} %kinetic_ref.1) | copy-start | bytes 352
  0.0 54.2 %all-to-all-start = ((f32[32,4,3456]{2,1,0:T(4,128)}), f32[32,4,3456]{2,1,0:T(4,128)S(1)}, u32[]{:S(2)}, u32[]{:S(2)}) async-start(f32[32,4,3456]{2,1,0:T(4,128)} %bitcast.13), calls=%async_computation | async-start | bytes 3538944 | tf_op jit(solution)/shard_map/all_to_all | solution.py:208
  11.9 1.5 copy-start.4
  13.4 1.0 copy-start.6
  46.1 1.2 copy-start.5
  54.2 48.8 %all-to-all-start.1 = ((f32[32,4,3456]{2,1,0:T(4,128)}), f32[32,4,3456]{2,1,0:T(4,128)S(1)}, u32[]{:S(2)}, u32[]{:S(2)}) async-start(f32[32,4,3456]{2,1,0:T(4,128)} %bitcast.14), calls=%async_computation.1 | async-start | bytes 3538944 | tf_op jit(solution)/shard_map/all_to_all | solution.py:208
  60.2 42.7 %collective-permute-start = (f32[32,4,3456]{2,1,0:T(4,128)S(1)}, f32[32,4,3456]{2,1,0:T(4,128)}, u32[]{:S(2)}, u32[]{:S(2)}) collective-permute-start(f32[32,4,3456]{2,1,0:T(4,128)S(1)} %all-to-all-done.refs_0_.refs_1_), channel_id=1, source_target_pairs={{0,64},{64,128},{128,192},{192,0},{1,65},{65,129},{129,193},{193,1... | collective-permute-start | bytes 5308424 | tf_op jit(solution)/shard_map/ppermute | solution.py:212
  61.8 44.0 %collective-permute-start.1 = (f32[32,4,3456]{2,1,0:T(4,128)S(1)}, f32[32,4,3456]{2,1,0:T(4,128)}, u32[]{:S(2)}, u32[]{:S(2)}) collective-permute-start(f32[32,4,3456]{2,1,0:T(4,128)S(1)} %all-to-all-done.refs_0_.refs_1_), channel_id=1, source_target_pairs={{0,192},{64,0},{128,64},{192,128},{1,193},{65,1},{129,65},{193,129... | collective-permute-start | bytes 5308424 | tf_op jit(solution)/shard_map/ppermute | solution.py:212
  103.0 5.9 %collective-permute-start.2 = (f32[32,4,3456]{2,1,0:T(4,128)S(1)}, f32[32,4,3456]{2,1,0:T(4,128)S(1)}, u32[]{:S(2)}, u32[]{:S(2)}) collective-permute-start(f32[32,4,3456]{2,1,0:T(4,128)S(1)} %all-to-all-done.1.refs_3_.refs_2_.refs_6_), channel_id=1, source_target_pairs={{0,4},{4,0},{1,5},{5,1},{2,6},{6,2},{3,7},{7,3},{8,12},{12,8},{9,1... | collective-permute-start | bytes 5308424 | tf_op jit(solution)/shard_map/ppermute | solution.py:216
  104.2 23.3 %collective-permute-start.3 = (f32[16,4,3456]{2,1,0:T(4,128)S(1)}, f32[16,4,3456]{2,1,0:T(4,128)S(1)}, u32[]{:S(2)}, u32[]{:S(2)}) collective-permute-start(f32[16,4,3456]{2,1,0:T(4,128)S(1)} %slice.8), channel_id=1, source_target_pairs={{0,64},{64,128},{128,192},{192,0},{1,65},{65,129},{129,193},{193,1... | collective-permute-start | bytes 2654216 | tf_op jit(solution)/shard_map/ppermute | solution.py:212
  107.0 21.9 %collective-permute-start.4 = (f32[16,4,3456]{2,1,0:T(4,128)S(1)}, f32[16,4,3456]{2,1,0:T(4,128)S(1)}, u32[]{:S(2)}, u32[]{:S(2)}) collective-permute-start(f32[16,4,3456]{2,1,0:T(4,128)S(1)} %slice.9), channel_id=1, source_target_pairs={{0,192},{64,0},{128,64},{192,128},{1,193},{65,1},{129,65},{193,129... | collective-permute-start | bytes 2654216 | tf_op jit(solution)/shard_map/ppermute | solution.py:212
  127.5 5.6 %copy-start = (f32[16,4,3456]{2,1,0:T(4,128)}, f32[16,4,3456]{2,1,0:T(4,128)S(1)}, u32[]{:S(2)}) copy-start(f32[16,4,3456]{2,1,0:T(4,128)S(1)} %collective-permute-done.3.refs_0_.refs_4_) | copy-start | bytes 2654212
  128.9 4.3 %copy-start.2 = (f32[16,4,3456]{2,1,0:T(4,128)}, f32[16,4,3456]{2,1,0:T(4,128)S(1)}, u32[]{:S(2)}) copy-start(f32[16,4,3456]{2,1,0:T(4,128)S(1)} %collective-permute-done.4.refs_1_.refs_5_) | copy-start | bytes 2654212
  156.7 21.6 %copy-start.1 = (f32[16,4,3456]{2,1,0:T(4,128)S(1)}, f32[16,4,3456]{2,1,0:T(4,128)}, u32[]{:S(2)}) copy-start(f32[16,4,3456]{2,1,0:T(4,128)} %copy-done) | copy-start | bytes 2654212
  178.4 1.2 copy-start.3
  187.5 8.1 %collective-permute-start.5 = (f32[32,4,3456]{2,1,0:T(4,128)S(1)}, f32[32,4,3456]{2,1,0:T(4,128)S(1)}, u32[]{:S(2)}, u32[]{:S(2)}) collective-permute-start(f32[32,4,3456]{2,1,0:T(4,128)S(1)} %rotated.3), channel_id=1, source_target_pairs={{0,4},{4,0},{1,5},{5,1},{2,6},{6,2},{3,7},{7,3},{8,12},{12,8},{9,1... | collective-permute-start | bytes 5308424 | tf_op jit(solution)/shard_map/ppermute | solution.py:216

commit v4 on v2

--- a/solution.py
+++ b/solution.py
@@ -11,7 +11,8 @@
 NAMES = ("x", "zl", "y", "core", "zh")
 COEF = ("y", "zl", "zh")
 NSPLIT = 32
-HIGH = lax.Precision.HIGH
+CHUNK = 1152
+WIDE = 1152
 PLANE = G * G
 BLK = 16 * G
 F32 = jnp.float32
@@ -193,7 +194,7 @@
             pltpu.VMEM((rows, 2 * PLANE), BF16),
             pltpu.VMEM((2 * rows, rows), BF16),
         ],
-        compiler_params=pltpu.CompilerParams(vmem_limit_bytes=48 * 1024 * 1024),
+        compiler_params=pltpu.CompilerParams(vmem_limit_bytes=36 * 1024 * 1024),
         cost_estimate=pl.CostEstimate(
             flops=24_000_000_000, transcendentals=0, bytes_accessed=12 * orbitals.size
         ),
@@ -201,13 +202,17 @@
     )(magic_taps, kinetic_taps, orbitals, potential.reshape(G, PLANE))
 
 
+def exchange(pieces):
+    return lax.all_to_all(pieces, COEF, split_axis=0, concat_axis=0, tiled=True)
+
+
 def to_cols(block):
     pieces = block.reshape(block.shape[0], NSPLIT, -1).transpose(1, 0, 2)
-    return lax.all_to_all(pieces, COEF, split_axis=0, concat_axis=0, tiled=True)
-
-
-def flat(pieces):
-    return pieces.reshape(-1, pieces.shape[-1])
+    return exchange(pieces)
+
+
+def sum_over_cols(part):
+    return jnp.sum(exchange(part.reshape(NSPLIT, -1, part.shape[1])), axis=0)
 
 
 def step_x(pieces, step):
@@ -216,38 +221,137 @@
 
 def swap_core(value):
     return lax.ppermute(value, "core", [(0, 1), (1, 0)])
+
+
+def rows_of(ref, scratch, start):
+    count = ref.shape[0]
+    for s in range(count):
+        scratch[start + 4 * s:start + 4 * s + 4, :] = ref[s]
+
+
+NT = (((1,), (1,)), ((), ()))
+
+
+def margin_kernel(*refs):
+    panels, (own_ref, swap_ref, out_ref, high_ref, low_ref, psi, hps, hsp) = refs[:-8], refs[-8:]
+    rows_of(own_ref, hps, 0)
+    rows_of(swap_ref, hps, hps.shape[0] // 2)
+    at = 0
+    for ref in panels:
+        rows_of(ref, psi, at)
+        at += 4 * ref.shape[0]
+    cols = hps.shape[0]
+    high, low = split_bf16(hps[...])
+    hsp[0:cols, :] = high
+    hsp[cols:, :] = low
+    p_hi, p_lo = split_bf16(psi[...])
+    high_ref[...] = p_hi
+    low_ref[...] = p_lo
+    both = lax.dot_general(hsp[...], p_hi, NT, preferred_element_type=F32)
+    cross = lax.dot_general(hsp[0:cols, :], p_lo, NT, preferred_element_type=F32)
+    total = (both[0:cols] + both[cols:] + cross) * (1.0 / NC)
+
+    @pl.when(pl.program_id(0) == 0)
+    def _():
+        out_ref[...] = total
+
+    @pl.when(pl.program_id(0) > 0)
+    def _():
+        out_ref[...] += total
+
+
+def chunk_spec(array, chunk):
+    return pl.BlockSpec((*array.shape[:-1], chunk), lambda k: (0,) * (len(array.shape) - 1) + (k,))
+
+
+def margin_part(panels, own, swap):
+    rows = sum(4 * v.shape[0] for v in panels)
+    cols = 8 * own.shape[0]
+    width = own.shape[2]
+    arrays = [*panels, own, swap]
+    half = jax.ShapeDtypeStruct((rows, width), BF16)
+    return pl.pallas_call(
+        margin_kernel,
+        grid=(width // CHUNK,),
+        out_shape=[jax.ShapeDtypeStruct((cols, rows), F32), half, half],
+        in_specs=[chunk_spec(v, CHUNK) for v in arrays],
+        out_specs=[pl.BlockSpec((cols, rows), lambda k: (0, 0))] + [chunk_spec(half, CHUNK)] * 2,
+        scratch_shapes=[
+            pltpu.VMEM((rows, CHUNK), F32),
+            pltpu.VMEM((cols, CHUNK), F32),
+            pltpu.VMEM((2 * cols, CHUNK), BF16),
+        ],
+        cost_estimate=pl.CostEstimate(
+            flops=6 * rows * cols * width, transcendentals=0,
+            bytes_accessed=4 * (2 * rows + cols) * width,
+        ),
+        compiler_params=pltpu.CompilerParams(vmem_limit_bytes=24 * 1024 * 1024),
+        name="margin_part",
+    )(*arrays)
+
+
+def rotate_kernel(margin_ref, *refs):
+    halves, (base_ref, mine_ref, other_ref, turn, res) = refs[:-5], refs[-5:]
+    cols = margin_ref.shape[0]
+
+    @pl.when(pl.program_id(0) == 0)
+    def _():
+        high, low = split_bf16(margin_ref[...])
+        turn[0:cols, :] = high
+        turn[cols:, :] = low
+
+    at = 0
+    total = None
+    for high_ref, low_ref in zip(halves[::2], halves[1::2]):
+        upto = at + high_ref.shape[0]
+        both = jnp.dot(turn[:, at:upto], high_ref[...], preferred_element_type=F32)
+        low = jnp.dot(turn[0:cols, at:upto], low_ref[...], preferred_element_type=F32)
+        value = both[0:cols] + both[cols:] + low
+        total = value if total is None else total + value
+        at = upto
+    res[...] = total
+    for s in range(mine_ref.shape[0]):
+        mine_ref[s] = base_ref[s] - res[4 * s:4 * s + 4, :]
+        other_ref[s] = res[cols // 2 + 4 * s:cols // 2 + 4 * s + 4, :]
+
+
+def rotated(margin, halves, base):
+    cols, rows = margin.shape
+    width = base.shape[2]
+    shape = jax.ShapeDtypeStruct(base.shape, F32)
+    return pl.pallas_call(
+        rotate_kernel,
+        grid=(width // WIDE,),
+        out_shape=[shape, shape],
+        in_specs=[pl.BlockSpec(margin.shape, lambda k: (0, 0))]
+        + [chunk_spec(v, WIDE) for v in (*halves, base)],
+        out_specs=[chunk_spec(base, WIDE)] * 2,
+        scratch_shapes=[pltpu.VMEM((2 * cols, rows), BF16), pltpu.VMEM((cols, WIDE), F32)],
+        cost_estimate=pl.CostEstimate(
+            flops=6 * rows * cols * width, transcendentals=0,
+            bytes_accessed=4 * (rows + 2 * cols) * width,
+        ),
+        compiler_params=pltpu.CompilerParams(vmem_limit_bytes=24 * 1024 * 1024),
+        name="rotated",
+    )(margin, *halves, base)
 
 
 def shards(orbitals, potential, magic_taps, kinetic_taps):
     own = to_cols(orbitals)
     hpsi = hamiltonian(orbitals, potential, magic_taps, kinetic_taps)
-    own, hpsi = lax.optimization_barrier((own, hpsi))
+    own, _ = lax.optimization_barrier((own, hpsi))
     left, right = step_x(own, 1), step_x(own, -1)
     hpsi_cols = to_cols(hpsi)
     half = NSPLIT // 2
     far_a, far_b = step_x(left[:half], 1), step_x(right[half:], -1)
     hpsi_swap = swap_core(hpsi_cols)
-    both = jnp.concatenate([flat(hpsi_cols), flat(hpsi_swap)], axis=0)
-    panels = [flat(v) for v in (own, left, right, far_a, far_b)]
-    part = jnp.concatenate(
-        [jnp.einsum("jc,ic->ji", psi, both, precision=HIGH) for psi in panels], axis=0
-    ) * (1.0 / NC)
-    rows = part.shape[0] // NSPLIT
-    terms = lax.all_to_all(
-        part.reshape(NSPLIT, rows, -1), COEF, split_axis=0, concat_axis=0, tiled=True
-    )
-    mine = jnp.sum(terms, axis=0)
-    margin = lax.all_to_all(
-        jnp.broadcast_to(mine[None], terms.shape), COEF, split_axis=0, concat_axis=0, tiled=True
-    ).reshape(part.shape)
-    stack = jnp.concatenate(panels, axis=0)
-    cols = margin.shape[1] // 2
-    other = jnp.einsum("ji,jc->ic", margin[:, cols:], stack, precision=HIGH)
-    from_other = swap_core(other)
-    grad_cols = flat(hpsi_cols) - jnp.einsum("ji,jc->ic", margin[:, :cols], stack, precision=HIGH) - from_other
-    back = lax.all_to_all(
-        grad_cols.reshape(hpsi_cols.shape), COEF, split_axis=0, concat_axis=0, tiled=True
-    )
+    near, *near_halves = margin_part([own, left, right], hpsi_cols, hpsi_swap)
+    far, *far_halves = margin_part([far_a, far_b], hpsi_cols, hpsi_swap)
+    mine = jnp.concatenate([sum_over_cols(near), sum_over_cols(far)], axis=1)
+    margin = exchange(jnp.broadcast_to(mine[None], (NSPLIT, *mine.shape))).reshape(-1, mine.shape[1])
+    grad_mine, grad_other = rotated(margin, near_halves + far_halves, hpsi_cols)
+    grad_cols = grad_mine - swap_core(grad_other)
+    back = exchange(grad_cols)
     return back.transpose(1, 0, 2).reshape(orbitals.shape)
 
 

time: 264 us -> 243 us (0.920)
  waiting for transfers between devices: 93.3 us -> 64.4 us
  blocking collectives: 49.3 us -> 69.5 us
  matrix products: 19 us -> 0 us
  Pallas kernels: 32.9 us -> 49.9 us
  local copies, waits for them, and re-layouts: 33 us -> 19 us
  starting transfers between devices: 34 us -> 36.7 us
    all_to_all x1 -> x2, blocking collectives: 49.3 us -> 69.5 us  [exchange(): return lax.all_to_all(pieces, COEF, split_axis=0, concat_axis=0, tiled=True)]
    dot_general x7 -> x0, matrix products: 19 us -> none  [the longest x5 8.2 us: shards(): jnp.einsum('jc,ic->ji', psi, both, precision=HIGH)]
    pallas_call x0 -> x3, Pallas kernels: none -> 18.2 us  [the longest x2 11.9 us: margin_part(): pl.pallas_call(margin_kernel, grid=(width // CHUNK,), out_shape=[jax.Shap...]
    reshape x8 -> x0, local copies, waits for them, and re-layouts: 17.7 us -> none  [the longest x7 17.2 us: flat(): return pieces.reshape(-1, pieces.shape[-1])]
    all_to_all x4, waiting for transfers between devices: 75.3 us -> 59.2 us  [exchange(): return lax.all_to_all(pieces, COEF, split_axis=0, concat_axis=0, tiled=True)]
    ppermute x4, waiting for transfers between devices: 14.3 us -> 1.57 us  [step_x(): return lax.ppermute(pieces, 'x', [(i, (i + step) % 4) for i in range(4)])]
    unnamed x34 -> x27, local copies, waits for them, and re-layouts: 9.63 us -> 13.7 us
    concatenate x2 -> x0, local copies, waits for them, and re-layouts: 2.72 us -> none  [the longest x1 1.72 us: shards(): both = jnp.concatenate([flat(hpsi_cols), flat(hpsi_swap)], axis=0)]
  transfers between devices with their start and end apart: 10 -> 10, of which waited for: 7 -> 6; matrix products, arithmetic and copies ran while one was open for 10% -> 3% of each run, Pallas kernels for 12% -> 18%
where the time goes in v4:
time: 243 us; the launch traced here: 242 us
  blocking collectives  69.5 us (29%)
  waiting for transfers between devices  64.4 us (27%)
  Pallas kernels  49.9 us (21%)
  starting transfers between devices  36.7 us (15%)
  local copies, waits for them, and re-layouts  19 us (8%)
  other arithmetic  2.44 us (1%)
    all_to_all x2, blocking collectives, exchange(): return lax.all_to_all(pieces, COEF, split_axis=0, concat_axis=0, tiled=True)  69.5 us
    all_to_all x4, waiting for transfers between devices, exchange(): return lax.all_to_all(pieces, COEF, split_axis=0, concat_axis=0, tiled=True)  59.2 us
    pallas_call x1, Pallas kernels, hamiltonian(): pl.pallas_call(h_kernel, out_shape=jax.ShapeDtypeStruct(orbitals.shape, F...  31.7 us
    all_to_all x4, starting transfers between devices, exchange(): return lax.all_to_all(pieces, COEF, split_axis=0, concat_axis=0, tiled=True)  30 us
    unnamed x27, local copies, waits for them, and re-layouts  13.7 us
    pallas_call x2, Pallas kernels, margin_part(): pl.pallas_call(margin_kernel, grid=(width // CHUNK,), out_shape=[jax.Shap...  11.9 us
    ppermute x4, starting transfers between devices, step_x(): return lax.ppermute(pieces, 'x', [(i, (i + step) % 4) for i in range(4)])  6.55 us
    pallas_call x1, Pallas kernels, rotated(): pl.pallas_call(rotate_kernel, grid=(width // WIDE,), out_shape=[shape, sh...  6.27 us
  transfers between devices with their start and end apart: 10, of which 6 were waited for; matrix products, arithmetic and copies ran while one was open for 3% of the time, Pallas kernels for 18%

profile of v4, /device:TPU:64, one launch (start us, length us, event | category | flops | bytes accessed | tf_op | source)
XLA Modules:
  0.0 242.0 jit_solution(16720555985882170511)
XLA Ops:
  0.0 11.0 %all-to-all-start = ((f32[32,4,3456]{2,1,0:T(4,128)}), f32[32,4,3456]{2,1,0:T(4,128)S(1)}, u32[]{:S(2)}, u32[]{:S(2)}) async-start(f32[32,4,3456]{2,1,0:T(4,128)} %bitcast.12), calls=%async_computation | async-start | bytes 3538944 | tf_op jit(solution)/shard_map/all_to_all | solution.py:206
  11.1 0.0 copy-done.12
  11.1 0.8 reshape.23.pot_ref
  11.9 0.0 copy-done.10
  11.9 0.0 copy-done.11
  11.9 1.5 copy-done.2
  13.4 1.0 copy-done.4
  14.4 31.7 %hamiltonian.1 = f32[4,110592]{1,0:T(4,128)S(1)} custom-call(f32[16]{0:T(128)S(1)} %copy-done.10, f32[29]{0:T(128)S(1)} %copy-done.11, f32[4,110592]{1,0:T(4,128)S(1)} %copy-done.2, f32[48,2304]{1,0:T(8,128)S(1)} %copy-done.4), custom_call_target="tpu_custom_call" | custom-call | flops 24000000000 | bytes 5308416 | tf_op jit(solution)/shard_map/hamiltonian/pallas_call | solution.py:179
  46.1 0.0 copy-start.3
  46.1 1.2 copy-done.3
  47.3 6.9 %all-to-all-done.refs_0_ = f32[32,4,3456]{2,1,0:T(4,128)S(1)} async-done(((f32[32,4,3456]{2,1,0:T(4,128)}), f32[32,4,3456]{2,1,0:T(4,128)S(1)}, u32[]{:S(2)}, u32[]{:S(2)}) %all-to-all-start) | async-done | bytes 1769504 | tf_op jit(solution)/shard_map/all_to_all | solution.py:206
  54.2 6.0 %all-to-all-start.1 = ((f32[32,4,3456]{2,1,0:T(4,128)}), f32[32,4,3456]{2,1,0:T(4,128)S(1)}, u32[]{:S(2)}, u32[]{:S(2)}) async-start(f32[32,4,3456]{2,1,0:T(4,128)} %bitcast.13), calls=%async_computation.1 | async-start | bytes 3538944 | tf_op jit(solution)/shard_map/all_to_all | solution.py:206
  60.2 1.6 collective-permute-start
  61.8 1.7 collective-permute-start.1
  63.5 39.4 %all-to-all-done.1.refs_3_.refs_2_.refs_4_ = f32[32,4,3456]{2,1,0:T(4,128)S(1)} async-done(((f32[32,4,3456]{2,1,0:T(4,128)}), f32[32,4,3456]{2,1,0:T(4,128)S(1)}, u32[]{:S(2)}, u32[]{:S(2)}) %all-to-all-start.1) | async-done | bytes 1769504 | tf_op jit(solution)/shard_map/all_to_all | solution.py:206
  103.0 0.0 collective-permute-start.2
  103.0 0.0 collective-permute-done.refs_1_
  103.0 2.2 slice.8
  105.1 1.5 collective-permute-start.3
  106.6 0.0 collective-permute-done.1.refs_2_
  106.6 2.2 slice.9
  108.8 1.7 collective-permute-start.4
  110.6 0.0 collective-permute-done.2.refs_4_.refs_3_
  110.6 7.3 %margin_part.2 = (f32[256,384]{1,0:T(8,128)S(1)}, bf16[384,3456]{1,0:T(8,128)(2,1)S(1)}, bf16[384,3456]{1,0:T(8,128)(2,1)S(1)}) custom-call(f32[32,4,3456]{2,1,0:T(4,128)S(1)} %all-to-all-done.refs_0_, f32[32,4,3456]{2,1,0:T(4,128)} %collective-permute-done.refs_1_, f32[32,4,3456]{2,1,0:T(4,128)} %collective-permute-done.1.refs_2_, ...), custom_call_target="tpu_custom_call" | custom-call | flops 2038431744 | bytes 14155776 | tf_op jit(solution)/shard_map/margin_part/pallas_call | solution.py:273
  117.9 0.0 copy-done
  117.9 0.8 copy-done.5
  118.6 1.5 copy-done.6
  120.2 1.6 copy-done.8
  121.7 7.6 %all-to-all-start.2 = ((f32[32,8,384]{2,1,0:T(8,128)}), f32[32,8,384]{2,1,0:T(8,128)}, u32[]{:S(2)}, u32[]{:S(2)}) async-start(f32[32,8,384]{2,1,0:T(8,128)} %bitcast.15), calls=%async_computation.2 | async-start | bytes 786432 | tf_op jit(solution)/shard_map/all_to_all | solution.py:206
  129.4 0.0 collective-permute-done.3.refs_0_
  129.4 1.6 collective-permute-done.4.refs_1_
  130.9 1.5 copy-done.1
  132.4 4.6 %margin_part.3 = (f32[256,128]{1,0:T(8,128)}, bf16[128,3456]{1,0:T(8,128)(2,1)S(1)}, bf16[128,3456]{1,0:T(8,128)(2,1)S(1)}) custom-call(f32[16,4,3456]{2,1,0:T(4,128)} %collective-permute-done.3.refs_0_, f32[16,4,3456]{2,1,0:T(4,128)} %collective-permute-done.4.refs_1_, f32[32,4,3456]{2,1,0:T(4,128)S(1)} %all-to-all-done.1.refs_3_.refs_2_.refs_4_, ...), custom_call_target="tpu_custom_call" | custom-call | flops 679477248 | bytes 7077888 | tf_op jit(solution)/shard_map/margin_part/pallas_call | solution.py:273
  137.1 5.1 %all-to-all-done.2 = f32[32,8,384]{2,1,0:T(8,128)} async-done(((f32[32,8,384]{2,1,0:T(8,128)}), f32[32,8,384]{2,1,0:T(8,128)}, u32[]{:S(2)}, u32[]{:S(2)}) %all-to-all-start.2) | async-done | bytes 393248 | tf_op jit(solution)/shard_map/all_to_all | solution.py:206
  142.1 5.3 %all-to-all-start.3 = ((f32[32,8,128]{2,1,0:T(8,128)}), f32[32,8,128]{2,1,0:T(8,128)}, u32[]{:S(2)}, u32[]{:S(2)}) async-start(f32[32,8,128]{2,1,0:T(8,128)} %bitcast.5), calls=%async_computation.3 | async-start | bytes 262144 | tf_op jit(solution)/shard_map/all_to_all | solution.py:206
  147.4 1.0 reduce_sum.18
  148.5 7.8 %all-to-all-done.3 = f32[32,8,128]{2,1,0:T(8,128)} async-done(((f32[32,8,128]{2,1,0:T(8,128)}), f32[32,8,128]{2,1,0:T(8,128)}, u32[]{:S(2)}, u32[]{:S(2)}) %all-to-all-start.3) | async-done | bytes 131104 | tf_op jit(solution)/shard_map/all_to_all | solution.py:206
  156.3 0.9 reduce_sum.19
  157.2 0.1 broadcast_in_dim.2
  157.3 20.2 %all_to_all.30 = f32[32,8,512]{2,1,0:T(8,128)S(1)} all-to-all(f32[32,8,512]{2,1,0:T(8,128)S(1)} %broadcast_in_dim.2), channel_id=1, replica_groups=mesh['x'=4,'zl'=2,'y'=4,'core'=2,'zh'=4] {'y','zl','zh'}, dimensions={0} | all-to-all | bytes 1048576 | tf_op jit(solution)/shard_map/all_to_all | solution.py:206
  177.5 1.7 copy-done.7
  179.3 1.7 copy-done.9
  181.0 6.3 %rotated.1 = (f32[32,4,3456]{2,1,0:T(4,128)S(1)}, f32[32,4,3456]{2,1,0:T(4,128)S(1)}) custom-call(f32[256,512]{1,0:T(8,128)S(1)} %bitcast.14, bf16[384,3456]{1,0:T(8,128)(2,1)S(1)} %copy-done.7, bf16[384,3456]{1,0:T(8,128)(2,1)S(1)} %copy-done.9, bf16[128,3456]{1,0:T(8,128)(2,1)S(1)} %get-tuple-element.19.refs_2_, ...), custom_call_target="tpu_custom_call" | custom-call | flops 2717908992 | bytes 14155776 | tf_op jit(solution)/shard_map/rotated/pallas_call | solution.py:322
  187.3 0.1 collective-permute-start.5
  187.4 3.7 %collective-permute-done.5 = f32[32,4,3456]{2,1,0:T(4,128)S(1)} collective-permute-done((f32[32,4,3456]{2,1,0:T(4,128)S(1)}, f32[32,4,3456]{2,1,0:T(4,128)S(1)}, u32[]{:S(2)}, u32[]{:S(2)}) %collective-permute-start.5) | collective-permute-done | bytes 1769504 | tf_op jit(solution)/shard_map/ppermute | solution.py:223
  191.1 0.5 sub.3
  191.6 49.2 %all_to_all.31 = f32[32,4,3456]{2,1,0:T(4,128)S(1)} all-to-all(f32[32,4,3456]{2,1,0:T(4,128)S(1)} %sub.3), channel_id=1, replica_groups=mesh['x'=4,'zl'=2,'y'=4,'core'=2,'zh'=4] {'y','zl','zh'}, dimensions={0} | all-to-all | bytes 3538944 | tf_op jit(solution)/shard_map/all_to_all | solution.py:206
  240.8 1.2 copy.6
  (13 shorter events, 0.0 us)
Async XLA Ops:
  0.0 11.1 %copy-start.12 = (f32[110592]{0:T(1024)S(1)}, f32[110592]{0:T(1024)}, u32[]{:S(2)}) copy-start(f32[110592]{0:T(1024)} %param.5) | copy-start | bytes 1327108
  0.0 11.9 %copy-start.10 = (f32[16]{0:T(128)S(1)}, f32[16]{0:T(128)}, u32[]{:S(2)}) copy-start(f32[16]{0:T(128)} %magic_ref.1) | copy-start | bytes 196
  0.0 11.9 %copy-start.11 = (f32[29]{0:T(128)S(1)}, f32[29]{0:T(128)}, u32[]{:S(2)}) copy-start(f32[29]{0:T(128)} %kinetic_ref.1) | copy-start | bytes 352
  0.0 54.2 %all-to-all-start = ((f32[32,4,3456]{2,1,0:T(4,128)}), f32[32,4,3456]{2,1,0:T(4,128)S(1)}, u32[]{:S(2)}, u32[]{:S(2)}) async-start(f32[32,4,3456]{2,1,0:T(4,128)} %bitcast.12), calls=%async_computation | async-start | bytes 3538944 | tf_op jit(solution)/shard_map/all_to_all | solution.py:206
  11.9 1.5 copy-start.2
  13.4 1.0 copy-start.4
  46.1 1.2 copy-start.3
  54.2 48.8 %all-to-all-start.1 = ((f32[32,4,3456]{2,1,0:T(4,128)}), f32[32,4,3456]{2,1,0:T(4,128)S(1)}, u32[]{:S(2)}, u32[]{:S(2)}) async-start(f32[32,4,3456]{2,1,0:T(4,128)} %bitcast.13), calls=%async_computation.1 | async-start | bytes 3538944 | tf_op jit(solution)/shard_map/all_to_all | solution.py:206
  60.2 42.7 %collective-permute-start = (f32[32,4,3456]{2,1,0:T(4,128)S(1)}, f32[32,4,3456]{2,1,0:T(4,128)}, u32[]{:S(2)}, u32[]{:S(2)}) collective-permute-start(f32[32,4,3456]{2,1,0:T(4,128)S(1)} %all-to-all-done.refs_0_), channel_id=1, source_target_pairs={{0,64},{64,128},{128,192},{192,0},{1,65},{65,129},{129,193},{193,1... | collective-permute-start | bytes 5308424 | tf_op jit(solution)/shard_map/ppermute | solution.py:219
  61.8 44.8 %collective-permute-start.1 = (f32[32,4,3456]{2,1,0:T(4,128)S(1)}, f32[32,4,3456]{2,1,0:T(4,128)}, u32[]{:S(2)}, u32[]{:S(2)}) collective-permute-start(f32[32,4,3456]{2,1,0:T(4,128)S(1)} %all-to-all-done.refs_0_), channel_id=1, source_target_pairs={{0,192},{64,0},{128,64},{192,128},{1,193},{65,1},{129,65},{193,129... | collective-permute-start | bytes 5308424 | tf_op jit(solution)/shard_map/ppermute | solution.py:219
  103.0 7.6 %collective-permute-start.2 = (f32[32,4,3456]{2,1,0:T(4,128)S(1)}, f32[32,4,3456]{2,1,0:T(4,128)S(1)}, u32[]{:S(2)}, u32[]{:S(2)}) collective-permute-start(f32[32,4,3456]{2,1,0:T(4,128)S(1)} %all-to-all-done.1.refs_3_.refs_2_.refs_4_), channel_id=1, source_target_pairs={{0,4},{4,0},{1,5},{5,1},{2,6},{6,2},{3,7},{7,3},{8,12},{12,8},{9,1... | collective-permute-start | bytes 5308424 | tf_op jit(solution)/shard_map/ppermute | solution.py:223
  105.1 24.2 %collective-permute-start.3 = (f32[16,4,3456]{2,1,0:T(4,128)}, f32[16,4,3456]{2,1,0:T(4,128)}, u32[]{:S(2)}, u32[]{:S(2)}) collective-permute-start(f32[16,4,3456]{2,1,0:T(4,128)} %slice.8), channel_id=1, source_target_pairs={{0,64},{64,128},{128,192},{192,0},{1,65},{65,129},{129,193},{193,1... | collective-permute-start | bytes 2654216 | tf_op jit(solution)/shard_map/ppermute | solution.py:219
  108.8 22.1 %collective-permute-start.4 = (f32[16,4,3456]{2,1,0:T(4,128)}, f32[16,4,3456]{2,1,0:T(4,128)}, u32[]{:S(2)}, u32[]{:S(2)}) collective-permute-start(f32[16,4,3456]{2,1,0:T(4,128)} %slice.9), channel_id=1, source_target_pairs={{0,192},{64,0},{128,64},{192,128},{1,193},{65,1},{129,65},{193,129... | collective-permute-start | bytes 2654216 | tf_op jit(solution)/shard_map/ppermute | solution.py:219
  110.6 7.3 %copy-start = (f32[32,4,3456]{2,1,0:T(4,128)}, f32[32,4,3456]{2,1,0:T(4,128)S(1)}, u32[]{:S(2)}) copy-start(f32[32,4,3456]{2,1,0:T(4,128)S(1)} %collective-permute-done.2.refs_4_.refs_3_) | copy-start | bytes 5308420
  117.9 0.8 copy-start.5
  118.6 1.5 copy-start.6
  120.2 1.6 copy-start.8
  121.7 20.4 %all-to-all-start.2 = ((f32[32,8,384]{2,1,0:T(8,128)}), f32[32,8,384]{2,1,0:T(8,128)}, u32[]{:S(2)}, u32[]{:S(2)}) async-start(f32[32,8,384]{2,1,0:T(8,128)} %bitcast.15), calls=%async_computation.2 | async-start | bytes 786432 | tf_op jit(solution)/shard_map/all_to_all | solution.py:206
  130.9 1.5 copy-start.1
  142.1 14.2 %all-to-all-start.3 = ((f32[32,8,128]{2,1,0:T(8,128)}), f32[32,8,128]{2,1,0:T(8,128)}, u32[]{:S(2)}, u32[]{:S(2)}) async-start(f32[32,8,128]{2,1,0:T(8,128)} %bitcast.5), calls=%async_computation.3 | async-start | bytes 262144 | tf_op jit(solution)/shard_map/all_to_all | solution.py:206
  177.5 1.8 copy-start.7
  179.3 1.7 copy-start.9
  187.3 3.8 %collective-permute-start.5 = (f32[32,4,3456]{2,1,0:T(4,128)S(1)}, f32[32,4,3456]{2,1,0:T(4,128)S(1)}, u32[]{:S(2)}, u32[]{:S(2)}) collective-permute-start(f32[32,4,3456]{2,1,0:T(4,128)S(1)} %get-tuple-element.22), channel_id=1, source_target_pairs={{0,4},{4,0},{1,5},{5,1},{2,6},{6,2},{3,7},{7,3},{8,12},{12,8},{9,1... | collective-permute-start | bytes 5308424 | tf_op jit(solution)/shard_map/ppermute | solution.py:223

commit v5 on v4

--- a/solution.py
+++ b/solution.py
@@ -211,10 +211,6 @@
     return exchange(pieces)
 
 
-def sum_over_cols(part):
-    return jnp.sum(exchange(part.reshape(NSPLIT, -1, part.shape[1])), axis=0)
-
-
 def step_x(pieces, step):
     return lax.ppermute(pieces, "x", [(i, (i + step) % 4) for i in range(4)])
 
@@ -232,62 +228,97 @@
 NT = (((1,), (1,)), ((), ()))
 
 
-def margin_kernel(*refs):
-    panels, (own_ref, swap_ref, out_ref, high_ref, low_ref, psi, hps, hsp) = refs[:-8], refs[-8:]
-    rows_of(own_ref, hps, 0)
-    rows_of(swap_ref, hps, hps.shape[0] // 2)
+def add_up(out, place, total):
+    @pl.when(pl.program_id(0) == 0)
+    def _():
+        out[:, place] = total
+
+    @pl.when(pl.program_id(0) > 0)
+    def _():
+        out[:, place] += total
+
+
+def margin_terms(panels, psi, hsp_ref, high_ref, low_ref):
     at = 0
     for ref in panels:
         rows_of(ref, psi, at)
         at += 4 * ref.shape[0]
-    cols = hps.shape[0]
-    high, low = split_bf16(hps[...])
-    hsp[0:cols, :] = high
-    hsp[cols:, :] = low
+    cols = hsp_ref.shape[0] // 2
     p_hi, p_lo = split_bf16(psi[...])
     high_ref[...] = p_hi
     low_ref[...] = p_lo
-    both = lax.dot_general(hsp[...], p_hi, NT, preferred_element_type=F32)
-    cross = lax.dot_general(hsp[0:cols, :], p_lo, NT, preferred_element_type=F32)
-    total = (both[0:cols] + both[cols:] + cross) * (1.0 / NC)
+    both = lax.dot_general(hsp_ref[...], p_hi, NT, preferred_element_type=F32)
+    cross = lax.dot_general(hsp_ref[0:cols, :], p_lo, NT, preferred_element_type=F32)
+    return (both[0:cols] + both[cols:] + cross) * (1.0 / NC)
+
+
+def near_kernel(*refs):
+    panels, (own_ref, swap_ref, out_ref, high_ref, low_ref, hsp_ref, psi, hps) = refs[:-8], refs[-8:]
+    cols = hps.shape[0]
+    rows_of(own_ref, hps, 0)
+    rows_of(swap_ref, hps, cols // 2)
+    high, low = split_bf16(hps[...])
+    hsp_ref[0:cols, :] = high
+    hsp_ref[cols:, :] = low
+    add_up(out_ref, slice(None), margin_terms(panels, psi, hsp_ref, high_ref, low_ref))
+
+
+def far_kernel(near_ref, hsp_ref, *refs):
+    panels, (out_ref, high_ref, low_ref, psi) = refs[:-4], refs[-4:]
+    start = near_ref.shape[1]
 
     @pl.when(pl.program_id(0) == 0)
     def _():
-        out_ref[...] = total
-
-    @pl.when(pl.program_id(0) > 0)
-    def _():
-        out_ref[...] += total
+        out_ref[:, 0:start] = near_ref[...]
+
+    add_up(out_ref, slice(start, None), margin_terms(panels, psi, hsp_ref, high_ref, low_ref))
 
 
 def chunk_spec(array, chunk):
     return pl.BlockSpec((*array.shape[:-1], chunk), lambda k: (0,) * (len(array.shape) - 1) + (k,))
 
 
-def margin_part(panels, own, swap):
-    rows = sum(4 * v.shape[0] for v in panels)
-    cols = 8 * own.shape[0]
-    width = own.shape[2]
-    arrays = [*panels, own, swap]
-    half = jax.ShapeDtypeStruct((rows, width), BF16)
+def in_hbm(rows, width):
+    return pltpu.MemorySpace.HBM((rows, width), BF16)
+
+
+def margin_call(kernel, rows, cols, out_cols, extra, whole, arrays, outs, name):
+    width = arrays[-1].shape[-1]
     return pl.pallas_call(
-        margin_kernel,
+        kernel,
         grid=(width // CHUNK,),
-        out_shape=[jax.ShapeDtypeStruct((cols, rows), F32), half, half],
-        in_specs=[chunk_spec(v, CHUNK) for v in arrays],
-        out_specs=[pl.BlockSpec((cols, rows), lambda k: (0, 0))] + [chunk_spec(half, CHUNK)] * 2,
-        scratch_shapes=[
-            pltpu.VMEM((rows, CHUNK), F32),
-            pltpu.VMEM((cols, CHUNK), F32),
-            pltpu.VMEM((2 * cols, CHUNK), BF16),
-        ],
+        out_shape=[jax.ShapeDtypeStruct((cols, out_cols), F32)] + [in_hbm(r, width) for r in outs],
+        in_specs=[pl.BlockSpec(v.shape, lambda k: (0, 0)) for v in whole]
+        + [chunk_spec(v, CHUNK) for v in arrays],
+        out_specs=[pl.BlockSpec((cols, out_cols), lambda k: (0, 0))]
+        + [pl.BlockSpec((r, CHUNK), lambda k: (0, k)) for r in outs],
+        scratch_shapes=[pltpu.VMEM((rows, CHUNK), F32)] + extra,
         cost_estimate=pl.CostEstimate(
             flops=6 * rows * cols * width, transcendentals=0,
-            bytes_accessed=4 * (2 * rows + cols) * width,
+            bytes_accessed=4 * (2 * rows + 2 * cols) * width,
         ),
-        compiler_params=pltpu.CompilerParams(vmem_limit_bytes=24 * 1024 * 1024),
-        name="margin_part",
-    )(*arrays)
+        compiler_params=pltpu.CompilerParams(vmem_limit_bytes=32 * 1024 * 1024),
+        name=name,
+    )(*whole, *arrays)
+
+
+def rows_in(panels):
+    return sum(4 * v.shape[0] for v in panels)
+
+
+def near_part(panels, own, swap):
+    rows, cols = rows_in(panels), rows_in([own, swap])
+    return margin_call(
+        near_kernel, rows, cols, rows, [pltpu.VMEM((cols, CHUNK), F32)], [],
+        [*panels, own, swap], [rows, rows, 2 * cols], "near_part",
+    )
+
+
+def far_part(near, hsp, panels):
+    rows, cols = rows_in(panels), near.shape[0]
+    return margin_call(
+        far_kernel, rows, cols, near.shape[1] + rows, [], [near], [hsp, *panels], [rows, rows], "far_part",
+    )
 
 
 def rotate_kernel(margin_ref, *refs):
@@ -345,10 +376,10 @@
     half = NSPLIT // 2
     far_a, far_b = step_x(left[:half], 1), step_x(right[half:], -1)
     hpsi_swap = swap_core(hpsi_cols)
-    near, *near_halves = margin_part([own, left, right], hpsi_cols, hpsi_swap)
-    far, *far_halves = margin_part([far_a, far_b], hpsi_cols, hpsi_swap)
-    mine = jnp.concatenate([sum_over_cols(near), sum_over_cols(far)], axis=1)
-    margin = exchange(jnp.broadcast_to(mine[None], (NSPLIT, *mine.shape))).reshape(-1, mine.shape[1])
+    near, *near_halves, hsp = near_part([own, left, right], hpsi_cols, hpsi_swap)
+    part, *far_halves = far_part(near, hsp, [far_a, far_b])
+    mine = jnp.sum(exchange(part.reshape(NSPLIT, -1, part.shape[1])), axis=0)
+    margin = exchange(jnp.broadcast_to(mine[None], (NSPLIT, *mine.shape))).reshape(part.shape)
     grad_mine, grad_other = rotated(margin, near_halves + far_halves, hpsi_cols)
     grad_cols = grad_mine - swap_core(grad_other)
     back = exchange(grad_cols)

time: 243 us -> 245 us (level)
  blocking collectives: 69.5 us -> 93.3 us
  starting transfers between devices: 36.7 us -> 23.9 us
  local copies, waits for them, and re-layouts: 19 us -> 13.8 us
  waiting for transfers between devices: 64.4 us -> 61.6 us
    all_to_all x2 -> x3, blocking collectives: 69.5 us -> 93.3 us  [exchange(): return lax.all_to_all(pieces, COEF, split_axis=0, concat_axis=0, tiled=True)]
    all_to_all x4 -> x2, starting transfers between devices: 30 us -> 17.1 us  [exchange(): return lax.all_to_all(pieces, COEF, split_axis=0, concat_axis=0, tiled=True)]
    all_to_all x4 -> x2, waiting for transfers between devices: 59.2 us -> 46.3 us  [exchange(): return lax.all_to_all(pieces, COEF, split_axis=0, concat_axis=0, tiled=True)]
    ppermute x4, waiting for transfers between devices: 1.57 us -> 11.7 us  [step_x(): return lax.ppermute(pieces, 'x', [(i, (i + step) % 4) for i in range(4)])]
    unnamed x27 -> x23, local copies, waits for them, and re-layouts: 13.7 us -> 10.4 us
  transfers between devices with their start and end apart: 10 -> 8, of which waited for: 6 -> 5; matrix products, arithmetic and copies ran while one was open for 3% -> 1% of each run, Pallas kernels for 18% -> 16%
where the time goes in v5:
time: 245 us; the launch traced here: 244 us
  blocking collectives  93.3 us (38%)
  waiting for transfers between devices  61.6 us (25%)
  Pallas kernels  49.8 us (20%)
  starting transfers between devices  23.9 us (10%)
  local copies, waits for them, and re-layouts  13.8 us (6%)
    all_to_all x3, blocking collectives, exchange(): return lax.all_to_all(pieces, COEF, split_axis=0, concat_axis=0, tiled=True)  93.3 us
    all_to_all x2, waiting for transfers between devices, exchange(): return lax.all_to_all(pieces, COEF, split_axis=0, concat_axis=0, tiled=True)  46.3 us
    pallas_call x1, Pallas kernels, hamiltonian(): pl.pallas_call(h_kernel, out_shape=jax.ShapeDtypeStruct(orbitals.shape, F...  31.7 us
    all_to_all x2, starting transfers between devices, exchange(): return lax.all_to_all(pieces, COEF, split_axis=0, concat_axis=0, tiled=True)  17.1 us
    pallas_call x2, Pallas kernels, margin_call(): pl.pallas_call(kernel, grid=(width // CHUNK,), out_shape=[jax.ShapeDtypeS...  11.8 us
    ppermute x4, waiting for transfers between devices, step_x(): return lax.ppermute(pieces, 'x', [(i, (i + step) % 4) for i in range(4)])  11.7 us
    unnamed x23, local copies, waits for them, and re-layouts  10.4 us
    ppermute x4, starting transfers between devices, step_x(): return lax.ppermute(pieces, 'x', [(i, (i + step) % 4) for i in range(4)])  6.71 us
  transfers between devices with their start and end apart: 8, of which 5 were waited for; matrix products, arithmetic and copies ran while one was open for 1% of the time, Pallas kernels for 16%

profile of v5, /device:TPU:64, one launch (start us, length us, event | category | flops | bytes accessed | tf_op | source)
XLA Modules:
  0.0 244.0 jit_solution(10603539117864388956)
XLA Ops:
  0.0 0.0 copy-start.8
  0.0 0.0 copy-start.9
  0.0 11.0 %all-to-all-start = ((f32[32,4,3456]{2,1,0:T(4,128)}), f32[32,4,3456]{2,1,0:T(4,128)S(1)}, u32[]{:S(2)}, u32[]{:S(2)}) async-start(f32[32,4,3456]{2,1,0:T(4,128)} %bitcast.11), calls=%async_computation | async-start | bytes 3538944 | tf_op jit(solution)/shard_map/all_to_all | solution.py:206
  11.1 0.0 copy-done.10
  11.1 0.8 reshape.20.pot_ref
  11.9 0.0 copy-done.8
  11.9 0.0 copy-done.9
  11.9 0.0 copy-start.1
  11.9 1.5 copy-done.1
  13.4 0.0 copy-start.3
  13.4 1.0 copy-done.3
  14.4 31.7 %hamiltonian.1 = f32[4,110592]{1,0:T(4,128)S(1)} custom-call(f32[16]{0:T(128)S(1)} %copy-done.8, f32[29]{0:T(128)S(1)} %copy-done.9, f32[4,110592]{1,0:T(4,128)S(1)} %copy-done.1, f32[48,2304]{1,0:T(8,128)S(1)} %copy-done.3), custom_call_target="tpu_custom_call" | custom-call | flops 24000000000 | bytes 5308416 | tf_op jit(solution)/shard_map/hamiltonian/pallas_call | solution.py:179
  46.1 0.0 copy-start.2
  46.1 1.2 copy-done.2
  47.3 6.9 %all-to-all-done.refs_0_ = f32[32,4,3456]{2,1,0:T(4,128)S(1)} async-done(((f32[32,4,3456]{2,1,0:T(4,128)}), f32[32,4,3456]{2,1,0:T(4,128)S(1)}, u32[]{:S(2)}, u32[]{:S(2)}) %all-to-all-start) | async-done | bytes 1769504 | tf_op jit(solution)/shard_map/all_to_all | solution.py:206
  54.2 6.0 %all-to-all-start.1 = ((f32[32,4,3456]{2,1,0:T(4,128)}), f32[32,4,3456]{2,1,0:T(4,128)S(1)}, u32[]{:S(2)}, u32[]{:S(2)}) async-start(f32[32,4,3456]{2,1,0:T(4,128)} %bitcast.12), calls=%async_computation.1 | async-start | bytes 3538944 | tf_op jit(solution)/shard_map/all_to_all | solution.py:206
  60.2 1.6 collective-permute-start
  61.8 1.7 collective-permute-start.1
  63.5 39.4 %all-to-all-done.1.refs_3_.refs_4_ = f32[32,4,3456]{2,1,0:T(4,128)S(1)} async-done(((f32[32,4,3456]{2,1,0:T(4,128)}), f32[32,4,3456]{2,1,0:T(4,128)S(1)}, u32[]{:S(2)}, u32[]{:S(2)}) %all-to-all-start.1) | async-done | bytes 1769504 | tf_op jit(solution)/shard_map/all_to_all | solution.py:206
  103.0 0.0 collective-permute-start.2
  103.0 0.0 collective-permute-done.refs_1_
  103.0 1.2 slice.8
  104.2 1.6 collective-permute-start.3
  105.8 0.0 collective-permute-done.1.refs_2_
  105.8 1.2 slice.9
  107.0 1.8 collective-permute-start.4
  108.8 0.0 collective-permute-done.2.refs_4_
  108.8 8.3 %near_part.1 = (f32[256,384]{1,0:T(8,128)S(1)}, bf16[384,3456]{1,0:T(8,128)(2,1)}, bf16[384,3456]{1,0:T(8,128)(2,1)}, bf16[512,3456]{1,0:T(8,128)(2,1)}) custom-call(f32[32,4,3456]{2,1,0:T(4,128)S(1)} %all-to-all-done.refs_0_, f32[32,4,3456]{2,1,0:T(4,128)} %collective-permute-done.refs_1_, f32[32,4,3456]{2,1,0:T(4,128)} %collective-permute-done.1.refs_2_, ...), custom_call_target="tpu_custom_call" | custom-call | flops 2038431744 | bytes 17694720 | tf_op jit(solution)/shard_map/near_part/pallas_call | solution.py:287
  117.2 10.4 %collective-permute-done.3.refs_0_ = f32[16,4,3456]{2,1,0:T(4,128)S(1)} collective-permute-done((f32[16,4,3456]{2,1,0:T(4,128)S(1)}, f32[16,4,3456]{2,1,0:T(4,128)S(1)}, u32[]{:S(2)}, u32[]{:S(2)}) %collective-permute-start.3) | collective-permute-done | bytes 884768 | tf_op jit(solution)/shard_map/ppermute | solution.py:215
  127.5 1.3 collective-permute-done.4.refs_1_
  128.9 0.0 copy-start
  128.9 2.0 copy-done
  130.9 3.5 %far_part.1 = (f32[256,512]{1,0:T(8,128)S(1)}, bf16[128,3456]{1,0:T(8,128)(2,1)}, bf16[128,3456]{1,0:T(8,128)(2,1)}) custom-call(f32[256,384]{1,0:T(8,128)S(1)} %get-tuple-element.16.near_ref, bf16[512,3456]{1,0:T(8,128)(2,1)S(1)} %copy-done, f32[16,4,3456]{2,1,0:T(4,128)S(1)} %collective-permute-done.3.refs_0_, ...), custom_call_target="tpu_custom_call" | custom-call | flops 679477248 | bytes 10616832 | tf_op jit(solution)/shard_map/far_part/pallas_call | solution.py:287
  134.3 0.0 copy-start.6
  134.3 22.6 %all_to_all.25 = f32[32,8,512]{2,1,0:T(8,128)} all-to-all(f32[32,8,512]{2,1,0:T(8,128)S(1)} %bitcast.14), channel_id=1, replica_groups=mesh['x'=4,'zl'=2,'y'=4,'core'=2,'zh'=4] {'y','zl','zh'}, dimensions={0} | all-to-all | bytes 1048576 | tf_op jit(solution)/shard_map/all_to_all | solution.py:206
  156.9 1.1 reduce_sum.9
  158.0 0.1 broadcast_in_dim.2
  158.1 21.4 %all_to_all.26 = f32[32,8,512]{2,1,0:T(8,128)S(1)} all-to-all(f32[32,8,512]{2,1,0:T(8,128)S(1)} %broadcast_in_dim.2), channel_id=1, replica_groups=mesh['x'=4,'zl'=2,'y'=4,'core'=2,'zh'=4] {'y','zl','zh'}, dimensions={0} | all-to-all | bytes 1048576 | tf_op jit(solution)/shard_map/all_to_all | solution.py:206
  179.5 0.0 copy-done.6
  179.5 0.0 copy-done.7
  179.5 1.7 copy-done.4
  181.3 1.7 copy-done.5
  183.0 6.3 %rotated.1 = (f32[32,4,3456]{2,1,0:T(4,128)S(1)}, f32[32,4,3456]{2,1,0:T(4,128)S(1)}) custom-call(f32[256,512]{1,0:T(8,128)S(1)} %bitcast.13, bf16[384,3456]{1,0:T(8,128)(2,1)S(1)} %copy-done.4, bf16[384,3456]{1,0:T(8,128)(2,1)S(1)} %copy-done.5, bf16[128,3456]{1,0:T(8,128)(2,1)S(1)} %copy-done.6, bf16[128,3456]{1,0:T(8,128)(2,1)S(1)} %copy-done.7, ...), custom_call_target="tpu_custom_call" | custom-call | flops 2717908992 | bytes 14155776 | tf_op jit(solution)/shard_map/rotated/pallas_call | solution.py:353
  189.3 0.1 collective-permute-start.5
  189.4 3.7 %collective-permute-done.5 = f32[32,4,3456]{2,1,0:T(4,128)S(1)} collective-permute-done((f32[32,4,3456]{2,1,0:T(4,128)S(1)}, f32[32,4,3456]{2,1,0:T(4,128)S(1)}, u32[]{:S(2)}, u32[]{:S(2)}) %collective-permute-start.5) | collective-permute-done | bytes 1769504 | tf_op jit(solution)/shard_map/ppermute | solution.py:219
  193.1 0.5 sub.3
  193.6 49.2 %all_to_all.27 = f32[32,4,3456]{2,1,0:T(4,128)S(1)} all-to-all(f32[32,4,3456]{2,1,0:T(4,128)S(1)} %sub.3), channel_id=1, replica_groups=mesh['x'=4,'zl'=2,'y'=4,'core'=2,'zh'=4] {'y','zl','zh'}, dimensions={0} | all-to-all | bytes 3538944 | tf_op jit(solution)/shard_map/all_to_all | solution.py:206
  242.8 1.2 copy.6
  (4 shorter events, 0.0 us)
Async XLA Ops:
  0.0 11.1 %copy-start.10 = (f32[110592]{0:T(1024)S(1)}, f32[110592]{0:T(1024)}, u32[]{:S(2)}) copy-start(f32[110592]{0:T(1024)} %param.5) | copy-start | bytes 1327108
  0.0 11.9 %copy-start.8 = (f32[16]{0:T(128)S(1)}, f32[16]{0:T(128)}, u32[]{:S(2)}) copy-start(f32[16]{0:T(128)} %magic_ref.1) | copy-start | bytes 196
  0.0 11.9 %copy-start.9 = (f32[29]{0:T(128)S(1)}, f32[29]{0:T(128)}, u32[]{:S(2)}) copy-start(f32[29]{0:T(128)} %kinetic_ref.1) | copy-start | bytes 352
  0.0 54.2 %all-to-all-start = ((f32[32,4,3456]{2,1,0:T(4,128)}), f32[32,4,3456]{2,1,0:T(4,128)S(1)}, u32[]{:S(2)}, u32[]{:S(2)}) async-start(f32[32,4,3456]{2,1,0:T(4,128)} %bitcast.11), calls=%async_computation | async-start | bytes 3538944 | tf_op jit(solution)/shard_map/all_to_all | solution.py:206
  11.9 1.5 copy-start.1
  13.4 1.0 copy-start.3
  46.1 1.2 copy-start.2
  54.2 48.8 %all-to-all-start.1 = ((f32[32,4,3456]{2,1,0:T(4,128)}), f32[32,4,3456]{2,1,0:T(4,128)S(1)}, u32[]{:S(2)}, u32[]{:S(2)}) async-start(f32[32,4,3456]{2,1,0:T(4,128)} %bitcast.12), calls=%async_computation.1 | async-start | bytes 3538944 | tf_op jit(solution)/shard_map/all_to_all | solution.py:206
  60.2 42.7 %collective-permute-start = (f32[32,4,3456]{2,1,0:T(4,128)S(1)}, f32[32,4,3456]{2,1,0:T(4,128)}, u32[]{:S(2)}, u32[]{:S(2)}) collective-permute-start(f32[32,4,3456]{2,1,0:T(4,128)S(1)} %all-to-all-done.refs_0_), channel_id=1, source_target_pairs={{0,64},{64,128},{128,192},{192,0},{1,65},{65,129},{129,193},{193,1... | collective-permute-start | bytes 5308424 | tf_op jit(solution)/shard_map/ppermute | solution.py:215
  61.8 44.0 %collective-permute-start.1 = (f32[32,4,3456]{2,1,0:T(4,128)S(1)}, f32[32,4,3456]{2,1,0:T(4,128)}, u32[]{:S(2)}, u32[]{:S(2)}) collective-permute-start(f32[32,4,3456]{2,1,0:T(4,128)S(1)} %all-to-all-done.refs_0_), channel_id=1, source_target_pairs={{0,192},{64,0},{128,64},{192,128},{1,193},{65,1},{129,65},{193,129... | collective-permute-start | bytes 5308424 | tf_op jit(solution)/shard_map/ppermute | solution.py:215
  103.0 5.9 %collective-permute-start.2 = (f32[32,4,3456]{2,1,0:T(4,128)S(1)}, f32[32,4,3456]{2,1,0:T(4,128)S(1)}, u32[]{:S(2)}, u32[]{:S(2)}) collective-permute-start(f32[32,4,3456]{2,1,0:T(4,128)S(1)} %all-to-all-done.1.refs_3_.refs_4_), channel_id=1, source_target_pairs={{0,4},{4,0},{1,5},{5,1},{2,6},{6,2},{3,7},{7,3},{8,12},{12,8},{9,1... | collective-permute-start | bytes 5308424 | tf_op jit(solution)/shard_map/ppermute | solution.py:219
  104.2 23.3 %collective-permute-start.3 = (f32[16,4,3456]{2,1,0:T(4,128)S(1)}, f32[16,4,3456]{2,1,0:T(4,128)S(1)}, u32[]{:S(2)}, u32[]{:S(2)}) collective-permute-start(f32[16,4,3456]{2,1,0:T(4,128)S(1)} %slice.8), channel_id=1, source_target_pairs={{0,64},{64,128},{128,192},{192,0},{1,65},{65,129},{129,193},{193,1... | collective-permute-start | bytes 2654216 | tf_op jit(solution)/shard_map/ppermute | solution.py:215
  107.0 21.9 %collective-permute-start.4 = (f32[16,4,3456]{2,1,0:T(4,128)S(1)}, f32[16,4,3456]{2,1,0:T(4,128)S(1)}, u32[]{:S(2)}, u32[]{:S(2)}) collective-permute-start(f32[16,4,3456]{2,1,0:T(4,128)S(1)} %slice.9), channel_id=1, source_target_pairs={{0,192},{64,0},{128,64},{192,128},{1,193},{65,1},{129,65},{193,129... | collective-permute-start | bytes 2654216 | tf_op jit(solution)/shard_map/ppermute | solution.py:215
  128.9 2.0 copy-start
  134.3 45.2 %copy-start.6 = (bf16[128,3456]{1,0:T(8,128)(2,1)S(1)}, bf16[128,3456]{1,0:T(8,128)(2,1)}, u32[]{:S(2)}) copy-start(bf16[128,3456]{1,0:T(8,128)(2,1)} %get-tuple-element.21.refs_2_) | copy-start | bytes 2654212
  134.3 45.2 %copy-start.7 = (bf16[128,3456]{1,0:T(8,128)(2,1)S(1)}, bf16[128,3456]{1,0:T(8,128)(2,1)}, u32[]{:S(2)}) copy-start(bf16[128,3456]{1,0:T(8,128)(2,1)} %get-tuple-element.22.refs_3_) | copy-start | bytes 2654212
  179.5 1.8 copy-start.4
  181.3 1.7 copy-start.5
  189.3 3.8 %collective-permute-start.5 = (f32[32,4,3456]{2,1,0:T(4,128)S(1)}, f32[32,4,3456]{2,1,0:T(4,128)S(1)}, u32[]{:S(2)}, u32[]{:S(2)}) collective-permute-start(f32[32,4,3456]{2,1,0:T(4,128)S(1)} %get-tuple-element.24), channel_id=1, source_target_pairs={{0,4},{4,0},{1,5},{5,1},{2,6},{6,2},{3,7},{7,3},{8,12},{12,8},{9,1... | collective-permute-start | bytes 5308424 | tf_op jit(solution)/shard_map/ppermute | solution.py:219

commit v6 on v5

--- a/solution.py
+++ b/solution.py
@@ -13,6 +13,7 @@
 NSPLIT = 32
 CHUNK = 1152
 WIDE = 1152
+VMEM_MOST = 58 * 1024 * 1024
 PLANE = G * G
 BLK = 16 * G
 F32 = jnp.float32
@@ -287,17 +288,17 @@
     return pl.pallas_call(
         kernel,
         grid=(width // CHUNK,),
-        out_shape=[jax.ShapeDtypeStruct((cols, out_cols), F32)] + [in_hbm(r, width) for r in outs],
+        out_shape=[jax.ShapeDtypeStruct((cols, out_cols), F32)] + outs(width),
         in_specs=[pl.BlockSpec(v.shape, lambda k: (0, 0)) for v in whole]
         + [chunk_spec(v, CHUNK) for v in arrays],
         out_specs=[pl.BlockSpec((cols, out_cols), lambda k: (0, 0))]
-        + [pl.BlockSpec((r, CHUNK), lambda k: (0, k)) for r in outs],
+        + [chunk_spec(v, CHUNK) for v in outs(width)],
         scratch_shapes=[pltpu.VMEM((rows, CHUNK), F32)] + extra,
         cost_estimate=pl.CostEstimate(
             flops=6 * rows * cols * width, transcendentals=0,
             bytes_accessed=4 * (2 * rows + 2 * cols) * width,
         ),
-        compiler_params=pltpu.CompilerParams(vmem_limit_bytes=32 * 1024 * 1024),
+        compiler_params=pltpu.CompilerParams(vmem_limit_bytes=24 * 1024 * 1024),
         name=name,
     )(*whole, *arrays)
 
@@ -310,14 +311,15 @@
     rows, cols = rows_in(panels), rows_in([own, swap])
     return margin_call(
         near_kernel, rows, cols, rows, [pltpu.VMEM((cols, CHUNK), F32)], [],
-        [*panels, own, swap], [rows, rows, 2 * cols], "near_part",
+        [*panels, own, swap], lambda w: [in_hbm(rows, w)] * 2 + [jax.ShapeDtypeStruct((2 * cols, w), BF16)], "near_part",
     )
 
 
 def far_part(near, hsp, panels):
     rows, cols = rows_in(panels), near.shape[0]
     return margin_call(
-        far_kernel, rows, cols, near.shape[1] + rows, [], [near], [hsp, *panels], [rows, rows], "far_part",
+        far_kernel, rows, cols, near.shape[1] + rows, [], [near], [hsp, *panels],
+        lambda w: [in_hbm(rows, w)] * 2, "far_part",
     )
 
 
@@ -362,7 +364,7 @@
             flops=6 * rows * cols * width, transcendentals=0,
             bytes_accessed=4 * (rows + 2 * cols) * width,
         ),
-        compiler_params=pltpu.CompilerParams(vmem_limit_bytes=24 * 1024 * 1024),
+        compiler_params=pltpu.CompilerParams(vmem_limit_bytes=VMEM_MOST),
         name="rotated",
     )(margin, *halves, base)
 
@@ -374,7 +376,9 @@
     left, right = step_x(own, 1), step_x(own, -1)
     hpsi_cols = to_cols(hpsi)
     half = NSPLIT // 2
-    far_a, far_b = step_x(left[:half], 1), step_x(right[half:], -1)
+    from_left, from_right = left[:half], right[half:]
+    far_a, far_b = step_x(from_left, 1), step_x(from_right, -1)
+    hpsi_cols, _, _ = lax.optimization_barrier((hpsi_cols, from_left, from_right))
     hpsi_swap = swap_core(hpsi_cols)
     near, *near_halves, hsp = near_part([own, left, right], hpsi_cols, hpsi_swap)
     part, *far_halves = far_part(near, hsp, [far_a, far_b])

time: 245 us -> 248 us (1.012)
  blocking collectives: 93.3 us -> 97.1 us
    all_to_all x2, waiting for transfers between devices: 46.3 us -> 7.32 us  [exchange(): return lax.all_to_all(pieces, COEF, split_axis=0, concat_axis=0, tiled=True)]
    ppermute x4, waiting for transfers between devices: 11.7 us -> 50.4 us  [step_x(): return lax.ppermute(pieces, 'x', [(i, (i + step) % 4) for i in range(4)])]
    all_to_all x3, blocking collectives: 93.3 us -> 97.1 us  [exchange(): return lax.all_to_all(pieces, COEF, split_axis=0, concat_axis=0, tiled=True)]
    unnamed x23 -> x21, local copies, waits for them, and re-layouts: 10.4 us -> 7.6 us
    pallas_call x1, Pallas kernels: 6.27 us -> 9.07 us  [rotated(): pl.pallas_call(rotate_kernel, grid=(width // WIDE,), out_shape=[shape, sh...]
  transfers between devices with their start and end apart: 8 -> 8, of which waited for: 5 -> 7; matrix products, arithmetic and copies ran while one was open for 1% -> 2% of each run, Pallas kernels for 16% -> 16%
where the time goes in v6:
time: 248 us; the launch traced here: 247 us
  blocking collectives  97.1 us (39%)
  waiting for transfers between devices  63.2 us (25%)
  Pallas kernels  51.3 us (21%)
  starting transfers between devices  22 us (9%)
  local copies, waits for them, and re-layouts  11.6 us (5%)
    all_to_all x3, blocking collectives, exchange(): return lax.all_to_all(pieces, COEF, split_axis=0, concat_axis=0, tiled=True)  97.1 us
    ppermute x4, waiting for transfers between devices, step_x(): return lax.ppermute(pieces, 'x', [(i, (i + step) % 4) for i in range(4)])  50.4 us
    pallas_call x1, Pallas kernels, hamiltonian(): pl.pallas_call(h_kernel, out_shape=jax.ShapeDtypeStruct(orbitals.shape, F...  31.7 us
    all_to_all x2, starting transfers between devices, exchange(): return lax.all_to_all(pieces, COEF, split_axis=0, concat_axis=0, tiled=True)  17.1 us
    pallas_call x2, Pallas kernels, margin_call(): pl.pallas_call(kernel, grid=(width // CHUNK,), out_shape=[jax.ShapeDtypeS...  10.5 us
    pallas_call x1, Pallas kernels, rotated(): pl.pallas_call(rotate_kernel, grid=(width // WIDE,), out_shape=[shape, sh...  9.07 us
    unnamed x21, local copies, waits for them, and re-layouts  7.6 us
    all_to_all x2, waiting for transfers between devices, exchange(): return lax.all_to_all(pieces, COEF, split_axis=0, concat_axis=0, tiled=True)  7.32 us
  transfers between devices with their start and end apart: 8, of which 7 were waited for; matrix products, arithmetic and copies ran while one was open for 2% of the time, Pallas kernels for 16%

profile of v6, /device:TPU:64, one launch (start us, length us, event | category | flops | bytes accessed | tf_op | source)
XLA Modules:
  0.0 247.3 jit_solution(532754363313281835)
XLA Ops:
  0.0 0.0 copy-start.5
  0.0 0.0 copy-start.8
  0.0 0.0 copy-start.9
  0.0 11.0 %all-to-all-start = ((f32[32,4,3456]{2,1,0:T(4,128)}), f32[32,4,3456]{2,1,0:T(4,128)S(1)}, u32[]{:S(2)}, u32[]{:S(2)}) async-start(f32[32,4,3456]{2,1,0:T(4,128)} %bitcast.11), calls=%async_computation | async-start | bytes 3538944 | tf_op jit(solution)/shard_map/all_to_all | solution.py:207
  11.1 1.9 reshape.20.pot_ref
  12.9 0.0 copy-done.5
  12.9 0.0 copy-done.8
  12.9 0.0 copy-done.9
  12.9 0.0 copy-start.7
  12.9 1.0 copy-done.7
  13.9 31.7 %hamiltonian.1 = f32[4,110592]{1,0:T(4,128)S(1)} custom-call(f32[16]{0:T(128)S(1)} %copy-done.8, f32[29]{0:T(128)S(1)} %copy-done.9, f32[4,110592]{1,0:T(4,128)S(1)} %copy-done.5, f32[48,2304]{1,0:T(8,128)S(1)} %copy-done.7), custom_call_target="tpu_custom_call" | custom-call | flops 24000000000 | bytes 5308416 | tf_op jit(solution)/shard_map/hamiltonian/pallas_call | solution.py:180
  45.6 0.0 copy-start.6
  45.6 1.2 copy-done.6
  46.9 7.3 %all-to-all-done.refs_0_ = f32[32,4,3456]{2,1,0:T(4,128)S(1)} async-done(((f32[32,4,3456]{2,1,0:T(4,128)}), f32[32,4,3456]{2,1,0:T(4,128)S(1)}, u32[]{:S(2)}, u32[]{:S(2)}) %all-to-all-start) | async-done | bytes 1769504 | tf_op jit(solution)/shard_map/all_to_all | solution.py:207
  54.2 6.0 %all-to-all-start.1 = ((f32[32,4,3456]{2,1,0:T(4,128)}), f32[32,4,3456]{2,1,0:T(4,128)S(1)}, u32[]{:S(2)}, u32[]{:S(2)}) async-start(f32[32,4,3456]{2,1,0:T(4,128)} %bitcast.12), calls=%async_computation.1 | async-start | bytes 3538944 | tf_op jit(solution)/shard_map/all_to_all | solution.py:207
  60.2 2.8 %collective-permute-start.1 = (f32[32,4,3456]{2,1,0:T(4,128)S(1)}, f32[32,4,3456]{2,1,0:T(4,128)S(1)}, u32[]{:S(2)}, u32[]{:S(2)}) collective-permute-start(f32[32,4,3456]{2,1,0:T(4,128)S(1)} %all-to-all-done.refs_0_), channel_id=1, source_target_pairs={{0,192},{64,0},{128,64},{192,128},{1,193},{65,1},{129,65},{193,129... | collective-permute-start | bytes 5308424 | tf_op jit(solution)/shard_map/ppermute | solution.py:216
  63.1 0.0 collective-permute-start
  63.1 36.7 %collective-permute-done.1.refs_2_ = f32[32,4,3456]{2,1,0:T(4,128)S(1)} collective-permute-done((f32[32,4,3456]{2,1,0:T(4,128)S(1)}, f32[32,4,3456]{2,1,0:T(4,128)S(1)}, u32[]{:S(2)}, u32[]{:S(2)}) %collective-permute-start.1) | collective-permute-done | bytes 1769504 | tf_op jit(solution)/shard_map/ppermute | solution.py:216
  99.8 0.0 copy-start.1
  99.8 1.1 slice.9
  100.9 2.3 collective-permute-done.refs_1_
  103.2 0.0 copy-done.1
  103.2 1.0 slice.8
  104.1 0.0 copy-start.3
  104.1 1.2 copy-done.3
  105.4 0.0 all-to-all-done.1.refs_3_.refs_4_
  105.4 0.0 collective-permute-start.2
  105.4 1.9 collective-permute-start.4
  107.3 0.2 collective-permute-start.3
  107.5 1.6 collective-permute-done.2.refs_4_
  109.1 0.0 copy-start.2
  109.1 1.5 copy-done.2
  110.5 0.0 copy-start.4
  110.5 1.5 copy-done.4
  112.0 7.0 %near_part.1 = (f32[256,384]{1,0:T(8,128)S(1)}, bf16[384,3456]{1,0:T(8,128)(2,1)}, bf16[384,3456]{1,0:T(8,128)(2,1)}, bf16[512,3456]{1,0:T(8,128)(2,1)S(1)}) custom-call(f32[32,4,3456]{2,1,0:T(4,128)S(1)} %all-to-all-done.refs_0_, f32[32,4,3456]{2,1,0:T(4,128)S(1)} %copy-done.4, f32[32,4,3456]{2,1,0:T(4,128)S(1)} %copy-done.2, ...), custom_call_target="tpu_custom_call" | custom-call | flops 2038431744 | bytes 17694720 | tf_op jit(solution)/shard_map/near_part/pallas_call | solution.py:288
  119.0 0.0 copy-done
  119.0 8.7 %collective-permute-done.4.refs_1_ = f32[16,4,3456]{2,1,0:T(4,128)S(1)} collective-permute-done((f32[16,4,3456]{2,1,0:T(4,128)}, f32[16,4,3456]{2,1,0:T(4,128)S(1)}, u32[]{:S(2)}, u32[]{:S(2)}) %collective-permute-start.4) | collective-permute-done | bytes 884768 | tf_op jit(solution)/shard_map/ppermute | solution.py:216
  127.6 2.8 %collective-permute-done.3.refs_0_ = f32[16,4,3456]{2,1,0:T(4,128)S(1)} collective-permute-done((f32[16,4,3456]{2,1,0:T(4,128)}, f32[16,4,3456]{2,1,0:T(4,128)S(1)}, u32[]{:S(2)}, u32[]{:S(2)}) %collective-permute-start.3) | collective-permute-done | bytes 884768 | tf_op jit(solution)/shard_map/ppermute | solution.py:216
  130.4 3.5 %far_part.1 = (f32[256,512]{1,0:T(8,128)S(1)}, bf16[128,3456]{1,0:T(8,128)(2,1)}, bf16[128,3456]{1,0:T(8,128)(2,1)}) custom-call(f32[256,384]{1,0:T(8,128)S(1)} %get-tuple-element.18.near_ref, bf16[512,3456]{1,0:T(8,128)(2,1)S(1)} %get-tuple-element.19.hsp_ref, f32[16,4,3456]{2,1,0:T(4,128)S(1)} %collective-permute-done.3.refs_0_, ...), custom_call_target="tpu_custom_call" | custom-call | flops 679477248 | bytes 10616832 | tf_op jit(solution)/shard_map/far_part/pallas_call | solution.py:288
  133.9 26.3 %all_to_all.25 = f32[32,8,512]{2,1,0:T(8,128)S(1)} all-to-all(f32[32,8,512]{2,1,0:T(8,128)S(1)} %bitcast.13), channel_id=1, replica_groups=mesh['x'=4,'zl'=2,'y'=4,'core'=2,'zh'=4] {'y','zl','zh'}, dimensions={0} | all-to-all | bytes 1048576 | tf_op jit(solution)/shard_map/all_to_all | solution.py:207
  160.3 0.1 broadcast_in_dim.2
  160.3 21.6 %all_to_all.26 = f32[32,8,512]{2,1,0:T(8,128)} all-to-all(f32[32,8,512]{2,1,0:T(8,128)S(1)} %broadcast_in_dim.2), channel_id=1, replica_groups=mesh['x'=4,'zl'=2,'y'=4,'core'=2,'zh'=4] {'y','zl','zh'}, dimensions={0} | all-to-all | bytes 1048576 | tf_op jit(solution)/shard_map/all_to_all | solution.py:207
  181.9 9.1 %rotated.1 = (f32[32,4,3456]{2,1,0:T(4,128)}, f32[32,4,3456]{2,1,0:T(4,128)}) custom-call(f32[256,512]{1,0:T(8,128)} %bitcast.15, bf16[384,3456]{1,0:T(8,128)(2,1)} %get-tuple-element.21.refs_0_, bf16[384,3456]{1,0:T(8,128)(2,1)} %get-tuple-element.22.refs_1_, bf16[128,3456]{1,0:T(8,128)(2,1)} %get-tuple-element.23.refs_2_, ...), custom_call_target="tpu_custom_call" | custom-call | flops 2717908992 | bytes 14155776 | tf_op jit(solution)/shard_map/rotated/pallas_call | solution.py:355
  191.0 0.0 collective-permute-start.5
  191.0 3.9 %collective-permute-done.5 = f32[32,4,3456]{2,1,0:T(4,128)S(1)} collective-permute-done((f32[32,4,3456]{2,1,0:T(4,128)}, f32[32,4,3456]{2,1,0:T(4,128)S(1)}, u32[]{:S(2)}, u32[]{:S(2)}) %collective-permute-start.5) | collective-permute-done | bytes 1769504 | tf_op jit(solution)/shard_map/ppermute | solution.py:220
  194.9 1.9 sub.3
  196.8 49.3 %all_to_all.27 = f32[32,4,3456]{2,1,0:T(4,128)S(1)} all-to-all(f32[32,4,3456]{2,1,0:T(4,128)S(1)} %sub.3), channel_id=1, replica_groups=mesh['x'=4,'zl'=2,'y'=4,'core'=2,'zh'=4] {'y','zl','zh'}, dimensions={0} | all-to-all | bytes 3538944 | tf_op jit(solution)/shard_map/all_to_all | solution.py:207
  246.1 1.2 copy.6
  (2 shorter events, 0.0 us)
Async XLA Ops:
  0.0 12.9 %copy-start.5 = (f32[4,110592]{1,0:T(4,128)S(1)}, f32[4,110592]{1,0:T(4,128)}, u32[]{:S(2)}) copy-start(f32[4,110592]{1,0:T(4,128)} %psi_ref.1) | copy-start | bytes 5308420
  0.0 12.9 %copy-start.8 = (f32[16]{0:T(128)S(1)}, f32[16]{0:T(128)}, u32[]{:S(2)}) copy-start(f32[16]{0:T(128)} %magic_ref.1) | copy-start | bytes 196
  0.0 12.9 %copy-start.9 = (f32[29]{0:T(128)S(1)}, f32[29]{0:T(128)}, u32[]{:S(2)}) copy-start(f32[29]{0:T(128)} %kinetic_ref.1) | copy-start | bytes 352
  0.0 54.2 %all-to-all-start = ((f32[32,4,3456]{2,1,0:T(4,128)}), f32[32,4,3456]{2,1,0:T(4,128)S(1)}, u32[]{:S(2)}, u32[]{:S(2)}) async-start(f32[32,4,3456]{2,1,0:T(4,128)} %bitcast.11), calls=%async_computation | async-start | bytes 3538944 | tf_op jit(solution)/shard_map/all_to_all | solution.py:207
  12.9 1.0 copy-start.7
  45.6 1.2 copy-start.6
  54.2 51.2 %all-to-all-start.1 = ((f32[32,4,3456]{2,1,0:T(4,128)}), f32[32,4,3456]{2,1,0:T(4,128)S(1)}, u32[]{:S(2)}, u32[]{:S(2)}) async-start(f32[32,4,3456]{2,1,0:T(4,128)} %bitcast.12), calls=%async_computation.1 | async-start | bytes 3538944 | tf_op jit(solution)/shard_map/all_to_all | solution.py:207
  60.2 39.5 %collective-permute-start.1 = (f32[32,4,3456]{2,1,0:T(4,128)S(1)}, f32[32,4,3456]{2,1,0:T(4,128)S(1)}, u32[]{:S(2)}, u32[]{:S(2)}) collective-permute-start(f32[32,4,3456]{2,1,0:T(4,128)S(1)} %all-to-all-done.refs_0_), channel_id=1, source_target_pairs={{0,192},{64,0},{128,64},{192,128},{1,193},{65,1},{129,65},{193,129... | collective-permute-start | bytes 5308424 | tf_op jit(solution)/shard_map/ppermute | solution.py:216
  63.1 40.1 %collective-permute-start = (f32[32,4,3456]{2,1,0:T(4,128)S(1)}, f32[32,4,3456]{2,1,0:T(4,128)S(1)}, u32[]{:S(2)}, u32[]{:S(2)}) collective-permute-start(f32[32,4,3456]{2,1,0:T(4,128)S(1)} %all-to-all-done.refs_0_), channel_id=1, source_target_pairs={{0,64},{64,128},{128,192},{192,0},{1,65},{65,129},{129,193},{193,1... | collective-permute-start | bytes 5308424 | tf_op jit(solution)/shard_map/ppermute | solution.py:216
  99.8 3.4 %copy-start.1 = (f32[32,4,3456]{2,1,0:T(4,128)}, f32[32,4,3456]{2,1,0:T(4,128)S(1)}, u32[]{:S(2)}) copy-start(f32[32,4,3456]{2,1,0:T(4,128)S(1)} %collective-permute-done.1.refs_2_) | copy-start | bytes 5308420
  104.1 1.2 copy-start.3
  105.4 13.6 %copy-start = (f32[32,4,3456]{2,1,0:T(4,128)}, f32[32,4,3456]{2,1,0:T(4,128)S(1)}, u32[]{:S(2)}) copy-start(f32[32,4,3456]{2,1,0:T(4,128)S(1)} %all-to-all-done.1.refs_3_.refs_4_) | copy-start | bytes 5308420
  105.4 3.7 %collective-permute-start.2 = (f32[32,4,3456]{2,1,0:T(4,128)S(1)}, f32[32,4,3456]{2,1,0:T(4,128)S(1)}, u32[]{:S(2)}, u32[]{:S(2)}) collective-permute-start(f32[32,4,3456]{2,1,0:T(4,128)S(1)} %all-to-all-done.1.refs_3_.refs_4_), channel_id=1, source_target_pairs={{0,4},{4,0},{1,5},{5,1},{2,6},{6,2},{3,7},{7,3},{8,12},{12,8},{9,1... | collective-permute-start | bytes 5308424 | tf_op jit(solution)/shard_map/ppermute | solution.py:220
  105.4 22.3 %collective-permute-start.4 = (f32[16,4,3456]{2,1,0:T(4,128)}, f32[16,4,3456]{2,1,0:T(4,128)S(1)}, u32[]{:S(2)}, u32[]{:S(2)}) collective-permute-start(f32[16,4,3456]{2,1,0:T(4,128)} %slice.9), channel_id=1, source_target_pairs={{0,192},{64,0},{128,64},{192,128},{1,193},{65,1},{129,65},{193,129... | collective-permute-start | bytes 2654216 | tf_op jit(solution)/shard_map/ppermute | solution.py:216
  107.3 23.1 %collective-permute-start.3 = (f32[16,4,3456]{2,1,0:T(4,128)}, f32[16,4,3456]{2,1,0:T(4,128)S(1)}, u32[]{:S(2)}, u32[]{:S(2)}) collective-permute-start(f32[16,4,3456]{2,1,0:T(4,128)} %slice.8), channel_id=1, source_target_pairs={{0,64},{64,128},{128,192},{192,0},{1,65},{65,129},{129,193},{193,1... | collective-permute-start | bytes 2654216 | tf_op jit(solution)/shard_map/ppermute | solution.py:216
  109.1 1.5 copy-start.2
  110.5 1.5 copy-start.4
  191.0 3.9 %collective-permute-start.5 = (f32[32,4,3456]{2,1,0:T(4,128)}, f32[32,4,3456]{2,1,0:T(4,128)S(1)}, u32[]{:S(2)}, u32[]{:S(2)}) collective-permute-start(f32[32,4,3456]{2,1,0:T(4,128)} %get-tuple-element.26), channel_id=1, source_target_pairs={{0,4},{4,0},{1,5},{5,1},{2,6},{6,2},{3,7},{7,3},{8,12},{12,8},{9,1... | collective-permute-start | bytes 5308424 | tf_op jit(solution)/shard_map/ppermute | solution.py:220

commit v7 on v6

--- a/solution.py
+++ b/solution.py
@@ -13,7 +13,6 @@
 NSPLIT = 32
 CHUNK = 1152
 WIDE = 1152
-VMEM_MOST = 58 * 1024 * 1024
 PLANE = G * G
 BLK = 16 * G
 F32 = jnp.float32
@@ -283,6 +282,14 @@
     return pltpu.MemorySpace.HBM((rows, width), BF16)
 
 
+def near_outs(rows, cols):
+    return lambda w: [in_hbm(rows, w)] * 2 + [jax.ShapeDtypeStruct((2 * cols, w), BF16)]
+
+
+def far_outs(rows):
+    return lambda w: [jax.ShapeDtypeStruct((rows, w), BF16)] * 2
+
+
 def margin_call(kernel, rows, cols, out_cols, extra, whole, arrays, outs, name):
     width = arrays[-1].shape[-1]
     return pl.pallas_call(
@@ -311,15 +318,14 @@
     rows, cols = rows_in(panels), rows_in([own, swap])
     return margin_call(
         near_kernel, rows, cols, rows, [pltpu.VMEM((cols, CHUNK), F32)], [],
-        [*panels, own, swap], lambda w: [in_hbm(rows, w)] * 2 + [jax.ShapeDtypeStruct((2 * cols, w), BF16)], "near_part",
+        [*panels, own, swap], near_outs(rows, cols), "near_part",
     )
 
 
 def far_part(near, hsp, panels):
     rows, cols = rows_in(panels), near.shape[0]
     return margin_call(
-        far_kernel, rows, cols, near.shape[1] + rows, [], [near], [hsp, *panels],
-        lambda w: [in_hbm(rows, w)] * 2, "far_part",
+        far_kernel, rows, cols, near.shape[1] + rows, [], [near], [hsp, *panels], far_outs(rows), "far_part",
     )
 
 
@@ -364,7 +370,7 @@
             flops=6 * rows * cols * width, transcendentals=0,
             bytes_accessed=4 * (rows + 2 * cols) * width,
         ),
-        compiler_params=pltpu.CompilerParams(vmem_limit_bytes=VMEM_MOST),
+        compiler_params=pltpu.CompilerParams(vmem_limit_bytes=48 * 1024 * 1024),
         name="rotated",
     )(margin, *halves, base)
 
@@ -376,9 +382,7 @@
     left, right = step_x(own, 1), step_x(own, -1)
     hpsi_cols = to_cols(hpsi)
     half = NSPLIT // 2
-    from_left, from_right = left[:half], right[half:]
-    far_a, far_b = step_x(from_left, 1), step_x(from_right, -1)
-    hpsi_cols, _, _ = lax.optimization_barrier((hpsi_cols, from_left, from_right))
+    far_a, far_b = step_x(left[:half], 1), step_x(right[half:], -1)
     hpsi_swap = swap_core(hpsi_cols)
     near, *near_halves, hsp = near_part([own, left, right], hpsi_cols, hpsi_swap)
     part, *far_halves = far_part(near, hsp, [far_a, far_b])

time: 248 us -> 238 us (0.960)
  blocking collectives: 97.1 us -> 92.4 us
  local copies, waits for them, and re-layouts: 11.6 us -> 8.43 us
    all_to_all x2, waiting for transfers between devices: 7.32 us -> 46.7 us  [exchange(): return lax.all_to_all(pieces, COEF, split_axis=0, concat_axis=0, tiled=True)]
    ppermute x4, waiting for transfers between devices: 50.4 us -> 11.7 us  [step_x(): return lax.ppermute(pieces, 'x', [(i, (i + step) % 4) for i in range(4)])]
    all_to_all x3, blocking collectives: 97.1 us -> 92.4 us  [exchange(): return lax.all_to_all(pieces, COEF, split_axis=0, concat_axis=0, tiled=True)]
    unnamed x21 -> x13, local copies, waits for them, and re-layouts: 7.6 us -> 3.43 us
  transfers between devices with their start and end apart: 8 -> 8, of which waited for: 7 -> 5; matrix products, arithmetic and copies ran while one was open for 2% -> 2% of each run, Pallas kernels for 16% -> 17%
where the time goes in v7:
time: 238 us; the launch traced here: 237 us
  blocking collectives  92.4 us (39%)
  waiting for transfers between devices  62.1 us (26%)
  Pallas kernels  49.4 us (21%)
  starting transfers between devices  23.9 us (10%)
  local copies, waits for them, and re-layouts  8.43 us (4%)
    all_to_all x3, blocking collectives, exchange(): return lax.all_to_all(pieces, COEF, split_axis=0, concat_axis=0, tiled=True)  92.4 us
    all_to_all x2, waiting for transfers between devices, exchange(): return lax.all_to_all(pieces, COEF, split_axis=0, concat_axis=0, tiled=True)  46.7 us
    pallas_call x1, Pallas kernels, hamiltonian(): pl.pallas_call(h_kernel, out_shape=jax.ShapeDtypeStruct(orbitals.shape, F...  31.7 us
    all_to_all x2, starting transfers between devices, exchange(): return lax.all_to_all(pieces, COEF, split_axis=0, concat_axis=0, tiled=True)  17.1 us
    ppermute x4, waiting for transfers between devices, step_x(): return lax.ppermute(pieces, 'x', [(i, (i + step) % 4) for i in range(4)])  11.7 us
    pallas_call x2, Pallas kernels, margin_call(): pl.pallas_call(kernel, grid=(width // CHUNK,), out_shape=[jax.ShapeDtypeS...  10.5 us
    pallas_call x1, Pallas kernels, rotated(): pl.pallas_call(rotate_kernel, grid=(width // WIDE,), out_shape=[shape, sh...  7.22 us
    ppermute x4, starting transfers between devices, step_x(): return lax.ppermute(pieces, 'x', [(i, (i + step) % 4) for i in range(4)])  6.71 us
  transfers between devices with their start and end apart: 8, of which 5 were waited for; matrix products, arithmetic and copies ran while one was open for 2% of the time, Pallas kernels for 17%

profile of v7, /device:TPU:64, one launch (start us, length us, event | category | flops | bytes accessed | tf_op | source)
XLA Modules:
  0.0 236.9 jit_solution(6218045413588210593)
XLA Ops:
  0.0 0.0 copy-start.1
  0.0 0.0 copy-start.4
  0.0 0.0 copy-start.5
  0.0 11.0 %all-to-all-start = ((f32[32,4,3456]{2,1,0:T(4,128)}), f32[32,4,3456]{2,1,0:T(4,128)S(1)}, u32[]{:S(2)}, u32[]{:S(2)}) async-start(f32[32,4,3456]{2,1,0:T(4,128)} %bitcast.11), calls=%async_computation | async-start | bytes 3538944 | tf_op jit(solution)/shard_map/all_to_all | solution.py:206
  11.1 1.9 reshape.20.pot_ref
  12.9 0.0 copy-done.1
  12.9 0.0 copy-done.4
  12.9 0.0 copy-done.5
  12.9 0.0 copy-start.3
  12.9 1.0 copy-done.3
  13.9 31.7 %hamiltonian.1 = f32[4,110592]{1,0:T(4,128)S(1)} custom-call(f32[16]{0:T(128)S(1)} %copy-done.4, f32[29]{0:T(128)S(1)} %copy-done.5, f32[4,110592]{1,0:T(4,128)S(1)} %copy-done.1, f32[48,2304]{1,0:T(8,128)S(1)} %copy-done.3), custom_call_target="tpu_custom_call" | custom-call | flops 24000000000 | bytes 5308416 | tf_op jit(solution)/shard_map/hamiltonian/pallas_call | solution.py:179
  45.6 0.0 copy-start.2
  45.7 1.2 copy-done.2
  46.8 7.3 %all-to-all-done.refs_0_ = f32[32,4,3456]{2,1,0:T(4,128)S(1)} async-done(((f32[32,4,3456]{2,1,0:T(4,128)}), f32[32,4,3456]{2,1,0:T(4,128)S(1)}, u32[]{:S(2)}, u32[]{:S(2)}) %all-to-all-start) | async-done | bytes 1769504 | tf_op jit(solution)/shard_map/all_to_all | solution.py:206
  54.2 6.0 %all-to-all-start.1 = ((f32[32,4,3456]{2,1,0:T(4,128)}), f32[32,4,3456]{2,1,0:T(4,128)S(1)}, u32[]{:S(2)}, u32[]{:S(2)}) async-start(f32[32,4,3456]{2,1,0:T(4,128)} %bitcast.12), calls=%async_computation.1 | async-start | bytes 3538944 | tf_op jit(solution)/shard_map/all_to_all | solution.py:206
  60.2 1.6 collective-permute-start
  61.8 1.7 collective-permute-start.1
  63.5 39.4 %all-to-all-done.1.refs_3_.refs_4_ = f32[32,4,3456]{2,1,0:T(4,128)S(1)} async-done(((f32[32,4,3456]{2,1,0:T(4,128)}), f32[32,4,3456]{2,1,0:T(4,128)S(1)}, u32[]{:S(2)}, u32[]{:S(2)}) %all-to-all-start.1) | async-done | bytes 1769504 | tf_op jit(solution)/shard_map/all_to_all | solution.py:206
  103.0 0.0 copy-start
  103.0 0.0 collective-permute-start.2
  103.0 0.0 collective-permute-done.refs_1_
  103.0 1.9 slice.8
  104.8 1.6 collective-permute-start.3
  106.4 0.0 collective-permute-done.1.refs_2_
  106.4 1.2 slice.9
  107.6 1.8 collective-permute-start.4
  109.5 0.0 collective-permute-done.2.refs_4_
  109.5 7.7 %near_part.1 = (f32[256,384]{1,0:T(8,128)S(1)}, bf16[384,3456]{1,0:T(8,128)(2,1)}, bf16[384,3456]{1,0:T(8,128)(2,1)}, bf16[512,3456]{1,0:T(8,128)(2,1)S(1)}) custom-call(f32[32,4,3456]{2,1,0:T(4,128)S(1)} %all-to-all-done.refs_0_, f32[32,4,3456]{2,1,0:T(4,128)} %collective-permute-done.refs_1_, f32[32,4,3456]{2,1,0:T(4,128)} %collective-permute-done.1.refs_2_, ...), custom_call_target="tpu_custom_call" | custom-call | flops 2038431744 | bytes 17694720 | tf_op jit(solution)/shard_map/near_part/pallas_call | solution.py:295
  117.2 0.0 copy-done
  117.2 10.3 %collective-permute-done.3.refs_0_ = f32[16,4,3456]{2,1,0:T(4,128)S(1)} collective-permute-done((f32[16,4,3456]{2,1,0:T(4,128)S(1)}, f32[16,4,3456]{2,1,0:T(4,128)S(1)}, u32[]{:S(2)}, u32[]{:S(2)}) %collective-permute-start.3) | collective-permute-done | bytes 884768 | tf_op jit(solution)/shard_map/ppermute | solution.py:215
  127.6 1.3 collective-permute-done.4.refs_1_
  128.9 2.8 %far_part.1 = (f32[256,512]{1,0:T(8,128)S(1)}, bf16[128,3456]{1,0:T(8,128)(2,1)S(1)}, bf16[128,3456]{1,0:T(8,128)(2,1)S(1)}) custom-call(f32[256,384]{1,0:T(8,128)S(1)} %get-tuple-element.16.near_ref, bf16[512,3456]{1,0:T(8,128)(2,1)S(1)} %get-tuple-element.17.hsp_ref, f32[16,4,3456]{2,1,0:T(4,128)S(1)} %collective-permute-done.3.refs_0_, ...), custom_call_target="tpu_custom_call" | custom-call | flops 679477248 | bytes 10616832 | tf_op jit(solution)/shard_map/far_part/pallas_call | solution.py:295
  131.7 21.6 %all_to_all.25 = f32[32,8,512]{2,1,0:T(8,128)S(1)} all-to-all(f32[32,8,512]{2,1,0:T(8,128)S(1)} %bitcast.14), channel_id=1, replica_groups=mesh['x'=4,'zl'=2,'y'=4,'core'=2,'zh'=4] {'y','zl','zh'}, dimensions={0} | all-to-all | bytes 1048576 | tf_op jit(solution)/shard_map/all_to_all | solution.py:206
  153.3 0.1 broadcast_in_dim.2
  153.4 21.5 %all_to_all.26 = f32[32,8,512]{2,1,0:T(8,128)S(1)} all-to-all(f32[32,8,512]{2,1,0:T(8,128)S(1)} %broadcast_in_dim.2), channel_id=1, replica_groups=mesh['x'=4,'zl'=2,'y'=4,'core'=2,'zh'=4] {'y','zl','zh'}, dimensions={0} | all-to-all | bytes 1048576 | tf_op jit(solution)/shard_map/all_to_all | solution.py:206
  174.9 7.2 %rotated.1 = (f32[32,4,3456]{2,1,0:T(4,128)S(1)}, f32[32,4,3456]{2,1,0:T(4,128)S(1)}) custom-call(f32[256,512]{1,0:T(8,128)S(1)} %bitcast.13, bf16[384,3456]{1,0:T(8,128)(2,1)} %get-tuple-element.19.refs_0_, bf16[384,3456]{1,0:T(8,128)(2,1)} %get-tuple-element.20.refs_1_, bf16[128,3456]{1,0:T(8,128)(2,1)S(1)} %get-tuple-element.21.refs_2_, ...), custom_call_target="tpu_custom_call" | custom-call | flops 2717908992 | bytes 14155776 | tf_op jit(solution)/shard_map/rotated/pallas_call | solution.py:361
  182.2 0.1 collective-permute-start.5
  182.3 3.7 %collective-permute-done.5 = f32[32,4,3456]{2,1,0:T(4,128)S(1)} collective-permute-done((f32[32,4,3456]{2,1,0:T(4,128)S(1)}, f32[32,4,3456]{2,1,0:T(4,128)S(1)}, u32[]{:S(2)}, u32[]{:S(2)}) %collective-permute-start.5) | collective-permute-done | bytes 1769504 | tf_op jit(solution)/shard_map/ppermute | solution.py:219
  185.9 0.5 sub.3
  186.4 49.2 %all_to_all.27 = f32[32,4,3456]{2,1,0:T(4,128)S(1)} all-to-all(f32[32,4,3456]{2,1,0:T(4,128)S(1)} %sub.3), channel_id=1, replica_groups=mesh['x'=4,'zl'=2,'y'=4,'core'=2,'zh'=4] {'y','zl','zh'}, dimensions={0} | all-to-all | bytes 3538944 | tf_op jit(solution)/shard_map/all_to_all | solution.py:206
  235.6 1.2 copy.6
  (1 shorter events, 0.0 us)
Async XLA Ops:
  0.0 12.9 %copy-start.1 = (f32[4,110592]{1,0:T(4,128)S(1)}, f32[4,110592]{1,0:T(4,128)}, u32[]{:S(2)}) copy-start(f32[4,110592]{1,0:T(4,128)} %psi_ref.1) | copy-start | bytes 5308420
  0.0 12.9 %copy-start.4 = (f32[16]{0:T(128)S(1)}, f32[16]{0:T(128)}, u32[]{:S(2)}) copy-start(f32[16]{0:T(128)} %magic_ref.1) | copy-start | bytes 196
  0.0 12.9 %copy-start.5 = (f32[29]{0:T(128)S(1)}, f32[29]{0:T(128)}, u32[]{:S(2)}) copy-start(f32[29]{0:T(128)} %kinetic_ref.1) | copy-start | bytes 352
  0.0 54.2 %all-to-all-start = ((f32[32,4,3456]{2,1,0:T(4,128)}), f32[32,4,3456]{2,1,0:T(4,128)S(1)}, u32[]{:S(2)}, u32[]{:S(2)}) async-start(f32[32,4,3456]{2,1,0:T(4,128)} %bitcast.11), calls=%async_computation | async-start | bytes 3538944 | tf_op jit(solution)/shard_map/all_to_all | solution.py:206
  12.9 1.0 copy-start.3
  45.6 1.2 copy-start.2
  54.2 48.8 %all-to-all-start.1 = ((f32[32,4,3456]{2,1,0:T(4,128)}), f32[32,4,3456]{2,1,0:T(4,128)S(1)}, u32[]{:S(2)}, u32[]{:S(2)}) async-start(f32[32,4,3456]{2,1,0:T(4,128)} %bitcast.12), calls=%async_computation.1 | async-start | bytes 3538944 | tf_op jit(solution)/shard_map/all_to_all | solution.py:206
  60.2 42.7 %collective-permute-start = (f32[32,4,3456]{2,1,0:T(4,128)S(1)}, f32[32,4,3456]{2,1,0:T(4,128)}, u32[]{:S(2)}, u32[]{:S(2)}) collective-permute-start(f32[32,4,3456]{2,1,0:T(4,128)S(1)} %all-to-all-done.refs_0_), channel_id=1, source_target_pairs={{0,64},{64,128},{128,192},{192,0},{1,65},{65,129},{129,193},{193,1... | collective-permute-start | bytes 5308424 | tf_op jit(solution)/shard_map/ppermute | solution.py:215
  61.8 44.6 %collective-permute-start.1 = (f32[32,4,3456]{2,1,0:T(4,128)S(1)}, f32[32,4,3456]{2,1,0:T(4,128)}, u32[]{:S(2)}, u32[]{:S(2)}) collective-permute-start(f32[32,4,3456]{2,1,0:T(4,128)S(1)} %all-to-all-done.refs_0_), channel_id=1, source_target_pairs={{0,192},{64,0},{128,64},{192,128},{1,193},{65,1},{129,65},{193,129... | collective-permute-start | bytes 5308424 | tf_op jit(solution)/shard_map/ppermute | solution.py:215
  103.0 14.3 %copy-start = (f32[32,4,3456]{2,1,0:T(4,128)}, f32[32,4,3456]{2,1,0:T(4,128)S(1)}, u32[]{:S(2)}) copy-start(f32[32,4,3456]{2,1,0:T(4,128)S(1)} %all-to-all-done.1.refs_3_.refs_4_) | copy-start | bytes 5308420
  103.0 6.5 %collective-permute-start.2 = (f32[32,4,3456]{2,1,0:T(4,128)S(1)}, f32[32,4,3456]{2,1,0:T(4,128)S(1)}, u32[]{:S(2)}, u32[]{:S(2)}) collective-permute-start(f32[32,4,3456]{2,1,0:T(4,128)S(1)} %all-to-all-done.1.refs_3_.refs_4_), channel_id=1, source_target_pairs={{0,4},{4,0},{1,5},{5,1},{2,6},{6,2},{3,7},{7,3},{8,12},{12,8},{9,1... | collective-permute-start | bytes 5308424 | tf_op jit(solution)/shard_map/ppermute | solution.py:219
  104.8 22.7 %collective-permute-start.3 = (f32[16,4,3456]{2,1,0:T(4,128)S(1)}, f32[16,4,3456]{2,1,0:T(4,128)S(1)}, u32[]{:S(2)}, u32[]{:S(2)}) collective-permute-start(f32[16,4,3456]{2,1,0:T(4,128)S(1)} %slice.8), channel_id=1, source_target_pairs={{0,64},{64,128},{128,192},{192,0},{1,65},{65,129},{129,193},{193,1... | collective-permute-start | bytes 2654216 | tf_op jit(solution)/shard_map/ppermute | solution.py:215
  107.6 21.2 %collective-permute-start.4 = (f32[16,4,3456]{2,1,0:T(4,128)S(1)}, f32[16,4,3456]{2,1,0:T(4,128)S(1)}, u32[]{:S(2)}, u32[]{:S(2)}) collective-permute-start(f32[16,4,3456]{2,1,0:T(4,128)S(1)} %slice.9), channel_id=1, source_target_pairs={{0,192},{64,0},{128,64},{192,128},{1,193},{65,1},{129,65},{193,129... | collective-permute-start | bytes 2654216 | tf_op jit(solution)/shard_map/ppermute | solution.py:215
  182.2 3.8 %collective-permute-start.5 = (f32[32,4,3456]{2,1,0:T(4,128)S(1)}, f32[32,4,3456]{2,1,0:T(4,128)S(1)}, u32[]{:S(2)}, u32[]{:S(2)}) collective-permute-start(f32[32,4,3456]{2,1,0:T(4,128)S(1)} %get-tuple-element.24), channel_id=1, source_target_pairs={{0,4},{4,0},{1,5},{5,1},{2,6},{6,2},{3,7},{7,3},{8,12},{12,8},{9,1... | collective-permute-start | bytes 5308424 | tf_op jit(solution)/shard_map/ppermute | solution.py:219

commit v8 on v7

--- a/solution.py
+++ b/solution.py
@@ -1,3 +1,5 @@
+import functools
+
 import jax
 import jax.numpy as jnp
 from jax import lax
@@ -329,8 +331,8 @@
     )
 
 
-def rotate_kernel(margin_ref, *refs):
-    halves, (base_ref, mine_ref, other_ref, turn, res) = refs[:-5], refs[-5:]
+def rotate_kernel(count, margin_ref, *refs):
+    halves, bases, (out_ref, turn, res) = refs[:count], refs[count:-3], refs[-3:]
     cols = margin_ref.shape[0]
 
     @pl.when(pl.program_id(0) == 0)
@@ -349,22 +351,22 @@
         total = value if total is None else total + value
         at = upto
     res[...] = total
-    for s in range(mine_ref.shape[0]):
-        mine_ref[s] = base_ref[s] - res[4 * s:4 * s + 4, :]
-        other_ref[s] = res[cols // 2 + 4 * s:cols // 2 + 4 * s + 4, :]
-
-
-def rotated(margin, halves, base):
-    cols, rows = margin.shape
-    width = base.shape[2]
-    shape = jax.ShapeDtypeStruct(base.shape, F32)
+    for s in range(out_ref.shape[0]):
+        value = res[4 * s:4 * s + 4, :]
+        out_ref[s] = bases[0][s] - value if bases else value
+
+
+def rotated(margin, side, halves, *bases):
+    cols, rows = margin.shape[0] // 2, margin.shape[1]
+    width = halves[0].shape[1]
+    out = jax.ShapeDtypeStruct((cols // 4, 4, width), F32)
     return pl.pallas_call(
-        rotate_kernel,
+        functools.partial(rotate_kernel, len(halves)),
         grid=(width // WIDE,),
-        out_shape=[shape, shape],
-        in_specs=[pl.BlockSpec(margin.shape, lambda k: (0, 0))]
-        + [chunk_spec(v, WIDE) for v in (*halves, base)],
-        out_specs=[chunk_spec(base, WIDE)] * 2,
+        out_shape=out,
+        in_specs=[pl.BlockSpec((cols, rows), lambda k: (side, 0))]
+        + [chunk_spec(v, WIDE) for v in (*halves, *bases)],
+        out_specs=chunk_spec(out, WIDE),
         scratch_shapes=[pltpu.VMEM((2 * cols, rows), BF16), pltpu.VMEM((cols, WIDE), F32)],
         cost_estimate=pl.CostEstimate(
             flops=6 * rows * cols * width, transcendentals=0,
@@ -372,7 +374,7 @@
         ),
         compiler_params=pltpu.CompilerParams(vmem_limit_bytes=48 * 1024 * 1024),
         name="rotated",
-    )(margin, *halves, base)
+    )(margin, *halves, *bases)
 
 
 def shards(orbitals, potential, magic_taps, kinetic_taps):
@@ -388,8 +390,9 @@
     part, *far_halves = far_part(near, hsp, [far_a, far_b])
     mine = jnp.sum(exchange(part.reshape(NSPLIT, -1, part.shape[1])), axis=0)
     margin = exchange(jnp.broadcast_to(mine[None], (NSPLIT, *mine.shape))).reshape(part.shape)
-    grad_mine, grad_other = rotated(margin, near_halves + far_halves, hpsi_cols)
-    grad_cols = grad_mine - swap_core(grad_other)
+    halves = near_halves + far_halves
+    from_other = swap_core(rotated(margin, 1, halves))
+    grad_cols = rotated(margin, 0, halves, hpsi_cols) - from_other
     back = exchange(grad_cols)
     return back.transpose(1, 0, 2).reshape(orbitals.shape)
 

time: 238 us -> 239 us (level)
  waiting for transfers between devices: 62.1 us -> 58.6 us
  Pallas kernels: 49.4 us -> 52.1 us
    ppermute x2, waiting for transfers between devices: 3.68 us -> 0.01 us  [swap_core(): return lax.ppermute(value, 'core', [(0, 1), (1, 0)])]
    pallas_call x1 -> x2, Pallas kernels: 7.22 us -> 9.92 us  [rotated(): pl.pallas_call(functools.partial(rotate_kernel, len(halves)), grid=(width...]
  transfers between devices with their start and end apart: 8 -> 8, of which waited for: 5 -> 4; matrix products, arithmetic and copies ran while one was open for 2% -> 1% of each run, Pallas kernels for 17% -> 19%
where the time goes in v8:
time: 239 us; the launch traced here: 238 us
  blocking collectives  93.5 us (39%)
  waiting for transfers between devices  58.6 us (25%)
  Pallas kernels  52.1 us (22%)
  starting transfers between devices  23.9 us (10%)
  local copies, waits for them, and re-layouts  8.25 us (3%)
    all_to_all x3, blocking collectives, exchange(): return lax.all_to_all(pieces, COEF, split_axis=0, concat_axis=0, tiled=True)  93.5 us
    all_to_all x2, waiting for transfers between devices, exchange(): return lax.all_to_all(pieces, COEF, split_axis=0, concat_axis=0, tiled=True)  46.3 us
    pallas_call x1, Pallas kernels, hamiltonian(): pl.pallas_call(h_kernel, out_shape=jax.ShapeDtypeStruct(orbitals.shape, F...  31.7 us
    all_to_all x2, starting transfers between devices, exchange(): return lax.all_to_all(pieces, COEF, split_axis=0, concat_axis=0, tiled=True)  17.1 us
    ppermute x4, waiting for transfers between devices, step_x(): return lax.ppermute(pieces, 'x', [(i, (i + step) % 4) for i in range(4)])  12.3 us
    pallas_call x2, Pallas kernels, margin_call(): pl.pallas_call(kernel, grid=(width // CHUNK,), out_shape=[jax.ShapeDtypeS...  10.5 us
    pallas_call x2, Pallas kernels, rotated(): pl.pallas_call(functools.partial(rotate_kernel, len(halves)), grid=(width...  9.92 us
    ppermute x4, starting transfers between devices, step_x(): return lax.ppermute(pieces, 'x', [(i, (i + step) % 4) for i in range(4)])  6.71 us
  transfers between devices with their start and end apart: 8, of which 4 were waited for; matrix products, arithmetic and copies ran while one was open for 1% of the time, Pallas kernels for 19%

profile of v8, /device:TPU:64, one launch (start us, length us, event | category | flops | bytes accessed | tf_op | source)
XLA Modules:
  0.0 238.0 jit_solution(14485572904703386861)
XLA Ops:
  0.0 0.0 copy-start.5
  0.0 0.0 copy-start.3
  0.0 0.0 copy-start.4
  0.0 11.0 %all-to-all-start = ((f32[32,4,3456]{2,1,0:T(4,128)}), f32[32,4,3456]{2,1,0:T(4,128)S(1)}, u32[]{:S(2)}, u32[]{:S(2)}) async-start(f32[32,4,3456]{2,1,0:T(4,128)} %bitcast.13), calls=%async_computation | async-start | bytes 3538944 | tf_op jit(solution)/shard_map/all_to_all | solution.py:208
  11.1 0.0 copy-done.5
  11.1 0.8 reshape.20.pot_ref
  11.9 0.0 copy-done.3
  11.9 0.0 copy-done.4
  11.9 0.0 copy-start
  11.9 1.5 copy-done
  13.4 0.0 copy-start.2
  13.4 1.0 copy-done.2
  14.4 31.7 %hamiltonian.1 = f32[4,110592]{1,0:T(4,128)S(1)} custom-call(f32[16]{0:T(128)S(1)} %copy-done.3, f32[29]{0:T(128)S(1)} %copy-done.4, f32[4,110592]{1,0:T(4,128)S(1)} %copy-done, f32[48,2304]{1,0:T(8,128)S(1)} %copy-done.2), custom_call_target="tpu_custom_call" | custom-call | flops 24000000000 | bytes 5308416 | tf_op jit(solution)/shard_map/hamiltonian/pallas_call | solution.py:181
  46.1 0.0 copy-start.1
  46.1 1.2 copy-done.1
  47.3 6.9 %all-to-all-done.refs_0_ = f32[32,4,3456]{2,1,0:T(4,128)S(1)} async-done(((f32[32,4,3456]{2,1,0:T(4,128)}), f32[32,4,3456]{2,1,0:T(4,128)S(1)}, u32[]{:S(2)}, u32[]{:S(2)}) %all-to-all-start) | async-done | bytes 1769504 | tf_op jit(solution)/shard_map/all_to_all | solution.py:208
  54.2 6.0 %all-to-all-start.1 = ((f32[32,4,3456]{2,1,0:T(4,128)}), f32[32,4,3456]{2,1,0:T(4,128)S(1)}, u32[]{:S(2)}, u32[]{:S(2)}) async-start(f32[32,4,3456]{2,1,0:T(4,128)} %bitcast.14), calls=%async_computation.1 | async-start | bytes 3538944 | tf_op jit(solution)/shard_map/all_to_all | solution.py:208
  60.2 1.6 collective-permute-start
  61.8 1.7 collective-permute-start.1
  63.5 39.4 %all-to-all-done.1.refs_3_.refs_4_ = f32[32,4,3456]{2,1,0:T(4,128)S(1)} async-done(((f32[32,4,3456]{2,1,0:T(4,128)}), f32[32,4,3456]{2,1,0:T(4,128)S(1)}, u32[]{:S(2)}, u32[]{:S(2)}) %all-to-all-start.1) | async-done | bytes 1769504 | tf_op jit(solution)/shard_map/all_to_all | solution.py:208
  103.0 0.0 collective-permute-start.2
  103.0 0.0 collective-permute-done.refs_1_
  103.0 1.2 slice.8
  104.2 1.6 collective-permute-start.3
  105.8 0.0 collective-permute-done.1.refs_2_
  105.8 1.2 slice.9
  107.0 1.8 collective-permute-start.4
  108.8 0.0 collective-permute-done.2.refs_4_
  108.8 7.7 %near_part.1 = (f32[256,384]{1,0:T(8,128)S(1)}, bf16[384,3456]{1,0:T(8,128)(2,1)}, bf16[384,3456]{1,0:T(8,128)(2,1)}, bf16[512,3456]{1,0:T(8,128)(2,1)S(1)}) custom-call(f32[32,4,3456]{2,1,0:T(4,128)S(1)} %all-to-all-done.refs_0_, f32[32,4,3456]{2,1,0:T(4,128)} %collective-permute-done.refs_1_, f32[32,4,3456]{2,1,0:T(4,128)} %collective-permute-done.1.refs_2_, ...), custom_call_target="tpu_custom_call" | custom-call | flops 2038431744 | bytes 17694720 | tf_op jit(solution)/shard_map/near_part/pallas_call | solution.py:297
  116.6 11.0 %collective-permute-done.3.refs_0_ = f32[16,4,3456]{2,1,0:T(4,128)S(1)} collective-permute-done((f32[16,4,3456]{2,1,0:T(4,128)S(1)}, f32[16,4,3456]{2,1,0:T(4,128)S(1)}, u32[]{:S(2)}, u32[]{:S(2)}) %collective-permute-start.3) | collective-permute-done | bytes 884768 | tf_op jit(solution)/shard_map/ppermute | solution.py:217
  127.5 1.3 collective-permute-done.4.refs_1_
  128.9 2.8 %far_part.1 = (f32[256,512]{1,0:T(8,128)S(1)}, bf16[128,3456]{1,0:T(8,128)(2,1)S(1)}, bf16[128,3456]{1,0:T(8,128)(2,1)S(1)}) custom-call(f32[256,384]{1,0:T(8,128)S(1)} %get-tuple-element.14.near_ref, bf16[512,3456]{1,0:T(8,128)(2,1)S(1)} %get-tuple-element.15.hsp_ref, f32[16,4,3456]{2,1,0:T(4,128)S(1)} %collective-permute-done.3.refs_0_, ...), custom_call_target="tpu_custom_call" | custom-call | flops 679477248 | bytes 10616832 | tf_op jit(solution)/shard_map/far_part/pallas_call | solution.py:297
  131.6 22.5 %all_to_all.25 = f32[32,8,512]{2,1,0:T(8,128)} all-to-all(f32[32,8,512]{2,1,0:T(8,128)S(1)} %bitcast.15), channel_id=1, replica_groups=mesh['x'=4,'zl'=2,'y'=4,'core'=2,'zh'=4] {'y','zl','zh'}, dimensions={0} | all-to-all | bytes 1048576 | tf_op jit(solution)/shard_map/all_to_all | solution.py:208
  154.1 1.1 reduce_sum.9
  155.2 0.1 broadcast_in_dim.2
  155.3 21.4 %all_to_all.26 = f32[32,8,512]{2,1,0:T(8,128)S(1)} all-to-all(f32[32,8,512]{2,1,0:T(8,128)S(1)} %broadcast_in_dim.2), channel_id=1, replica_groups=mesh['x'=4,'zl'=2,'y'=4,'core'=2,'zh'=4] {'y','zl','zh'}, dimensions={0} | all-to-all | bytes 1048576 | tf_op jit(solution)/shard_map/all_to_all | solution.py:208
  176.7 4.9 %rotated.3 = f32[32,4,3456]{2,1,0:T(4,128)S(1)} custom-call(f32[256,512]{1,0:T(8,128)S(1)} %bitcast.11, bf16[384,3456]{1,0:T(8,128)(2,1)} %get-tuple-element.17.refs_0_, bf16[384,3456]{1,0:T(8,128)(2,1)} %get-tuple-element.18.refs_1_, bf16[128,3456]{1,0:T(8,128)(2,1)S(1)} %get-tuple-element.19.refs_2_, bf16[128,3456]{1,0:T(8,128)(2,1)S(1)} %get-tuple-element.20.refs_3_), custom_call_target="tpu_custom_call" | custom-call | flops 1358954496 | bytes 10616832 | tf_op jit(solution)/shard_map/rotated/pallas_call | solution.py:363
  181.7 0.1 collective-permute-start.5
  181.8 5.0 %rotated.2 = f32[32,4,3456]{2,1,0:T(4,128)S(1)} custom-call(f32[256,512]{1,0:T(8,128)S(1)} %bitcast.12, bf16[384,3456]{1,0:T(8,128)(2,1)} %get-tuple-element.17.refs_0_, bf16[384,3456]{1,0:T(8,128)(2,1)} %get-tuple-element.18.refs_1_, bf16[128,3456]{1,0:T(8,128)(2,1)S(1)} %get-tuple-element.19.refs_2_, bf16[128,3456]{1,0:T(8,128)(2,1)S(1)} %get-tuple-element.20.refs_3_, ...), custom_call_target="tpu_custom_call" | custom-call | flops 1358954496 | bytes 10616832 | tf_op jit(solution)/shard_map/rotated/pallas_call | solution.py:363
  186.8 0.0 collective-permute-done.5
  186.8 0.5 sub.3
  187.2 49.6 %all_to_all.27 = f32[32,4,3456]{2,1,0:T(4,128)S(1)} all-to-all(f32[32,4,3456]{2,1,0:T(4,128)S(1)} %sub.3), channel_id=1, replica_groups=mesh['x'=4,'zl'=2,'y'=4,'core'=2,'zh'=4] {'y','zl','zh'}, dimensions={0} | all-to-all | bytes 3538944 | tf_op jit(solution)/shard_map/all_to_all | solution.py:208
  236.8 1.2 copy.6
Async XLA Ops:
  0.0 11.1 %copy-start.5 = (f32[110592]{0:T(1024)S(1)}, f32[110592]{0:T(1024)}, u32[]{:S(2)}) copy-start(f32[110592]{0:T(1024)} %param.5) | copy-start | bytes 1327108
  0.0 11.9 %copy-start.3 = (f32[16]{0:T(128)S(1)}, f32[16]{0:T(128)}, u32[]{:S(2)}) copy-start(f32[16]{0:T(128)} %magic_ref.1) | copy-start | bytes 196
  0.0 11.9 %copy-start.4 = (f32[29]{0:T(128)S(1)}, f32[29]{0:T(128)}, u32[]{:S(2)}) copy-start(f32[29]{0:T(128)} %kinetic_ref.1) | copy-start | bytes 352
  0.0 54.2 %all-to-all-start = ((f32[32,4,3456]{2,1,0:T(4,128)}), f32[32,4,3456]{2,1,0:T(4,128)S(1)}, u32[]{:S(2)}, u32[]{:S(2)}) async-start(f32[32,4,3456]{2,1,0:T(4,128)} %bitcast.13), calls=%async_computation | async-start | bytes 3538944 | tf_op jit(solution)/shard_map/all_to_all | solution.py:208
  11.9 1.5 copy-start
  13.4 1.0 copy-start.2
  46.1 1.2 copy-start.1
  54.2 48.8 %all-to-all-start.1 = ((f32[32,4,3456]{2,1,0:T(4,128)}), f32[32,4,3456]{2,1,0:T(4,128)S(1)}, u32[]{:S(2)}, u32[]{:S(2)}) async-start(f32[32,4,3456]{2,1,0:T(4,128)} %bitcast.14), calls=%async_computation.1 | async-start | bytes 3538944 | tf_op jit(solution)/shard_map/all_to_all | solution.py:208
  60.2 42.7 %collective-permute-start = (f32[32,4,3456]{2,1,0:T(4,128)S(1)}, f32[32,4,3456]{2,1,0:T(4,128)}, u32[]{:S(2)}, u32[]{:S(2)}) collective-permute-start(f32[32,4,3456]{2,1,0:T(4,128)S(1)} %all-to-all-done.refs_0_), channel_id=1, source_target_pairs={{0,64},{64,128},{128,192},{192,0},{1,65},{65,129},{129,193},{193,1... | collective-permute-start | bytes 5308424 | tf_op jit(solution)/shard_map/ppermute | solution.py:217
  61.8 44.0 %collective-permute-start.1 = (f32[32,4,3456]{2,1,0:T(4,128)S(1)}, f32[32,4,3456]{2,1,0:T(4,128)}, u32[]{:S(2)}, u32[]{:S(2)}) collective-permute-start(f32[32,4,3456]{2,1,0:T(4,128)S(1)} %all-to-all-done.refs_0_), channel_id=1, source_target_pairs={{0,192},{64,0},{128,64},{192,128},{1,193},{65,1},{129,65},{193,129... | collective-permute-start | bytes 5308424 | tf_op jit(solution)/shard_map/ppermute | solution.py:217
  103.0 5.9 %collective-permute-start.2 = (f32[32,4,3456]{2,1,0:T(4,128)S(1)}, f32[32,4,3456]{2,1,0:T(4,128)S(1)}, u32[]{:S(2)}, u32[]{:S(2)}) collective-permute-start(f32[32,4,3456]{2,1,0:T(4,128)S(1)} %all-to-all-done.1.refs_3_.refs_4_), channel_id=1, source_target_pairs={{0,4},{4,0},{1,5},{5,1},{2,6},{6,2},{3,7},{7,3},{8,12},{12,8},{9,1... | collective-permute-start | bytes 5308424 | tf_op jit(solution)/shard_map/ppermute | solution.py:221
  104.2 23.3 %collective-permute-start.3 = (f32[16,4,3456]{2,1,0:T(4,128)S(1)}, f32[16,4,3456]{2,1,0:T(4,128)S(1)}, u32[]{:S(2)}, u32[]{:S(2)}) collective-permute-start(f32[16,4,3456]{2,1,0:T(4,128)S(1)} %slice.8), channel_id=1, source_target_pairs={{0,64},{64,128},{128,192},{192,0},{1,65},{65,129},{129,193},{193,1... | collective-permute-start | bytes 2654216 | tf_op jit(solution)/shard_map/ppermute | solution.py:217
  107.0 21.9 %collective-permute-start.4 = (f32[16,4,3456]{2,1,0:T(4,128)S(1)}, f32[16,4,3456]{2,1,0:T(4,128)S(1)}, u32[]{:S(2)}, u32[]{:S(2)}) collective-permute-start(f32[16,4,3456]{2,1,0:T(4,128)S(1)} %slice.9), channel_id=1, source_target_pairs={{0,192},{64,0},{128,64},{192,128},{1,193},{65,1},{129,65},{193,129... | collective-permute-start | bytes 2654216 | tf_op jit(solution)/shard_map/ppermute | solution.py:217
  181.7 5.1 %collective-permute-start.5 = (f32[32,4,3456]{2,1,0:T(4,128)S(1)}, f32[32,4,3456]{2,1,0:T(4,128)S(1)}, u32[]{:S(2)}, u32[]{:S(2)}) collective-permute-start(f32[32,4,3456]{2,1,0:T(4,128)S(1)} %rotated.3), channel_id=1, source_target_pairs={{0,4},{4,0},{1,5},{5,1},{2,6},{6,2},{3,7},{7,3},{8,12},{12,8},{9,1... | collective-permute-start | bytes 5308424 | tf_op jit(solution)/shard_map/ppermute | solution.py:221

commit v9 on v8

--- a/solution.py
+++ b/solution.py
@@ -208,6 +208,13 @@
     return lax.all_to_all(pieces, COEF, split_axis=0, concat_axis=0, tiled=True)
 
 
+def spread(value, axes, count):
+    copies = jnp.broadcast_to(value[None], (count, *value.shape))
+    return lax.all_to_all(copies, axes, split_axis=0, concat_axis=0, tiled=True).reshape(
+        -1, value.shape[1]
+    )
+
+
 def to_cols(block):
     pieces = block.reshape(block.shape[0], NSPLIT, -1).transpose(1, 0, 2)
     return exchange(pieces)
@@ -389,7 +396,7 @@
     near, *near_halves, hsp = near_part([own, left, right], hpsi_cols, hpsi_swap)
     part, *far_halves = far_part(near, hsp, [far_a, far_b])
     mine = jnp.sum(exchange(part.reshape(NSPLIT, -1, part.shape[1])), axis=0)
-    margin = exchange(jnp.broadcast_to(mine[None], (NSPLIT, *mine.shape))).reshape(part.shape)
+    margin = spread(spread(mine, ("zl", "zh"), 8), ("y",), 4)
     halves = near_halves + far_halves
     from_other = swap_core(rotated(margin, 1, halves))
     grad_cols = rotated(margin, 0, halves, hpsi_cols) - from_other

time: 239 us -> 239 us (level)
    all_to_all x3 -> x2, blocking collectives: 93.5 us -> 72.3 us  [exchange(): return lax.all_to_all(pieces, COEF, split_axis=0, concat_axis=0, tiled=True)]
    all_to_all x0 -> x2, blocking collectives: none -> 20.9 us  [spread(): lax.all_to_all(copies, axes, split_axis=0, concat_axis=0, tiled=True)]
where the time goes in v9:
time: 239 us; the launch traced here: 238 us
  blocking collectives  93.2 us (39%)
  waiting for transfers between devices  58.6 us (25%)
  Pallas kernels  52.1 us (22%)
  starting transfers between devices  23.9 us (10%)
  local copies, waits for them, and re-layouts  8.27 us (3%)
    all_to_all x2, blocking collectives, exchange(): return lax.all_to_all(pieces, COEF, split_axis=0, concat_axis=0, tiled=True)  72.3 us
    all_to_all x2, waiting for transfers between devices, exchange(): return lax.all_to_all(pieces, COEF, split_axis=0, concat_axis=0, tiled=True)  46.3 us
    pallas_call x1, Pallas kernels, hamiltonian(): pl.pallas_call(h_kernel, out_shape=jax.ShapeDtypeStruct(orbitals.shape, F...  31.7 us
    all_to_all x2, blocking collectives, spread(): lax.all_to_all(copies, axes, split_axis=0, concat_axis=0, tiled=True)  20.9 us
    all_to_all x2, starting transfers between devices, exchange(): return lax.all_to_all(pieces, COEF, split_axis=0, concat_axis=0, tiled=True)  17.1 us
    ppermute x4, waiting for transfers between devices, step_x(): return lax.ppermute(pieces, 'x', [(i, (i + step) % 4) for i in range(4)])  12.3 us
    pallas_call x2, Pallas kernels, margin_call(): pl.pallas_call(kernel, grid=(width // CHUNK,), out_shape=[jax.ShapeDtypeS...  10.5 us
    pallas_call x2, Pallas kernels, rotated(): pl.pallas_call(functools.partial(rotate_kernel, len(halves)), grid=(width...  9.91 us
  transfers between devices with their start and end apart: 8, of which 4 were waited for; matrix products, arithmetic and copies ran while one was open for 1% of the time, Pallas kernels for 19%

profile of v9, /device:TPU:64, one launch (start us, length us, event | category | flops | bytes accessed | tf_op | source)
XLA Modules:
  0.0 237.7 jit_solution(11773216326575397302)
XLA Ops:
  0.0 0.0 copy-start.5
  0.0 0.0 copy-start.3
  0.0 0.0 copy-start.4
  0.0 11.0 %all-to-all-start = ((f32[32,4,3456]{2,1,0:T(4,128)}), f32[32,4,3456]{2,1,0:T(4,128)S(1)}, u32[]{:S(2)}, u32[]{:S(2)}) async-start(f32[32,4,3456]{2,1,0:T(4,128)} %bitcast.14), calls=%async_computation | async-start | bytes 3538944 | tf_op jit(solution)/shard_map/all_to_all | solution.py:208
  11.1 0.0 copy-done.5
  11.1 0.8 reshape.21.pot_ref
  11.9 0.0 copy-done.3
  11.9 0.0 copy-done.4
  11.9 0.0 copy-start
  11.9 1.5 copy-done
  13.4 0.0 copy-start.2
  13.4 1.0 copy-done.2
  14.4 31.7 %hamiltonian.1 = f32[4,110592]{1,0:T(4,128)S(1)} custom-call(f32[16]{0:T(128)S(1)} %copy-done.3, f32[29]{0:T(128)S(1)} %copy-done.4, f32[4,110592]{1,0:T(4,128)S(1)} %copy-done, f32[48,2304]{1,0:T(8,128)S(1)} %copy-done.2), custom_call_target="tpu_custom_call" | custom-call | flops 24000000000 | bytes 5308416 | tf_op jit(solution)/shard_map/hamiltonian/pallas_call | solution.py:181
  46.1 0.0 copy-start.1
  46.1 1.2 copy-done.1
  47.3 6.9 %all-to-all-done.refs_0_ = f32[32,4,3456]{2,1,0:T(4,128)S(1)} async-done(((f32[32,4,3456]{2,1,0:T(4,128)}), f32[32,4,3456]{2,1,0:T(4,128)S(1)}, u32[]{:S(2)}, u32[]{:S(2)}) %all-to-all-start) | async-done | bytes 1769504 | tf_op jit(solution)/shard_map/all_to_all | solution.py:208
  54.2 6.0 %all-to-all-start.1 = ((f32[32,4,3456]{2,1,0:T(4,128)}), f32[32,4,3456]{2,1,0:T(4,128)S(1)}, u32[]{:S(2)}, u32[]{:S(2)}) async-start(f32[32,4,3456]{2,1,0:T(4,128)} %bitcast.15), calls=%async_computation.1 | async-start | bytes 3538944 | tf_op jit(solution)/shard_map/all_to_all | solution.py:208
  60.2 1.6 collective-permute-start
  61.8 1.7 collective-permute-start.1
  63.5 39.4 %all-to-all-done.1.refs_3_.refs_4_ = f32[32,4,3456]{2,1,0:T(4,128)S(1)} async-done(((f32[32,4,3456]{2,1,0:T(4,128)}), f32[32,4,3456]{2,1,0:T(4,128)S(1)}, u32[]{:S(2)}, u32[]{:S(2)}) %all-to-all-start.1) | async-done | bytes 1769504 | tf_op jit(solution)/shard_map/all_to_all | solution.py:208
  103.0 0.0 collective-permute-start.2
  103.0 0.0 collective-permute-done.refs_1_
  103.0 1.2 slice.8
  104.2 1.6 collective-permute-start.3
  105.8 0.0 collective-permute-done.1.refs_2_
  105.8 1.2 slice.9
  107.0 1.8 collective-permute-start.4
  108.8 0.0 collective-permute-done.2.refs_4_
  108.8 7.7 %near_part.1 = (f32[256,384]{1,0:T(8,128)S(1)}, bf16[384,3456]{1,0:T(8,128)(2,1)}, bf16[384,3456]{1,0:T(8,128)(2,1)}, bf16[512,3456]{1,0:T(8,128)(2,1)S(1)}) custom-call(f32[32,4,3456]{2,1,0:T(4,128)S(1)} %all-to-all-done.refs_0_, f32[32,4,3456]{2,1,0:T(4,128)} %collective-permute-done.refs_1_, f32[32,4,3456]{2,1,0:T(4,128)} %collective-permute-done.1.refs_2_, ...), custom_call_target="tpu_custom_call" | custom-call | flops 2038431744 | bytes 17694720 | tf_op jit(solution)/shard_map/near_part/pallas_call | solution.py:304
  116.6 11.0 %collective-permute-done.3.refs_0_ = f32[16,4,3456]{2,1,0:T(4,128)S(1)} collective-permute-done((f32[16,4,3456]{2,1,0:T(4,128)S(1)}, f32[16,4,3456]{2,1,0:T(4,128)S(1)}, u32[]{:S(2)}, u32[]{:S(2)}) %collective-permute-start.3) | collective-permute-done | bytes 884768 | tf_op jit(solution)/shard_map/ppermute | solution.py:224
  127.5 1.3 collective-permute-done.4.refs_1_
  128.9 2.8 %far_part.1 = (f32[256,512]{1,0:T(8,128)S(1)}, bf16[128,3456]{1,0:T(8,128)(2,1)S(1)}, bf16[128,3456]{1,0:T(8,128)(2,1)S(1)}) custom-call(f32[256,384]{1,0:T(8,128)S(1)} %get-tuple-element.14.near_ref, bf16[512,3456]{1,0:T(8,128)(2,1)S(1)} %get-tuple-element.15.hsp_ref, f32[16,4,3456]{2,1,0:T(4,128)S(1)} %collective-permute-done.3.refs_0_, ...), custom_call_target="tpu_custom_call" | custom-call | flops 679477248 | bytes 10616832 | tf_op jit(solution)/shard_map/far_part/pallas_call | solution.py:304
  131.6 22.5 %all_to_all.30 = f32[32,8,512]{2,1,0:T(8,128)} all-to-all(f32[32,8,512]{2,1,0:T(8,128)S(1)} %bitcast.16), channel_id=1, replica_groups=mesh['x'=4,'zl'=2,'y'=4,'core'=2,'zh'=4] {'y','zl','zh'}, dimensions={0} | all-to-all | bytes 1048576 | tf_op jit(solution)/shard_map/all_to_all | solution.py:208
  154.1 1.1 reduce_sum.9
  155.2 10.4 %all_to_all.31 = f32[8,8,512]{2,1,0:T(8,128)S(1)} all-to-all(f32[8,8,512]{2,1,0:T(8,128)S(1)} %broadcast_in_dim.6), channel_id=1, replica_groups=mesh['x'=4,'zl'=2,'y'=4,'core'=2,'zh'=4] {'zl','zh'}, dimensions={0} | all-to-all | bytes 262144 | tf_op jit(solution)/shard_map/all_to_all | solution.py:213
  165.7 10.5 %all_to_all.32 = f32[4,64,512]{2,1,0:T(8,128)S(1)} all-to-all(f32[4,64,512]{2,1,0:T(8,128)S(1)} %broadcast_in_dim.15), channel_id=1, replica_groups=mesh['x'=4,'zl'=2,'y'=4,'core'=2,'zh'=4] {'y'}, dimensions={0} | all-to-all | bytes 1048576 | tf_op jit(solution)/shard_map/all_to_all | solution.py:213
  176.2 4.9 %rotated.3 = f32[32,4,3456]{2,1,0:T(4,128)S(1)} custom-call(f32[256,512]{1,0:T(8,128)S(1)} %bitcast.12, bf16[384,3456]{1,0:T(8,128)(2,1)} %get-tuple-element.17.refs_0_, bf16[384,3456]{1,0:T(8,128)(2,1)} %get-tuple-element.18.refs_1_, bf16[128,3456]{1,0:T(8,128)(2,1)S(1)} %get-tuple-element.19.refs_2_, bf16[128,3456]{1,0:T(8,128)(2,1)S(1)} %get-tuple-element.20.refs_3_), custom_call_target="tpu_custom_call" | custom-call | flops 1358954496 | bytes 10616832 | tf_op jit(solution)/shard_map/rotated/pallas_call | solution.py:370
  181.1 0.1 collective-permute-start.5
  181.2 5.0 %rotated.2 = f32[32,4,3456]{2,1,0:T(4,128)S(1)} custom-call(f32[256,512]{1,0:T(8,128)S(1)} %bitcast.13, bf16[384,3456]{1,0:T(8,128)(2,1)} %get-tuple-element.17.refs_0_, bf16[384,3456]{1,0:T(8,128)(2,1)} %get-tuple-element.18.refs_1_, bf16[128,3456]{1,0:T(8,128)(2,1)S(1)} %get-tuple-element.19.refs_2_, bf16[128,3456]{1,0:T(8,128)(2,1)S(1)} %get-tuple-element.20.refs_3_, ...), custom_call_target="tpu_custom_call" | custom-call | flops 1358954496 | bytes 10616832 | tf_op jit(solution)/shard_map/rotated/pallas_call | solution.py:370
  186.2 0.0 collective-permute-done.5
  186.2 0.5 sub.3
  186.7 49.8 %all_to_all.33 = f32[32,4,3456]{2,1,0:T(4,128)S(1)} all-to-all(f32[32,4,3456]{2,1,0:T(4,128)S(1)} %sub.3), channel_id=1, replica_groups=mesh['x'=4,'zl'=2,'y'=4,'core'=2,'zh'=4] {'y','zl','zh'}, dimensions={0} | all-to-all | bytes 3538944 | tf_op jit(solution)/shard_map/all_to_all | solution.py:208
  236.5 1.2 copy.6
  (2 shorter events, 0.1 us)
Async XLA Ops:
  0.0 11.1 %copy-start.5 = (f32[110592]{0:T(1024)S(1)}, f32[110592]{0:T(1024)}, u32[]{:S(2)}) copy-start(f32[110592]{0:T(1024)} %param.5) | copy-start | bytes 1327108
  0.0 11.9 %copy-start.3 = (f32[16]{0:T(128)S(1)}, f32[16]{0:T(128)}, u32[]{:S(2)}) copy-start(f32[16]{0:T(128)} %magic_ref.1) | copy-start | bytes 196
  0.0 11.9 %copy-start.4 = (f32[29]{0:T(128)S(1)}, f32[29]{0:T(128)}, u32[]{:S(2)}) copy-start(f32[29]{0:T(128)} %kinetic_ref.1) | copy-start | bytes 352
  0.0 54.2 %all-to-all-start = ((f32[32,4,3456]{2,1,0:T(4,128)}), f32[32,4,3456]{2,1,0:T(4,128)S(1)}, u32[]{:S(2)}, u32[]{:S(2)}) async-start(f32[32,4,3456]{2,1,0:T(4,128)} %bitcast.14), calls=%async_computation | async-start | bytes 3538944 | tf_op jit(solution)/shard_map/all_to_all | solution.py:208
  11.9 1.5 copy-start
  13.4 1.0 copy-start.2
  46.1 1.2 copy-start.1
  54.2 48.8 %all-to-all-start.1 = ((f32[32,4,3456]{2,1,0:T(4,128)}), f32[32,4,3456]{2,1,0:T(4,128)S(1)}, u32[]{:S(2)}, u32[]{:S(2)}) async-start(f32[32,4,3456]{2,1,0:T(4,128)} %bitcast.15), calls=%async_computation.1 | async-start | bytes 3538944 | tf_op jit(solution)/shard_map/all_to_all | solution.py:208
  60.2 42.7 %collective-permute-start = (f32[32,4,3456]{2,1,0:T(4,128)S(1)}, f32[32,4,3456]{2,1,0:T(4,128)}, u32[]{:S(2)}, u32[]{:S(2)}) collective-permute-start(f32[32,4,3456]{2,1,0:T(4,128)S(1)} %all-to-all-done.refs_0_), channel_id=1, source_target_pairs={{0,64},{64,128},{128,192},{192,0},{1,65},{65,129},{129,193},{193,1... | collective-permute-start | bytes 5308424 | tf_op jit(solution)/shard_map/ppermute | solution.py:224
  61.8 44.0 %collective-permute-start.1 = (f32[32,4,3456]{2,1,0:T(4,128)S(1)}, f32[32,4,3456]{2,1,0:T(4,128)}, u32[]{:S(2)}, u32[]{:S(2)}) collective-permute-start(f32[32,4,3456]{2,1,0:T(4,128)S(1)} %all-to-all-done.refs_0_), channel_id=1, source_target_pairs={{0,192},{64,0},{128,64},{192,128},{1,193},{65,1},{129,65},{193,129... | collective-permute-start | bytes 5308424 | tf_op jit(solution)/shard_map/ppermute | solution.py:224
  103.0 5.9 %collective-permute-start.2 = (f32[32,4,3456]{2,1,0:T(4,128)S(1)}, f32[32,4,3456]{2,1,0:T(4,128)S(1)}, u32[]{:S(2)}, u32[]{:S(2)}) collective-permute-start(f32[32,4,3456]{2,1,0:T(4,128)S(1)} %all-to-all-done.1.refs_3_.refs_4_), channel_id=1, source_target_pairs={{0,4},{4,0},{1,5},{5,1},{2,6},{6,2},{3,7},{7,3},{8,12},{12,8},{9,1... | collective-permute-start | bytes 5308424 | tf_op jit(solution)/shard_map/ppermute | solution.py:228
  104.2 23.3 %collective-permute-start.3 = (f32[16,4,3456]{2,1,0:T(4,128)S(1)}, f32[16,4,3456]{2,1,0:T(4,128)S(1)}, u32[]{:S(2)}, u32[]{:S(2)}) collective-permute-start(f32[16,4,3456]{2,1,0:T(4,128)S(1)} %slice.8), channel_id=1, source_target_pairs={{0,64},{64,128},{128,192},{192,0},{1,65},{65,129},{129,193},{193,1... | collective-permute-start | bytes 2654216 | tf_op jit(solution)/shard_map/ppermute | solution.py:224
  107.0 21.9 %collective-permute-start.4 = (f32[16,4,3456]{2,1,0:T(4,128)S(1)}, f32[16,4,3456]{2,1,0:T(4,128)S(1)}, u32[]{:S(2)}, u32[]{:S(2)}) collective-permute-start(f32[16,4,3456]{2,1,0:T(4,128)S(1)} %slice.9), channel_id=1, source_target_pairs={{0,192},{64,0},{128,64},{192,128},{1,193},{65,1},{129,65},{193,129... | collective-permute-start | bytes 2654216 | tf_op jit(solution)/shard_map/ppermute | solution.py:224
  181.1 5.1 %collective-permute-start.5 = (f32[32,4,3456]{2,1,0:T(4,128)S(1)}, f32[32,4,3456]{2,1,0:T(4,128)S(1)}, u32[]{:S(2)}, u32[]{:S(2)}) collective-permute-start(f32[32,4,3456]{2,1,0:T(4,128)S(1)} %rotated.3), channel_id=1, source_target_pairs={{0,4},{4,0},{1,5},{5,1},{2,6},{6,2},{3,7},{7,3},{8,12},{12,8},{9,1... | collective-permute-start | bytes 5308424 | tf_op jit(solution)/shard_map/ppermute | solution.py:228
